TPU v7x, 32 devices: a whole 2x2x4 slice. The times are simulated.
32 devices in a mesh: seq: 4 (over y, x), fsdp: 8 (over z, core).
Axes of the slice: x: 2, y: 2, z: 4, core: 2. Of those that a mesh axis runs over, the one named last changes fastest.
Arguments:
- hidden_in: bfloat16 [8, 1024, 1024], P('fsdp', 'seq'), may hold values from -10 to 10
- segment_ids: int32 [8, 1024], P('fsdp'), may hold values from 0 to 2, never falling along the last dimension, each value on 1 to 768 neighbouring positions
- valid_tokens: int32 [8, 1024], P('fsdp'), may hold values from 0 to 1
- w_qkv: bfloat16 [1024, 3072], P('fsdp'), may hold values from -0.1875 to 0.1875
- w_attn_out: bfloat16 [1024, 1024], P('fsdp'), may hold values from -2 to 2
- w_in_proj: bfloat16 [1024, 5248], P('fsdp'), may hold values from -0.1875 to 0.1875
- w_out_proj: bfloat16 [2624, 1024], P('fsdp'), may hold values from -0.125 to 0.125
- attn_gain: bfloat16 [1024], P('fsdp'), may hold values from 0.25 to 1.75
- mlp_gain: bfloat16 [1024], P('fsdp'), may hold values from 0.25 to 1.75
- cotangent: bfloat16 [8, 1024, 1024], P('fsdp', 'seq'), may hold values from -6 to 6
Outputs:
- hidden_out: bfloat16 [8, 1024, 1024], P('fsdp', 'seq')
- grad_in: float32 [8, 1024, 1024], P('fsdp', 'seq')
- grad_qkv: float32 [1024, 3072], P('fsdp')
- grad_attn_out: float32 [1024, 1024], P('fsdp')
- grad_in_proj: float32 [1024, 5248], P('fsdp')
- grad_out_proj: float32 [2624, 1024], P('fsdp')
- grad_attn_gain: float32 [1024], P('fsdp')
- grad_mlp_gain: float32 [1024], P('fsdp')
- rms_values: float32 [3], replicated
All inputs are finite; a program needn't handle non-finite values.
Results may differ from a plain program's by a relative error of at most 0.014.
The roundings to bfloat16 on the way count: a program that leaves them out, or rounds other values in their place, can miss the bound.
Values may be sent and summed in bfloat16 or wider, within the bound.
No kernel may reach another device: no remote copies, remote signals or barrier semaphores. Data moves between devices by JAX's collectives and lax.ppermute only.
A program may use at most 192 MiB of HBM per device.

v0:
```python
import jax
import jax.numpy as jnp
from jax import lax
from jax.sharding import PartitionSpec as P

D = 1024
HEADS = 16
HD = 64
FF = 2624


ROPE_BASE = 160000.0
NORM_EPS = 1e-05


def norm_rows(values, gain_row):
    average = jnp.mean(values, axis=-1, keepdims=True)
    centered = values - average
    variance = jnp.mean(centered * centered, axis=-1, keepdims=True)
    return centered * lax.rsqrt(variance + NORM_EPS) * gain_row


def rotate(head_values, positions):
    half_width = head_values.shape[-1] // 2
    frequency = ROPE_BASE ** (
        -2.0 * jnp.arange(half_width, dtype=jnp.float32) / head_values.shape[-1]
    )
    angles = positions.astype(jnp.float32)[:, None] * frequency[None, :]
    cosine = jnp.cos(angles)[:, None, :]
    sine_part = jnp.sin(angles)[:, None, :]
    first_half = head_values[..., :half_width]
    second = head_values[..., half_width:]
    return jnp.concatenate(
        [first_half * cosine - second * sine_part, second * cosine + first_half * sine_part],
        axis=-1,
    )


def gelu_gate(inputs, gates):
    return 0.5 * inputs * (1.0 + jax.scipy.special.erf(inputs * 0.7071067811865476)) * gates


def allowed_mask(seg_block, row_ids, seg_all, valid_all):
    col_ids = jnp.arange(seg_all.shape[0], dtype=jnp.int32)
    return (seg_block[:, None] == seg_all[None, :]) & (
        (valid_all[None, :] > 0) | (row_ids[:, None] == col_ids[None, :])
    )


def attend_forward(queries, key_heads, value_heads, seg_all, valid_all):
    length, head_local, head_width = queries.shape
    block_rows = min(512, length)
    block_count = length // block_rows
    score_scale = float(head_width) ** (-0.5)
    row_ids = jnp.arange(length, dtype=jnp.int32).reshape(block_count, block_rows)

    def one_block(block_items):
        query_block, seg_block, row_block = block_items
        scores = (
            jnp.einsum("qhd,khd->hqk", query_block, key_heads, preferred_element_type=jnp.float32)
            * score_scale
        )
        allowed = allowed_mask(seg_block, row_block, seg_all, valid_all)[None]
        scores = jnp.where(allowed, scores, -1e30)
        row_max = jnp.max(scores, axis=-1, keepdims=True)
        exponent = jnp.exp(scores - row_max)
        denominator = jnp.sum(exponent, axis=-1, keepdims=True)
        weights = (exponent / denominator).astype(jnp.bfloat16)
        output = jnp.einsum(
            "hqk,khd->qhd", weights, value_heads, preferred_element_type=jnp.float32
        )
        return (output, (row_max + jnp.log(denominator))[..., 0])

    outputs, log_sums = lax.map(
        one_block,
        (
            queries.reshape(block_count, block_rows, head_local, head_width),
            seg_all.reshape(block_count, block_rows),
            row_ids,
        ),
    )
    return (outputs.reshape(length, head_local, head_width), log_sums)


def attend_backward(queries, key_heads, value_heads, grad_out, log_sums, seg_all, valid_all):
    length, head_local, head_width = queries.shape
    block_rows = min(512, length)
    block_count = length // block_rows
    score_scale = float(head_width) ** (-0.5)
    row_ids = jnp.arange(length, dtype=jnp.int32).reshape(block_count, block_rows)

    def one_block(carried, block_items):
        key_grad, value_grad = carried
        query_block, grad_block, lse_block, seg_block, row_block = block_items
        scores = (
            jnp.einsum("qhd,khd->hqk", query_block, key_heads, preferred_element_type=jnp.float32)
            * score_scale
        )
        allowed = allowed_mask(seg_block, row_block, seg_all, valid_all)[None]
        scores = jnp.where(allowed, scores, -1e30)
        weights = jnp.exp(scores - lse_block[..., None])
        weights_low = weights.astype(jnp.bfloat16)
        value_grad = value_grad + jnp.einsum(
            "hqk,qhd->khd", weights_low, grad_block, preferred_element_type=jnp.float32
        )
        weight_grad = jnp.einsum(
            "qhd,khd->hqk", grad_block, value_heads, preferred_element_type=jnp.float32
        )
        inner_sum = jnp.sum(weights * weight_grad, axis=-1, keepdims=True)
        score_grad = (weights * (weight_grad - inner_sum)).astype(jnp.bfloat16)
        query_grad = (
            jnp.einsum("hqk,khd->qhd", score_grad, key_heads, preferred_element_type=jnp.float32)
            * score_scale
        )
        key_grad = (
            key_grad
            + jnp.einsum(
                "hqk,qhd->khd", score_grad, query_block, preferred_element_type=jnp.float32
            )
            * score_scale
        )
        return ((key_grad, value_grad), query_grad)

    empty_grad = jnp.zeros((length, head_local, head_width), jnp.float32)
    block_items = (
        queries.reshape(block_count, block_rows, head_local, head_width),
        grad_out.reshape(block_count, block_rows, head_local, head_width),
        log_sums,
        seg_all.reshape(block_count, block_rows),
        row_ids,
    )
    (key_grad, value_grad), query_grads = lax.scan(one_block, (empty_grad, empty_grad), block_items)
    return (query_grads.reshape(length, head_local, head_width), key_grad, value_grad)


def on_device(
    hidden_in,
    segment_ids,
    valid_tokens,
    w_qkv,
    w_attn_out,
    w_in_proj,
    w_out_proj,
    attn_gain,
    mlp_gain,
    cotangent,
):
    seq_size = lax.axis_size("seq")
    seq_index = lax.axis_index("seq")
    inputs = hidden_in[0].astype(jnp.float32)
    tokens = inputs.shape[0]
    length = tokens * seq_size
    head_local = HEADS // seq_size
    seg_all = segment_ids[0]
    valid_all = valid_tokens[0]
    offset = seq_index * tokens
    valid_mine = lax.dynamic_slice_in_dim(valid_all, offset, tokens).astype(jnp.float32)[:, None]
    positions = offset + jnp.arange(tokens, dtype=jnp.int32)
    attn_full = (
        lax.all_gather(w_qkv, "fsdp", axis=0, tiled=True),
        lax.all_gather(w_attn_out, "fsdp", axis=0, tiled=True),
        lax.all_gather(attn_gain, "fsdp", axis=0, tiled=True),
    )
    mlp_full = (
        lax.all_gather(w_in_proj, "fsdp", axis=0, tiled=True),
        lax.all_gather(w_out_proj, "fsdp", axis=0, tiled=True),
        lax.all_gather(mlp_gain, "fsdp", axis=0, tiled=True),
    )
    qkv_weight, out_weight, gain_one = attn_full
    in_weight, down_weight, gain_two = mlp_full
    gain_one = gain_one.astype(jnp.float32)
    gain_two = gain_two.astype(jnp.float32)
    normed_low = norm_rows(inputs, gain_one).astype(jnp.bfloat16)
    projected = jnp.dot(normed_low, qkv_weight, preferred_element_type=jnp.float32).reshape(
        tokens, 3, HEADS, HD
    )

    def rope_pair(pair_heads):
        return jnp.stack(
            [rotate(pair_heads[:, 0], positions), rotate(pair_heads[:, 1], positions)], axis=1
        )

    turned = jnp.concatenate([rope_pair(projected[:, :2]), projected[:, 2:]], axis=1).astype(
        jnp.bfloat16
    )
    by_heads = lax.all_to_all(
        turned.reshape(tokens, 3, seq_size, head_local * HD),
        "seq",
        split_axis=2,
        concat_axis=0,
        tiled=True,
    )
    by_heads = by_heads.reshape(length, 3, head_local, HD)
    queries = by_heads[:, 0]
    key_heads = by_heads[:, 1]
    value_heads = by_heads[:, 2]
    attended, log_sums = attend_forward(queries, key_heads, value_heads, seg_all, valid_all)
    attended_low = attended.astype(jnp.bfloat16).reshape(length, 1, head_local * HD)
    mixed_low = lax.all_to_all(
        attended_low, "seq", split_axis=0, concat_axis=1, tiled=True
    ).reshape(tokens, D)
    attn_branch = jnp.dot(mixed_low, out_weight, preferred_element_type=jnp.float32)
    middle = inputs + attn_branch
    normed_two_low = norm_rows(middle, gain_two).astype(jnp.bfloat16)
    widened = jnp.dot(normed_two_low, in_weight, preferred_element_type=jnp.float32)
    inner_in = widened[:, :FF]
    inner_gate = widened[:, FF:]
    hidden_low = gelu_gate(inner_in, inner_gate).astype(jnp.bfloat16)
    mlp_branch = jnp.dot(hidden_low, down_weight, preferred_element_type=jnp.float32)
    result = middle + mlp_branch
    stat_sums = lax.psum(
        (
            jnp.sum(valid_mine * result * result),
            jnp.sum(valid_mine * attn_branch * attn_branch),
            jnp.sum(valid_mine * mlp_branch * mlp_branch),
            jnp.sum(valid_mine),
        ),
        ("seq", "fsdp"),
    )
    valid_count = jnp.maximum(stat_sums[3], 1.0)
    root_means = jnp.sqrt(jnp.stack([stat_sums[0], stat_sums[1], stat_sums[2]]) / (valid_count * D))
    back_attn = (
        lax.all_gather(w_qkv, "fsdp", axis=0, tiled=True),
        lax.all_gather(w_attn_out, "fsdp", axis=0, tiled=True),
        lax.all_gather(attn_gain, "fsdp", axis=0, tiled=True),
    )
    back_mlp = (
        lax.all_gather(w_in_proj, "fsdp", axis=0, tiled=True),
        lax.all_gather(w_out_proj, "fsdp", axis=0, tiled=True),
        lax.all_gather(mlp_gain, "fsdp", axis=0, tiled=True),
    )
    qkv_back, out_back = (back_attn[0], back_attn[1])
    in_back, down_back = (back_mlp[0], back_mlp[1])
    grad_result = cotangent[0].astype(jnp.float32)
    grad_mlp_low = grad_result.astype(jnp.bfloat16)
    grad_down = jnp.einsum(
        "tf,td->fd", hidden_low, grad_mlp_low, preferred_element_type=jnp.float32
    )
    grad_hidden = jnp.einsum(
        "td,fd->tf", grad_mlp_low, down_back, preferred_element_type=jnp.float32
    )
    _, gelu_pull = jax.vjp(gelu_gate, inner_in, inner_gate)
    grad_inner_in, grad_inner_gate = gelu_pull(grad_hidden)
    grad_widened = jnp.concatenate([grad_inner_in, grad_inner_gate], axis=1).astype(jnp.bfloat16)
    grad_in_weight = jnp.einsum(
        "td,tf->df", normed_two_low, grad_widened, preferred_element_type=jnp.float32
    )
    grad_normed_two = jnp.einsum(
        "tf,df->td", grad_widened, in_back, preferred_element_type=jnp.float32
    )
    _, second_pull = jax.vjp(norm_rows, middle, gain_two)
    grad_middle_part, grad_gain_two = second_pull(grad_normed_two)
    grad_middle = grad_result + grad_middle_part
    mlp_sums = (
        lax.psum_scatter(grad_in_weight, "fsdp", scatter_dimension=0, tiled=True),
        lax.psum_scatter(grad_down, "fsdp", scatter_dimension=0, tiled=True),
        lax.psum_scatter(grad_gain_two, "fsdp", scatter_dimension=0, tiled=True),
    )
    grad_attn_low = grad_middle.astype(jnp.bfloat16)
    grad_out_weight = jnp.einsum(
        "td,te->de", mixed_low, grad_attn_low, preferred_element_type=jnp.float32
    )
    grad_mixed = jnp.einsum(
        "te,de->td", grad_attn_low, out_back, preferred_element_type=jnp.float32
    ).astype(jnp.bfloat16)
    grad_by_heads = lax.all_to_all(
        grad_mixed.reshape(tokens, seq_size, head_local * HD),
        "seq",
        split_axis=1,
        concat_axis=0,
        tiled=True,
    )
    grad_by_heads = grad_by_heads.reshape(length, head_local, HD)
    query_grad, key_grad, value_grad = attend_backward(
        queries, key_heads, value_heads, grad_by_heads, log_sums, seg_all, valid_all
    )
    stacked = (
        jnp.stack([query_grad, key_grad, value_grad], axis=1)
        .astype(jnp.bfloat16)
        .reshape(length, 3, 1, head_local * HD)
    )
    grad_turned = (
        lax.all_to_all(stacked, "seq", split_axis=0, concat_axis=2, tiled=True)
        .reshape(tokens, 3, HEADS, HD)
        .astype(jnp.float32)
    )
    _, rope_pull = jax.vjp(rope_pair, projected[:, :2])
    (grad_pair,) = rope_pull(grad_turned[:, :2])
    grad_projected = (
        jnp.concatenate([grad_pair, grad_turned[:, 2:]], axis=1)
        .reshape(tokens, 3 * D)
        .astype(jnp.bfloat16)
    )
    grad_qkv_weight = jnp.einsum(
        "td,te->de", normed_low, grad_projected, preferred_element_type=jnp.float32
    )
    grad_normed = jnp.einsum(
        "te,de->td", grad_projected, qkv_back, preferred_element_type=jnp.float32
    )
    _, first_pull = jax.vjp(norm_rows, inputs, gain_one)
    grad_input_part, grad_gain_one = first_pull(grad_normed)
    grad_inputs = grad_middle + grad_input_part
    attn_sums = (
        lax.psum_scatter(grad_qkv_weight, "fsdp", scatter_dimension=0, tiled=True),
        lax.psum_scatter(grad_out_weight, "fsdp", scatter_dimension=0, tiled=True),
        lax.psum_scatter(grad_gain_one, "fsdp", scatter_dimension=0, tiled=True),
    )
    summed = lax.psum(
        (attn_sums[0], attn_sums[1], attn_sums[2], mlp_sums[0], mlp_sums[1], mlp_sums[2]), "seq"
    )
    final_grads = (summed[0], summed[1], summed[3], summed[4], summed[2], summed[5])
    return (
        result.astype(jnp.bfloat16)[None],
        grad_inputs[None],
        final_grads[0],
        final_grads[1],
        final_grads[2],
        final_grads[3],
        final_grads[4],
        final_grads[5],
        root_means,
    )


def solution(mesh):
    in_specs = (
        P("fsdp", "seq", None),
        P("fsdp", None),
        P("fsdp", None),
        P("fsdp", None),
        P("fsdp", None),
        P("fsdp", None),
        P("fsdp", None),
        P("fsdp"),
        P("fsdp"),
        P("fsdp", "seq", None),
    )
    out_specs = (
        P("fsdp", "seq", None),
        P("fsdp", "seq", None),
        P("fsdp", None),
        P("fsdp", None),
        P("fsdp", None),
        P("fsdp", None),
        P("fsdp"),
        P("fsdp"),
        P(),
    )
    return jax.shard_map(
        on_device, mesh=mesh, in_specs=in_specs, out_specs=out_specs, check_vma=False
    )
```

profile of v0, /device:TPU:0, one launch (start us, length us, event | category | flops | bytes accessed | tf_op | source)
XLA Modules:
  0.0 950.7 jit_solution(4761089183071408924)
XLA Ops:
  9.4 13.6 %all-gather = bf16[8,1,128]{2,1,0:T(2,128)(2,1)S(1)} all-gather(bf16[1,1,128]{2,1,0:T(2,128)(2,1)} %bitcast.267), channel_id=1, replica_groups=mesh['seq'=4,'fsdp'=8] {'fsdp'}, dimensions={0}, use_global_device_ids=true | all-gather | bytes 2304 | tf_op jit(solution)/shard_map/all_gather | solution.py:162
  24.8 52.3 %all-gather.7.cloned.1.call-done = bf16[1024,3072]{1,0:T(8,128)(2,1)} async-done(((bf16[128,3072]{1,0:T(8,128)(2,1)}), bf16[1024,3072]{1,0:T(8,128)(2,1)}) %all-gather.7.cloned.1.call-update) | async-done | bytes 6291472 | tf_op jit(solution)/shard_map/all_gather | solution.py:160
  77.1 8.7 copy.74
  85.8 4.8 fusion.65
  98.1 18.0 %all-to-all-done = bf16[256,3,4,256]{0,3,1,2:T(8,128)(2,1)S(1)} async-done(((bf16[256,3,4,256]{0,3,1,2:T(8,128)(2,1)}), bf16[256,3,4,256]{0,3,1,2:T(8,128)(2,1)S(1)}, u32[]{:S(2)}, u32[]{:S(2)}) %all-to-all-start) | async-done | bytes 1572896 | tf_op jit(solution)/shard_map/all_to_all | solution.py:186
  124.5 15.6 %while.27 = (s32[]{:T(128)}, bf16[2,512,4,64]{1,3,2,0:T(8,128)(2,1)S(1)}, f32[2,4,512]{2,1,0:T(4,128)S(1)}, s32[2,512]{1,0:T(2,128)S(1)}, s32[1,1024]{1,0:T(1,12...) while((s32[]{:T(128)}, ...), condition=%wide.region_5.6_spmd, body=%wide.region_2.5_spmd.sunk | while | flops 564132864 | bytes 29186172 | solution.py:74
  146.0 4.6 reduce.10
  152.6 4.1 all-to-all-start.1
  156.8 10.5 %all-gather.1 = bf16[8,1,128]{2,1,0:T(2,128)(2,1)S(1)} all-gather(bf16[1,1,128]{2,1,0:T(2,128)(2,1)S(1)} %bitcast.268), channel_id=1, replica_groups=mesh['seq'=4,'fsdp'=8] {'fsdp'}, dimensions={0}, use_global_device_ids=true | all-gather | bytes 2304 | tf_op jit(solution)/shard_map/all_gather | solution.py:167
  176.8 32.4 %all-gather.11.cloned.1.call-done = bf16[1024,5248]{1,0:T(8,128)(2,1)} async-done(((bf16[128,5248]{1,0:T(8,128)(2,1)}), bf16[1024,5248]{1,0:T(8,128)(2,1)}) %all-gather.11.cloned.1.call-update) | async-done | bytes 10747920 | tf_op jit(solution)/shard_map/all_gather | solution.py:165
  209.2 9.0 fusion.81
  218.2 47.9 %all-gather.13.cloned.1.call-done = bf16[2624,1024]{1,0:T(8,128)(2,1)} async-done(((bf16[328,1024]{1,0:T(8,128)(2,1)}), bf16[2624,1024]{1,0:T(8,128)(2,1)}) %all-gather.13.cloned.1.call-update) | async-done | bytes 5373968 | tf_op jit(solution)/shard_map/all_gather | solution.py:166
  266.1 9.1 add_convert_fusion
  275.2 6.3 fusion.47
  281.5 6.7 fusion.61
  293.7 7.0 fusion.67
  307.9 8.3 all-to-all-done.2
  321.0 42.2 %while.28 = (s32[]{:T(128)}, f32[1024,4,64]{0,2,1:T(8,128)S(1)}, f32[1024,4,64]{0,2,1:T(8,128)}, bf16[2,512,4,64]{1,3,2,0:T(8,128)(2,1)}, bf16[2,512,4,64]{1,3,2...) while((s32[]{:T(128)}, f32[1024,4,64]{0,2,1:T(8,128)S(1)}, ...), condition=%wide.region_12.13_spmd.clone, body=%wide.region_10.12_spmd.clone.sunk | while | flops 1377172480 | bytes 143735600 | solution.py:132
  333.3 4.8 fusion.149
  353.9 4.7 fusion.149
  358.6 4.6 fusion.148
  370.8 28.0 %all_to_all.54 = bf16[1024,3,1,256]{3,1,2,0:T(4,128)(2,1)S(1)} all-to-all(bf16[1024,3,1,256]{3,1,2,0:T(4,128)(2,1)S(1)} %copy.90), channel_id=1, replica_groups=mesh['seq'=4,'fsdp'=8] {'seq'}, dimensions={0} | all-to-all | bytes 3145728 | tf_op jit(solution)/shard_map/all_to_all | solution.py:283
  406.4 6.6 fusion.71
  414.2 11.0 %fusion.46 = f32[1024,5248]{1,0:T(8,128)} fusion(bf16[256,2624]{1,0:T(8,128)(2,1)} %get-tuple-element.352, bf16[256,2624]{1,0:T(8,128)(2,1)} %get-tuple-element.351, f32[256,1024]{1,0:T(8,128)S(1)} %copy-done.3, f32[1024]{0:T(1024)S(1)} %bitcast.254, f32[256]{0:T(256)S(1)} %fusion.74, f32[256]{0:T(256)S(1)} %broadcast_multiply_fusion), kind=kOutput, calls=%fused_computation.69 | convolution fusion | flops 2757885952 | bytes 25237504 | tf_op jit(solution)/shard_map/td,tf->df/dot_general | solution.py:245
  425.3 28.7 %reduce-scatter.11.cloned.1.call-done = f32[328,1024]{1,0:T(8,128)} async-done(((f32[2624,1024]{1,0:T(8,128)}), f32[328,1024]{1,0:T(8,128)}) %reduce-scatter.11.cloned.1.call-update) | async-done | bytes 1343504 | tf_op jit(solution)/shard_map/reduce_scatter | solution.py:256
  454.0 129.9 %reduce-scatter.5.cloned.1.call-done = f32[128,3072]{1,0:T(8,128)} async-done(((f32[1024,3072]{1,0:T(8,128)}), f32[128,3072]{1,0:T(8,128)}) %reduce-scatter.5.cloned.1.call-update) | async-done | bytes 1572880 | tf_op jit(solution)/shard_map/reduce_scatter | solution.py:304
  583.9 213.4 %reduce-scatter.9.cloned.1.call-done = f32[128,5248]{1,0:T(8,128)} async-done(((f32[1024,5248]{1,0:T(8,128)}), f32[128,5248]{1,0:T(8,128)}) %reduce-scatter.9.cloned.1.call-update) | async-done | bytes 2686992 | tf_op jit(solution)/shard_map/reduce_scatter | solution.py:255
  798.6 39.2 %all-reduce.8 = (f32[1]{0:T(128)}, f32[1]{0:T(128)}, f32[1]{0:T(128)}, f32[]{:T(128)}) all-reduce(f32[1]{0:T(128)} %bitcast.50, f32[1]{0:T(128)} %bitcast.49, f32[1]{0:T(128)} %bitcast.48, f32[]{:T(128)} %get-tuple-element.337), channel_id=1, replica_groups=mesh['seq'=4,'fsdp'=8] {'seq','fsdp'}, use_global_device_ids=true, to_apply=%region_34.35 | all-reduce | flops 4 | bytes 32 | tf_op jit(solution)/shard_map/psum | solution.py:211
  841.0 5.0 fusion.55
  847.5 16.0 %all-reduce.9 = (f32[1024]{0:T(1024)S(1)}, f32[1024]{0:T(1024)S(1)}) all-reduce(f32[1024]{0:T(1024)S(1)} %get-tuple-element.272, f32[1024]{0:T(1024)S(1)} %copy-done.36), channel_id=6, replica_groups=mesh['seq'=4,'fsdp'=8] {'fsdp'}, use_global_device_ids=true, to_apply=%region_24.25.clone | all-reduce | flops 2048 | bytes 16384
  863.6 9.2 all-reduce.10
  875.7 60.8 %all-reduce.14.cloned.1.call-done = (f32[128,3072]{1,0:T(8,128)}, f32[128,1024]{1,0:T(8,128)}, f32[128,5248]{1,0:T(8,128)}, f32[328,1024]{1,0:T(8,128)}) async-done(((f32[128,3072]{1,0:T(8,128)}, f32[128,1024]{1,0:T(8,128)}, f32[128,5248]{1,0:T(8,128)}, f32[328,1024]{1,0:T(8,128)}), (f32[128,3072]{1,0:T(8,128)}, f32[128,1024]{1,0:T(8,128)}, f32[128,5248]{1,0:T(8,128)}, ...) | async-done | bytes 6127632 | tf_op jit(solution)/shard_map/psum | solution.py:308
  (218 shorter events, 129.4 us)
Async XLA Ops:
  7.2 17.1 %copy-start.4 = (bf16[1,256,1024]{2,1,0:T(8,128)(2,1)S(1)}, bf16[1,256,1024]{2,1,0:T(8,128)(2,1)}, u32[]{:S(2)}) copy-start(bf16[1,256,1024]{2,1,0:T(8,128)(2,1)} %param.14) | copy-start | bytes 1572868
  7.2 69.9 %all-gather.7.cloned.1.call-start = ((), (), s32[]{:S(2)}) async-start(), calls=%async_computation.8 | async-start | bytes 7077888 | tf_op jit(solution)/shard_map/all_gather | solution.py:160
  7.9 165.1 %all-gather.9.cloned.1.call-start = ((), (), s32[]{:S(2)}) async-start(), calls=%async_computation.9 | async-start | bytes 2359296 | tf_op jit(solution)/shard_map/all_gather | solution.py:161
  8.7 200.5 %all-gather.11.cloned.1.call-start = ((), (), s32[]{:S(2)}) async-start(), calls=%async_computation.10 | async-start | bytes 12091392 | tf_op jit(solution)/shard_map/all_gather | solution.py:165
  23.0 62.7 %copy-start.26 = (f32[8,1,128]{2,1,0:T(1,128)}, f32[8,1,128]{2,1,0:T(1,128)S(1)}, u32[]{:S(2)}) copy-start(f32[8,1,128]{2,1,0:T(1,128)S(1)} %convert_element_type.149) | copy-start | bytes 12292
  24.3 61.5 %copy-start.28 = (f32[256]{0:T(256)}, f32[256]{0:T(256)S(1)}, u32[]{:S(2)}) copy-start(f32[256]{0:T(256)S(1)} %broadcast_multiply_fusion.1) | copy-start | bytes 3076
  24.6 61.2 %copy-start.34 = (f32[256]{0:T(256)}, f32[256]{0:T(256)S(1)}, u32[]{:S(2)}) copy-start(f32[256]{0:T(256)S(1)} %fusion.54) | copy-start | bytes 3076
  24.6 61.2 %copy-start.30 = (f32[256]{0:T(256)}, f32[256]{0:T(256)S(1)}, u32[]{:S(2)}) copy-start(f32[256]{0:T(256)S(1)} %fusion.73) | copy-start | bytes 3076
  24.8 66.1 %copy-start.22 = (f32[256,32]{0,1:T(8,128)}, f32[256,32]{0,1:T(8,128)S(1)}, u32[]{:S(2)}) copy-start(f32[256,32]{0,1:T(8,128)S(1)} %get-tuple-element.374) | copy-start | bytes 98308
  24.8 66.1 %copy-start.24 = (f32[256,32]{0,1:T(8,128)}, f32[256,32]{0,1:T(8,128)S(1)}, u32[]{:S(2)}) copy-start(f32[256,32]{0,1:T(8,128)S(1)} %get-tuple-element.375) | copy-start | bytes 98308
  91.4 6.1 copy-start.20
  92.7 23.5 %all-to-all-start = ((bf16[256,3,4,256]{0,3,1,2:T(8,128)(2,1)}), bf16[256,3,4,256]{0,3,1,2:T(8,128)(2,1)S(1)}, u32[]{:S(2)}, u32[]{:S(2)}) async-start(bf16[256,3,4,256]{0,3,1,2:T(8,128)(2,1)} %pad_maximum_fusion.3), calls=%async_computation | async-start | bytes 3145728 | tf_op jit(solution)/shard_map/all_to_all | solution.py:186
  96.4 169.7 %all-gather.13.cloned.1.call-start = ((), (), s32[]{:S(2)}) async-start(), calls=%async_computation.11 | async-start | bytes 6045696 | tf_op jit(solution)/shard_map/all_gather | solution.py:166
  141.5 15.3 %copy-start.37 = (bf16[128]{0:T(256)(128)(2,1)S(1)}, bf16[128]{0:T(256)(128)(2,1)}, u32[]{:S(2)}) copy-start(bf16[128]{0:T(256)(128)(2,1)} %param.22) | copy-start | bytes 772
  152.6 15.3 %all-to-all-start.1 = ((bf16[4,2,32768]{2,1,0:T(2,128)(2,1)}), bf16[4,2,32768]{2,1,0:T(2,128)(2,1)}, u32[]{:S(2)}, u32[]{:S(2)}) async-start(bf16[4,2,32768]{2,1,0:T(2,128)(2,1)} %reshape.507), calls=%async_computation.1 | async-start | bytes 1048576 | tf_op jit(solution)/shard_map/all_to_all | solution.py:199
  156.7 268.6 %reduce-scatter.7.cloned.1.call-start = ((), (), s32[]{:S(2)}) async-start(), calls=%async_computation.13 | async-start | bytes 4718592 | tf_op jit(solution)/shard_map/reduce_scatter | solution.py:305
  176.5 111.7 %copy-start.2 = (f32[256,1024]{1,0:T(8,128)}, f32[256,1024]{1,0:T(8,128)S(1)}, u32[]{:S(2)}) copy-start(f32[256,1024]{1,0:T(8,128)S(1)} %get-tuple-element.342) | copy-start | bytes 3145732
  209.2 56.9 %copy-start.12 = (bf16[1,256,1024]{2,1,0:T(8,128)(2,1)S(1)}, bf16[1,256,1024]{2,1,0:T(8,128)(2,1)}, u32[]{:S(2)}) copy-start(bf16[1,256,1024]{2,1,0:T(8,128)(2,1)} %param.23) | copy-start | bytes 1572868
  266.1 9.1 copy-start.6
  275.2 6.3 copy-start.17
  281.5 6.8 copy-start.19
  292.7 161.3 %reduce-scatter.11.cloned.1.call-start = ((), (), s32[]{:S(2)}) async-start(), calls=%async_computation.15 | async-start | bytes 12091392 | tf_op jit(solution)/shard_map/reduce_scatter | solution.py:256
  304.0 12.2 %all-to-all-start.2 = ((bf16[256,4,256]{0,2,1:T(8,128)(2,1)}), bf16[256,4,256]{0,2,1:T(8,128)(2,1)S(1)}, u32[]{:S(2)}, u32[]{:S(2)}) async-start(bf16[256,4,256]{0,2,1:T(8,128)(2,1)} %bitcast.33), calls=%async_computation.2 | async-start | bytes 1048576 | tf_op jit(solution)/shard_map/all_to_all | solution.py:266
  307.7 276.2 %reduce-scatter.5.cloned.1.call-start = ((), (), s32[]{:S(2)}) async-start(), calls=%async_computation.12 | async-start | bytes 14155776 | tf_op jit(solution)/shard_map/reduce_scatter | solution.py:304
  330.0 8.2 copy-start.1
  350.6 8.0 copy-start.1
  413.0 384.3 %reduce-scatter.9.cloned.1.call-start = ((), (), s32[]{:S(2)}) async-start(), calls=%async_computation.14 | async-start | bytes 24182784 | tf_op jit(solution)/shard_map/reduce_scatter | solution.py:255
  425.2 372.1 %copy-start.38 = (u32[32]{0:T(128)S(1)}, u32[32]{0:T(128)}, u32[]{:S(2)}) copy-start(u32[32]{0:T(128)} %constant.113) | copy-start | bytes 388
  425.2 511.3 %all-reduce.14.cloned.1.call-start = ((), (), s32[]{:S(2)}) async-start(), calls=%async_computation.16 | async-start | bytes 12255232 | tf_op jit(solution)/shard_map/psum | solution.py:308
  840.9 6.5 copy-start.36
  841.0 31.9 %copy-start.8 = (f32[256,1024]{1,0:T(8,128)S(1)}, f32[256,1024]{1,0:T(8,128)}, u32[]{:S(2)}) copy-start(f32[256,1024]{1,0:T(8,128)} %copy-done.7) | copy-start | bytes 3145732
  841.0 31.9 %copy-start.33 = (f32[256]{0:T(256)S(1)}, f32[256]{0:T(256)}, u32[]{:S(2)}) copy-start(f32[256]{0:T(256)} %copy-done.32) | copy-start | bytes 3076
  (23 other events, 55.5 us)
Sparse Core Ops, SparseCore 0:
  9.6 67.4 all-gather.6
  78.7 27.8 all-gather.8
  108.2 100.9 all-gather.10
  210.7 55.3 all-gather.12
  292.8 48.6 reduce-scatter.6
  343.7 110.2 reduce-scatter.10
  456.3 127.5 reduce-scatter.4
  586.3 210.9 reduce-scatter.8
  801.2 135.2 all-reduce.13
where the time goes:
time: 956 us; the launch traced here: 951 us
  waiting for transfers between devices  594 us (62%)
  matrix products  117 us (12%)
  blocking collectives  116 us (12%)
  local copies, waits for them, and re-layouts  60.1 us (6%)
  other arithmetic  34.9 us (4%)
  between operations  16 us (2%)
  starting transfers between devices  12.1 us (1%)
    reduce_scatter x1, waiting for transfers between devices, on_device(): lax.psum_scatter(grad_in_weight, 'fsdp', scatter_dimension=0, tiled=True)  213 us
    reduce_scatter x1, waiting for transfers between devices, on_device(): lax.psum_scatter(grad_qkv_weight, 'fsdp', scatter_dimension=0, tiled=True)  130 us
    psum x1, waiting for transfers between devices, on_device(): lax.psum((attn_sums[0], attn_sums[1], attn_sums[2], mlp_sums[0], mlp_sums...  60.8 us
    all_gather x1, waiting for transfers between devices, on_device(): lax.all_gather(w_qkv, 'fsdp', axis=0, tiled=True)  52.3 us
    all_gather x1, waiting for transfers between devices, on_device(): lax.all_gather(w_out_proj, 'fsdp', axis=0, tiled=True)  47.9 us
    psum x1, blocking collectives, on_device(): lax.psum((jnp.sum(valid_mine * result * result), jnp.sum(valid_mine * att...  39.2 us
    all_gather x1, waiting for transfers between devices, on_device(): lax.all_gather(w_in_proj, 'fsdp', axis=0, tiled=True)  32.4 us
    reduce_scatter x1, waiting for transfers between devices, on_device(): lax.psum_scatter(grad_down, 'fsdp', scatter_dimension=0, tiled=True)  28.7 us
  transfers between devices with their start and end apart: 12, of which 9 were waited for; matrix products, arithmetic and copies ran while one was open for 18% of the time, Pallas kernels for 0%

commit v1 on v0

v1 whole, which is shorter than its diff:
```python
import functools

import jax
import jax.numpy as jnp
from jax import lax
from jax.experimental import pallas as pl
from jax.experimental.pallas import tpu as pltpu
from jax.sharding import PartitionSpec as P

D = 1024
HEADS = 16
HD = 64
FF = 2624

ROPE_BASE = 160000.0
NORM_EPS = 1e-05
BF = jnp.bfloat16
F32 = jnp.float32


def swap(x, axis, bit):
    return lax.ppermute(x, axis, [(i, i ^ bit) for i in range(lax.axis_size(axis))])


def share_seq(block):
    size = lax.axis_size("seq")
    if size != 4:
        return [block] + [swap(block, "seq", k) for k in range(1, size)]
    half = block.shape[0] // 2
    one = swap(block, "seq", 1)
    two = swap(block, "seq", 2)
    upper = swap(two[:half], "seq", 1)
    lower = swap(one[half:], "seq", 2)
    return [block, one, two, jnp.concatenate([upper, lower], axis=0)]


def reduce_seq(blocks):
    total = blocks[0]
    for k in range(1, len(blocks)):
        total = total + swap(blocks[k].astype(BF), "seq", k).astype(F32)
    return total


def reduce_seq_relay(blocks):
    if len(blocks) != 4:
        return reduce_seq(blocks)
    own, one, two, three = blocks
    half = own.shape[0] // 2
    upper = swap(three[:half].astype(BF), "seq", 1).astype(F32)
    lower = swap(three[half:].astype(BF), "seq", 2).astype(F32)
    to_two = jnp.concatenate([two[:half] + upper, two[half:]], axis=0).astype(BF)
    to_one = jnp.concatenate([one[:half], one[half:] + lower], axis=0).astype(BF)
    return own + swap(to_two, "seq", 2).astype(F32) + swap(to_one, "seq", 1).astype(F32)


def paired():
    return lax.axis_size("fsdp") == 2 * lax.axis_size("seq")


def spread_rows(block):
    size = lax.axis_size("fsdp")
    same = [block] + [swap(block, "fsdp", k) for k in range(2, size, 2)]
    other = [swap(b, "fsdp", 1) for b in same]
    return [b for pair in zip(same, other) for b in pair]


def gather_rows(block):
    if not paired():
        return lax.all_gather(block, "fsdp", axis=0)
    me = lax.axis_index("fsdp")
    parts = spread_rows(block)
    whole = jnp.zeros((len(parts),) + block.shape, block.dtype)
    for k, part in enumerate(parts):
        whole = lax.dynamic_update_index_in_dim(whole, part, me ^ k, 0)
    return whole


def transpose_devices(x):
    seq, fsdp = lax.axis_size("seq"), lax.axis_size("fsdp")
    pairs = [
        (s * fsdp + 2 * z + c, z * fsdp + 2 * s + c)
        for s in range(seq)
        for z in range(fsdp // 2)
        for c in range(2)
    ]
    return lax.ppermute(x, ("seq", "fsdp"), pairs)


def stack_seq(block):
    me = lax.axis_index("seq")
    parts = share_seq(block)
    whole = jnp.zeros((len(parts),) + block.shape, block.dtype)
    for k, part in enumerate(parts):
        whole = lax.dynamic_update_index_in_dim(whole, part, me ^ k, 0)
    return whole


def reduce_z(blocks):
    count = blocks.shape[0]
    z = lax.axis_index("fsdp") // 2
    low = blocks.astype(BF)
    total = lax.dynamic_index_in_dim(blocks, z, 0, keepdims=False)
    for k in range(1, count):
        part = lax.dynamic_index_in_dim(low, z ^ k, 0, keepdims=False)
        total = total + swap(part, "fsdp", 2 * k).astype(F32)
    return total


def reduce_core(pairs):
    core = lax.axis_index("fsdp") % 2
    away = lax.dynamic_index_in_dim(pairs, 1 - core, 1, keepdims=False)
    mine = lax.dynamic_index_in_dim(pairs, core, 1, keepdims=False)
    return mine + swap(away.astype(BF), "fsdp", 1).astype(F32)


def reduce_rows(partial):
    size = lax.axis_size("fsdp")
    if not paired():
        return lax.psum_scatter(partial, "fsdp", scatter_dimension=0, tiled=True)
    rows = partial.shape[0] // size
    return reduce_z(reduce_core(partial.reshape(size // 2, 2, rows, partial.shape[1])))


def sum_everywhere(values):
    for axis in ("fsdp", "seq"):
        bit = 1
        while bit < lax.axis_size(axis):
            values = values + swap(values, axis, bit)
            bit *= 2
    return values


def gather_gains(gains):
    size, rows = lax.axis_size("fsdp"), gains.shape[1]
    whole = jnp.zeros((2, size * rows), gains.dtype)
    whole = lax.dynamic_update_slice(whole, gains, (0, lax.axis_index("fsdp") * rows))
    bit = 1
    while bit < size:
        whole = whole + swap(whole, "fsdp", bit)
        bit *= 2
    return whole


def half_swap(values):
    width = values.shape[1]
    lane = lax.broadcasted_iota(jnp.int32, values.shape, 1)
    ahead = pltpu.roll(values, width - HD // 2, 1)
    behind = pltpu.roll(values, HD // 2, 1)
    return jnp.where(lane % HD < HD // 2, ahead, behind)


def wide(table, width):
    return jnp.concatenate([table] * (width // table.shape[1]), axis=1)


def qkv_kernel(*refs):
    count = 4
    xs = refs[:count]
    w_ref, gain_ref, cos_ref, sin_ref, a_ref, q_ref, k_ref, v_ref, held = refs[count:]
    step = pl.program_id(0)
    for i in range(count):

        @pl.when(step == i)
        def _():
            held[...] = xs[i][...].astype(F32)

    values = held[...]
    centered = values - jnp.mean(values, axis=1, keepdims=True)
    variance = jnp.mean(centered * centered, axis=1, keepdims=True)
    low = (centered * lax.rsqrt(variance + NORM_EPS) * gain_ref[...]).astype(BF)
    a_ref[...] = low
    p = jnp.dot(low, w_ref[...], preferred_element_type=F32)
    part = p.shape[1] // 3
    turned = p[:, : 2 * part]
    turned = turned * wide(cos_ref[...], 2 * part) + half_swap(turned) * wide(sin_ref[...], 2 * part)
    q_ref[...] = turned[:, :part].astype(BF) * (HD**-0.5)
    k_ref[...] = turned[:, part:].astype(BF)
    v_ref[...] = p[:, 2 * part :].astype(BF)


def project_qkv(blocks, weight, gain, cosine, sine):
    rows, width = blocks[0].shape
    part = weight.shape[1] // 3
    count = len(blocks)
    whole = lambda a: pl.BlockSpec(a.shape, lambda i: (0, 0))
    tile = lambda n: pl.BlockSpec((rows, n), lambda i: (i, 0))
    shape = lambda n: jax.ShapeDtypeStruct((rows * count, n), BF)
    return pl.pallas_call(
        qkv_kernel,
        grid=(count,),
        in_specs=[whole(b) for b in blocks]
        + [whole(weight), whole(gain), tile(cosine.shape[1]), tile(sine.shape[1])],
        out_specs=[tile(width), tile(part), tile(part), tile(part)],
        out_shape=[shape(width), shape(part), shape(part), shape(part)],
        scratch_shapes=[pltpu.VMEM((rows, width), F32)],
        cost_estimate=pl.CostEstimate(
            flops=2 * rows * count * width * 3 * part,
            bytes_accessed=2 * rows * count * (2 * width + 3 * part) + 2 * width * 3 * part,
            transcendentals=0,
        ),
        name="qkv",
    )(*blocks, weight, gain, cosine, sine)


def mask_bias(seg_col, valid_col, seg_row, first_row):
    shape = (seg_col.shape[0], seg_row.shape[1])
    key = lax.broadcasted_iota(jnp.int32, shape, 0)
    query = lax.broadcasted_iota(jnp.int32, shape, 1) + first_row
    allowed = (seg_col == seg_row) & ((valid_col > 0) | (key == query))
    return jnp.where(allowed, 0.0, -1e30)


def forward_kernel(q_ref, k_ref, v_ref, segc_ref, valc_ref, segr_ref, o_ref, lse_ref, vt_ref, ot_ref, bias_ref):
    step = pl.program_id(0)
    rows, width = q_ref.shape

    @pl.when(step == 0)
    def _():
        vt_ref[...] = v_ref[...].T

    bias_ref[...] = mask_bias(segc_ref[...], valc_ref[...], segr_ref[...], step * rows)
    qt = q_ref[...].T
    feature = lax.broadcasted_iota(jnp.int32, qt.shape, 0) // HD

    def head(h, carry):
        mine = jnp.where(feature == h, qt, jnp.zeros_like(qt))
        scores = jnp.dot(k_ref[...], mine, preferred_element_type=F32) + bias_ref[...]
        top = jnp.max(scores, axis=0, keepdims=True)
        exponent = jnp.exp(scores - top)
        total = jnp.sum(exponent, axis=0, keepdims=True)
        weights = (exponent * (1.0 / total)).astype(BF)
        start = pl.multiple_of(h * HD, HD)
        ot_ref[pl.ds(start, HD), :] = jnp.dot(
            vt_ref[pl.ds(start, HD), :], weights, preferred_element_type=F32
        )
        lse_ref[pl.ds(h, 1), :] = top + jnp.log(total)
        return carry

    lax.fori_loop(0, width // HD, head, 0)
    o_ref[...] = ot_ref[...].T.astype(BF)


def attend_forward(q, k, v, seg_col, valid_col, seg_row, rows):
    length, width = q.shape
    whole = lambda a: pl.BlockSpec(a.shape, lambda i: (0, 0))
    tile = pl.BlockSpec((rows, width), lambda i: (i, 0))
    return pl.pallas_call(
        forward_kernel,
        grid=(length // rows,),
        in_specs=[tile, whole(k), whole(v), whole(seg_col), whole(valid_col), pl.BlockSpec((1, rows), lambda i: (0, i))],
        out_specs=[tile, pl.BlockSpec((8, rows), lambda i: (0, i))],
        out_shape=[jax.ShapeDtypeStruct((length, width), BF), jax.ShapeDtypeStruct((8, length), F32)],
        scratch_shapes=[pltpu.VMEM((width, length), BF), pltpu.VMEM((width, rows), F32), pltpu.VMEM((length, rows), F32)],
        cost_estimate=pl.CostEstimate(
            flops=4 * length * length * width, bytes_accessed=8 * length * width, transcendentals=length * length * 4
        ),
        name="attend",
    )(q, k, v, seg_col, valid_col, seg_row)


def backward_kernel(
    q_ref, go_ref, lse_ref, k_ref, v_ref, segc_ref, valc_ref, segr_ref, cos_ref, sin_ref,
    gp_ref, kt_ref, dk_ref, dv_ref, dqt_ref, bias_ref,
):
    step = pl.program_id(0)
    rows, width = q_ref.shape

    @pl.when(step == 0)
    def _():
        kt_ref[...] = k_ref[...].T
        dk_ref[...] = jnp.zeros_like(dk_ref)
        dv_ref[...] = jnp.zeros_like(dv_ref)

    bias_ref[...] = mask_bias(segc_ref[...], valc_ref[...], segr_ref[...], step * rows)
    qt, got = q_ref[...].T, go_ref[...].T
    feature = lax.broadcasted_iota(jnp.int32, qt.shape, 0) // HD
    lane = lax.broadcasted_iota(jnp.int32, (rows, width), 1) // HD
    none = jnp.zeros_like(qt)
    none_row = jnp.zeros((rows, width), BF)

    def head(h, carry):
        scores = jnp.dot(k_ref[...], jnp.where(feature == h, qt, none), preferred_element_type=F32)
        weights = jnp.exp(scores + bias_ref[...] - lse_ref[pl.ds(h, 1), :])
        upstream = jnp.dot(v_ref[...], jnp.where(feature == h, got, none), preferred_element_type=F32)
        inner = jnp.sum(weights * upstream, axis=0, keepdims=True)
        low = (weights * (upstream - inner)).astype(BF)
        dv_ref[...] += jnp.dot(
            weights.astype(BF), jnp.where(lane == h, go_ref[...], none_row), preferred_element_type=F32
        )
        dk_ref[...] += jnp.dot(low, jnp.where(lane == h, q_ref[...], none_row), preferred_element_type=F32)
        start = pl.multiple_of(h * HD, HD)
        dqt_ref[pl.ds(start, HD), :] = jnp.dot(kt_ref[pl.ds(start, HD), :], low, preferred_element_type=F32)
        return carry

    lax.fori_loop(0, width // HD, head, 0)

    def unturn(values, cosine, sine):
        values = values.astype(BF).astype(F32)
        return (values * wide(cosine, width) - half_swap(values) * wide(sine, width)).astype(BF)

    here = pl.ds(pl.multiple_of(step * rows, rows), rows)
    gp_ref[here, :width] = unturn(dqt_ref[...].T * (HD**-0.5), cos_ref[here, :], sin_ref[here, :])

    @pl.when(step == pl.num_programs(0) - 1)
    def _():
        gp_ref[:, width : 2 * width] = unturn(dk_ref[...], cos_ref[...], sin_ref[...])
        gp_ref[:, 2 * width :] = dv_ref[...].astype(BF)


def attend_backward(q, k, v, grad_out, lse, seg_col, valid_col, seg_row, cosine, sine, rows):
    length, width = q.shape
    whole = lambda a: pl.BlockSpec(a.shape, lambda i: (0, 0))
    tile = pl.BlockSpec((rows, width), lambda i: (i, 0))
    return pl.pallas_call(
        backward_kernel,
        grid=(length // rows,),
        in_specs=[
            tile, tile, pl.BlockSpec((8, rows), lambda i: (0, i)), whole(k), whole(v),
            whole(seg_col), whole(valid_col), pl.BlockSpec((1, rows), lambda i: (0, i)), whole(cosine), whole(sine),
        ],
        out_specs=pl.BlockSpec((length, 3 * width), lambda i: (0, 0)),
        out_shape=jax.ShapeDtypeStruct((length, 3 * width), BF),
        scratch_shapes=[
            pltpu.VMEM((width, length), BF), pltpu.VMEM((length, width), F32), pltpu.VMEM((length, width), F32),
            pltpu.VMEM((width, rows), F32), pltpu.VMEM((length, rows), F32),
        ],
        cost_estimate=pl.CostEstimate(
            flops=10 * length * length * width, bytes_accessed=20 * length * width, transcendentals=length * length * 4
        ),
        name="attend_back",
    )(q, grad_out, lse, k, v, seg_col, valid_col, seg_row, cosine, sine)


def normal(values):
    centered = values - jnp.mean(values, axis=-1, keepdims=True)
    scale = lax.rsqrt(jnp.mean(centered * centered, axis=-1, keepdims=True) + NORM_EPS)
    return centered * scale, scale


def norm_back(upstream, gain, values):
    unit, scale = normal(values)
    weighted = upstream * gain
    return scale * (
        weighted
        - jnp.mean(weighted, axis=-1, keepdims=True)
        - unit * jnp.mean(weighted * unit, axis=-1, keepdims=True)
    )


def gelu_gate(inputs, gates):
    return 0.5 * inputs * (1.0 + lax.erf(inputs * 0.7071067811865476)) * gates


def matmul(a, b):
    return jnp.dot(a, b, preferred_element_type=F32)


def matmul_nt(a, b):
    return lax.dot_general(a, b, (((1,), (1,)), ((), ())), preferred_element_type=F32)


def matmul_tn(a, b):
    return lax.dot_general(a, b, (((0,), (0,)), ((), ())), preferred_element_type=F32)


def on_device(
    hidden_in, segment_ids, valid_tokens, w_qkv, w_attn_out, w_in_proj, w_out_proj, attn_gain, mlp_gain, cotangent
):
    seq_size, fsdp_size = lax.axis_size("seq"), lax.axis_size("fsdp")
    seq, fsdp = lax.axis_index("seq"), lax.axis_index("fsdp")
    x_low, cot = hidden_in[0], cotangent[0]
    tokens = x_low.shape[0]
    length = tokens * seq_size
    part = D // seq_size
    hidden = FF // seq_size
    rel = [seq ^ k for k in range(seq_size)]

    x_blocks = share_seq(x_low)
    gains = gather_gains(jnp.stack([attn_gain, mlp_gain])).astype(F32)
    gain_one, gain_two = gains[0:1], gains[1:2]
    qkv_mine = jnp.concatenate(
        [lax.dynamic_slice_in_dim(w_qkv, i * D + seq * part, part, axis=1) for i in range(3)], axis=1
    )
    qkv_weight = gather_rows(qkv_mine).reshape(D, 3 * part)
    cot_blocks = share_seq(cot)
    in_mine = jnp.stack(
        [lax.dynamic_slice_in_dim(w_in_proj, i * FF + seq * hidden, hidden, axis=1) for i in range(2)]
    )
    in_weight = jnp.swapaxes(gather_rows(in_mine), 0, 1).reshape(2, D, hidden)
    if paired():
        down_mine = transpose_devices(lax.dynamic_slice_in_dim(w_out_proj, seq * part, part, axis=1))
        down_weight = gather_rows(down_mine).reshape(seq_size, 2, down_mine.shape[0], part)
        down_weight = down_weight.transpose(1, 2, 0, 3).reshape(hidden, D)
        out_mine = gather_rows(lax.dynamic_slice_in_dim(w_attn_out, seq * part, part, axis=1)).reshape(D, part)
        out_cols = stack_seq(out_mine)
        out_weight = jnp.swapaxes(out_cols, 0, 1).reshape(D, D)
    else:
        down_weight = lax.all_gather(w_out_proj, "fsdp", axis=0, tiled=True)
        down_weight = lax.dynamic_slice_in_dim(down_weight, seq * hidden, hidden, axis=0)
        out_weight = lax.all_gather(w_attn_out, "fsdp", axis=0, tiled=True)

    def by_block(row):
        return jnp.concatenate([lax.dynamic_slice_in_dim(row, r * tokens, tokens) for r in rel])

    seg_all, valid_all = by_block(segment_ids[0]), by_block(valid_tokens[0])
    positions = by_block(jnp.arange(length, dtype=jnp.int32))
    frequency = ROPE_BASE ** (-2.0 * jnp.arange(HD // 2, dtype=F32) / HD)
    angles = positions.astype(F32)[:, None] * frequency[None, :]
    cosine, sine = lax.optimization_barrier((jnp.cos(angles), jnp.sin(angles)))
    cosine = jnp.concatenate([cosine] * 4, axis=1)
    sine = jnp.concatenate([-sine, sine] * 2, axis=1)
    seg_col, valid_col, seg_row = seg_all[:, None], valid_all[:, None], seg_all[None, :]

    a_low, q, k, v = project_qkv(x_blocks, qkv_weight, gain_one, cosine, sine)
    mixed, lse = attend_forward(q, k, v, seg_col, valid_col, seg_row, tokens)

    def to_tokens(blocks):
        came = [blocks[:tokens]] + [
            swap(blocks[i * tokens : (i + 1) * tokens], "seq", i) for i in range(1, seq_size)
        ]
        whole = jnp.zeros((tokens, D), blocks.dtype)
        for r, block in zip(rel, came):
            whole = lax.dynamic_update_slice(whole, block, (0, r * part))
        return whole

    mixed_low = to_tokens(mixed)
    x = x_low.astype(F32)
    attn_branch = matmul(mixed_low, out_weight)
    middle = x + attn_branch
    normed_two = (normal(middle)[0] * gain_two).astype(BF)

    b_blocks = share_seq(normed_two)
    m_blocks, gz_i, gz_g, gb_blocks = [], [], [], []
    for b, g in zip(b_blocks, cot_blocks):
        grad_hidden = matmul_nt(g, down_weight)
        inner, gate = matmul(b, in_weight[0]), matmul(b, in_weight[1])
        value, pull = jax.vjp(gelu_gate, inner, gate)
        gi, gg = pull(grad_hidden)
        gi, gg = gi.astype(BF), gg.astype(BF)
        m_blocks.append(value.astype(BF))
        gz_i.append(gi)
        gz_g.append(gg)
        gb_blocks.append(matmul_nt(gi, in_weight[0]) + matmul_nt(gg, in_weight[1]))
    grad_normed_two = reduce_seq(gb_blocks)
    grad_middle = cot.astype(F32) + norm_back(grad_normed_two, gain_two, middle)
    grad_attn_low = grad_middle.astype(BF)
    grad_mixed = matmul_nt(grad_attn_low, out_weight).astype(BF)

    def to_heads(blocks):
        sent = [lax.dynamic_slice_in_dim(blocks, r * part, part, axis=1) for r in rel]
        return jnp.concatenate([sent[0]] + [swap(sent[i], "seq", i) for i in range(1, seq_size)], axis=0)

    grad_by_heads = to_heads(grad_mixed)

    mlp_branch = reduce_seq([matmul(m, down_weight) for m in m_blocks])
    result = middle + mlp_branch
    valid_mine = valid_all[:tokens].astype(F32)[:, None]
    stats = jnp.stack(
        [
            jnp.sum(valid_mine * result * result),
            jnp.sum(valid_mine * attn_branch * attn_branch),
            jnp.sum(valid_mine * mlp_branch * mlp_branch),
            jnp.sum(valid_mine),
        ]
    )
    stats = sum_everywhere(jnp.broadcast_to(stats[:, None], (4, 128)))[:, 0]
    root_means = jnp.sqrt(stats[:3] / (jnp.maximum(stats[3], 1.0) * D))

    def share_columns(mine):
        rows, count, width = mine.shape
        low = mine.astype(BF)
        if paired():
            every = stack_seq(low)
        else:
            every = lax.all_gather(low, "seq", axis=0)
        return every.transpose(1, 2, 0, 3).reshape(rows, count * seq_size * width).astype(F32)

    b_all, m_all = jnp.concatenate(b_blocks), jnp.concatenate(m_blocks)
    cot_all = jnp.concatenate(cot_blocks)
    gz_all = jnp.concatenate([jnp.concatenate(gz_i), jnp.concatenate(gz_g)], axis=1)
    grad_in_mine = reduce_rows(matmul_tn(b_all, gz_all))
    grad_in_weight = share_columns(grad_in_mine.reshape(-1, 2, hidden))
    grad_down_part = matmul_tn(m_all, cot_all)
    grad_out_part = matmul_tn(mixed_low, grad_attn_low)
    if paired():
        rows = hidden // 2
        halves = reduce_core(grad_down_part.reshape(1, 2, rows, D))[0]
        quarter = reduce_z(halves.reshape(rows, seq_size, part).transpose(1, 0, 2))
        quarter = transpose_devices(quarter.astype(BF)).astype(F32)
        grad_down = share_columns(quarter[:, None, :])
        rows = D // fsdp_size
        out_core = reduce_core(grad_out_part.reshape(fsdp_size // 2, 2, rows, D)).reshape(D // 2, D)
        out_seq = reduce_seq([lax.dynamic_slice_in_dim(out_core, r * part, part, axis=1) for r in rel])
        out_mine = reduce_z(out_seq.reshape(fsdp_size // 2, rows, part))
        grad_out_weight = share_columns(out_mine[:, None, :])
    else:
        spread = jnp.zeros((FF, D), F32)
        spread = lax.dynamic_update_slice(spread, grad_down_part, (seq * hidden, 0))
        grad_down = lax.psum(lax.psum_scatter(spread, "fsdp", scatter_dimension=0, tiled=True), "seq")
        grad_out_weight = lax.psum(
            lax.psum_scatter(grad_out_part, "fsdp", scatter_dimension=0, tiled=True), "seq"
        )

    gp = attend_backward(
        q, k, v, grad_by_heads, lse, seg_col, valid_col, seg_row, cosine, sine, tokens
    )
    ga_parts = matmul_nt(gp, qkv_weight)
    grad_qkv_mine = reduce_rows(matmul_tn(a_low, gp))
    grad_normed = reduce_seq_relay([ga_parts[i * tokens : (i + 1) * tokens] for i in range(seq_size)])
    grad_inputs = grad_middle + norm_back(grad_normed, gain_one, x)
    grad_qkv_weight = share_columns(grad_qkv_mine.reshape(-1, 3, part))

    def gain_gradient(weight, gradient, gain):
        return jnp.sum(weight.astype(F32) * gradient, axis=1) / gain.astype(F32)

    return (
        result.astype(BF)[None],
        grad_inputs[None],
        grad_qkv_weight,
        grad_out_weight,
        grad_in_weight,
        grad_down,
        gain_gradient(w_qkv, grad_qkv_weight, attn_gain),
        gain_gradient(w_in_proj, grad_in_weight, mlp_gain),
        root_means,
    )


def solution(mesh):
    in_specs = (
        P("fsdp", "seq", None),
        P("fsdp", None),
        P("fsdp", None),
        P("fsdp", None),
        P("fsdp", None),
        P("fsdp", None),
        P("fsdp", None),
        P("fsdp"),
        P("fsdp"),
        P("fsdp", "seq", None),
    )
    out_specs = (
        P("fsdp", "seq", None),
        P("fsdp", "seq", None),
        P("fsdp", None),
        P("fsdp", None),
        P("fsdp", None),
        P("fsdp", None),
        P("fsdp"),
        P("fsdp"),
        P(),
    )
    return jax.shard_map(on_device, mesh=mesh, in_specs=in_specs, out_specs=out_specs, check_vma=False)
```

time: 956 us -> 575 us (0.60)
  waiting for transfers between devices: 594 us -> 114 us
  starting transfers between devices: 12.1 us -> 141 us
  blocking collectives: 116 us -> 0 us
  local copies, waits for them, and re-layouts: 60.1 us -> 153 us
  matrix products: 117 us -> 62.1 us
  Pallas kernels: 0 us -> 50.5 us
  between operations: 16 us -> 3.55 us
  other arithmetic: 34.9 us -> 45 us
    reduce_scatter x4 -> x0, waiting for transfers between devices: 372 us -> none  [the longest x1 213 us: on_device(): lax.psum_scatter(grad_in_weight, 'fsdp', scatter_dimension=0, tiled=True)]
    ppermute x0 -> x105, starting transfers between devices: none -> 141 us  [the longest x103 139 us: swap(): lax.ppermute(x, axis, [(i, i ^ bit) for i in range(lax.axis_size(axis))])]
    all_gather x4 -> x0, waiting for transfers between devices: 133 us -> none  [the longest x1 52.3 us: on_device(): lax.all_gather(w_qkv, 'fsdp', axis=0, tiled=True)]
    ppermute x0 -> x105, waiting for transfers between devices: none -> 114 us  [the longest x103 114 us: swap(): lax.ppermute(x, axis, [(i, i ^ bit) for i in range(lax.axis_size(axis))])]
    dynamic_update_slice x0 -> x52, local copies, waits for them, and re-layouts: none -> 76.1 us  [the longest x19 47.4 us: stack_seq(): whole = lax.dynamic_update_index_in_dim(whole, part, me ^ k, 0)]
    psum x1 -> x0, waiting for transfers between devices: 60.8 us -> none  [on_device(): lax.psum((attn_sums[0], attn_sums[1], attn_sums[2], mlp_sums[0], mlp_sums...]
    dot_general x26 -> x31, matrix products: 117 us -> 62.1 us  [the longest x4 24.1 us: matmul_tn(): lax.dot_general(a, b, (((0,), (0,)), ((), ())), preferred_element_type=F32)]
    pallas_call x0 -> x3, Pallas kernels: none -> 50.5 us  [the longest x1 23.9 us: attend_backward(): pl.pallas_call(backward_kernel, grid=(length // rows,), in_specs=[tile, t...]
  transfers between devices with their start and end apart: 12 -> 105, of which waited for: 9 -> 28; matrix products, arithmetic and copies ran while one was open for 18% -> 43% of each run, Pallas kernels for 0% -> 9%
where the time goes in v1:
time: 575 us; the launch traced here: 568 us
  local copies, waits for them, and re-layouts  153 us (27%)
  starting transfers between devices  141 us (25%)
  waiting for transfers between devices  114 us (20%)
  matrix products  62.1 us (11%)
  Pallas kernels  50.5 us (9%)
  other arithmetic  45 us (8%)
    ppermute x103, starting transfers between devices, swap(): lax.ppermute(x, axis, [(i, i ^ bit) for i in range(lax.axis_size(axis))])  139 us
    ppermute x103, waiting for transfers between devices, swap(): lax.ppermute(x, axis, [(i, i ^ bit) for i in range(lax.axis_size(axis))])  114 us
    dynamic_update_slice x19, local copies, waits for them, and re-layouts, stack_seq(): whole = lax.dynamic_update_index_in_dim(whole, part, me ^ k, 0)  47.4 us
    dynamic_update_slice x30, local copies, waits for them, and re-layouts, gather_rows(): whole = lax.dynamic_update_index_in_dim(whole, part, me ^ k, 0)  28.7 us
    dot_general x4, matrix products, matmul_tn(): lax.dot_general(a, b, (((0,), (0,)), ((), ())), preferred_element_type=F32)  24.1 us
    pallas_call x1, Pallas kernels, attend_backward(): pl.pallas_call(backward_kernel, grid=(length // rows,), in_specs=[tile, t...  23.9 us
    dot_general x14, matrix products, matmul_nt(): lax.dot_general(a, b, (((1,), (1,)), ((), ())), preferred_element_type=F32)  23.4 us
    pallas_call x1, Pallas kernels, attend_forward(): pl.pallas_call(forward_kernel, grid=(length // rows,), in_specs=[tile, wh...  19.4 us
  transfers between devices with their start and end apart: 105, of which 28 were waited for; matrix products, arithmetic and copies ran while one was open for 43% of the time, Pallas kernels for 9%

profile of v1, /device:TPU:0, one launch (start us, length us, event | category | flops | bytes accessed | tf_op | source)
XLA Modules:
  0.0 568.3 jit_solution(2151012836155274831)
XLA Ops:
  40.3 4.1 collective-permute-start
  78.2 16.1 %collective-permute-done.29 = bf16[2,128,656]{2,1,0:T(8,128)(2,1)S(1)} collective-permute-done((bf16[2,128,656]{2,1,0:T(8,128)(2,1)S(1)}, bf16[2,128,656]{2,1,0:T(8,128)(2,1)S(1)}, u32[]{:S(2)}, u32[]{:S(2)}) %collective-permute-start.29) | collective-permute-done | bytes 335904 | tf_op jit(solution)/shard_map/ppermute | solution.py:22
  95.9 6.5 %collective-permute-done.37 = bf16[328,256]{1,0:T(8,128)(2,1)S(1)} collective-permute-done((bf16[328,256]{1,0:T(8,128)(2,1)}, bf16[328,256]{1,0:T(8,128)(2,1)S(1)}, u32[]{:S(2)}, u32[]{:S(2)}) %collective-permute-start.37) | collective-permute-done | bytes 167968 | tf_op jit(solution)/shard_map/ppermute | solution.py:22
  108.3 8.2 %collective-permute-done.39 = bf16[328,256]{1,0:T(8,128)(2,1)S(1)} collective-permute-done((bf16[328,256]{1,0:T(8,128)(2,1)}, bf16[328,256]{1,0:T(8,128)(2,1)S(1)}, u32[]{:S(2)}, u32[]{:S(2)}) %collective-permute-start.39) | collective-permute-done | bytes 167968 | tf_op jit(solution)/shard_map/ppermute | solution.py:22
  118.0 6.9 %collective-permute-done.41 = bf16[328,256]{1,0:T(8,128)(2,1)S(1)} collective-permute-done((bf16[328,256]{1,0:T(8,128)(2,1)}, bf16[328,256]{1,0:T(8,128)(2,1)S(1)}, u32[]{:S(2)}, u32[]{:S(2)}) %collective-permute-start.41) | collective-permute-done | bytes 167968 | tf_op jit(solution)/shard_map/ppermute | solution.py:22
  136.9 19.7 %collective-permute-done.31 = bf16[2,128,656]{2,1,0:T(8,128)(2,1)S(1)} collective-permute-done((bf16[2,128,656]{2,1,0:T(8,128)(2,1)S(1)}, bf16[2,128,656]{2,1,0:T(8,128)(2,1)S(1)}, u32[]{:S(2)}, u32[]{:S(2)}) %collective-permute-start.31) | collective-permute-done | bytes 335904 | tf_op jit(solution)/shard_map/ppermute | solution.py:22
  168.1 3.5 collective-permute-done.3
  173.5 7.2 %qkv.1 = (bf16[1024,1024]{1,0:T(8,128)(2,1)}, bf16[1024,256]{1,0:T(8,128)(2,1)}, bf16[1024,256]{1,0:T(8,128)(2,1)}, bf16[1024,256]{1,0:T(8,128)(2,1)}) custom-call(bf16[256,1024]{1,0:T(8,128)(2,1)} %bitcast.361, bf16[256,1024]{1,0:T(8,128)(2,1)} %collective-permute-done.refs_1_, bf16[256,1024]{1,0:T(8,128)(2,1)} %collective-permute-done.1.refs_2_, ...), custom_call_target="tpu_custom_call" | custom-call | flops 1610612736 | bytes 7340032 | tf_op jit(solution)/shard_map/qkv/pallas_call | solution.py:188
  180.7 19.4 %attend.1 = (bf16[1024,256]{1,0:T(8,128)(2,1)}, f32[8,1024]{1,0:T(8,128)}) custom-call(bf16[1024,256]{1,0:T(8,128)(2,1)} %get-tuple-element.19.q_ref, bf16[1024,256]{1,0:T(8,128)(2,1)} %get-tuple-element.20.k_ref, bf16[1024,256]{1,0:T(8,128)(2,1)} %get-tuple-element.21.v_ref, s32[1024,1]{1,0:T(8,128)} %copy.64.segc_ref, s32[1024,1]{1,0:T(8,128)} %copy.65.valc_ref, ...), custom_call_target="tpu_custom_call" | custom-call | flops 1073741824 | bytes 2097152 | tf_op jit(solution)/shard_map/attend/pallas_call | solution.py:247
  221.5 5.4 collective-permute-done.45
  248.5 17.8 %fusion = f32[1024,1312]{0,1:T(8,128)} fusion(bf16[1024,1024]{1,0:T(8,128)(2,1)S(1)} %get-tuple-element.113, bf16[256,656]{0,1:T(8,128)(2,1)S(1)} %get-tuple-element.90, bf16[256,656]{0,1:T(8,128)(2,1)S(1)} %get-tuple-element.87, bf16[256,656]{0,1:T(8,128)(2,1)S(1)} %get-tuple-element.81, bf16[256,656]{0,1:T(8,128)(2,1)S(1)} %get-tuple-element.84, ...), kind=kOutput, calls=%fused_computation | convolution fusion | flops 2772959232 | bytes 10158080 | tf_op jit(solution)/shard_map/dot_general | solution.py:363
  267.7 8.3 %reshape.237 = f32[4,2,128,1312]{2,1,0,3:T(2,128)} reshape(f32[1024,1312]{0,1:T(8,128)} %fusion) | data formatting | bytes 10747904 | tf_op jit(solution)/shard_map/reshape | solution.py:121
  276.0 3.6 fusion.17
  285.9 4.2 constant_dynamic-slice_fusion.5
  290.8 3.8 fusion.38
  298.5 8.7 %collective-permute-start.101 = (f32[4,128]{0,1:T(8,128)S(1)}, f32[4,128]{0,1:T(8,128)S(1)}, u32[]{:S(2)}, u32[]{:S(2)}) collective-permute-start(f32[4,128]{0,1:T(8,128)S(1)} %broadcast_add_fusion), channel_id=1, source_target_pairs={{0,2},{1,3},{2,0},{3,1},{4,6},{5,7},{6,4},{7,5},{8,10},{9,11},{10,... | collective-permute-start | bytes 6152 | tf_op jit(solution)/shard_map/ppermute | solution.py:22
  312.4 3.2 collective-permute-done.102
  331.2 23.9 %attend_back.1 = bf16[1024,768]{1,0:T(8,128)(2,1)} custom-call(bf16[1024,256]{1,0:T(8,128)(2,1)} %get-tuple-element.19.q_ref, bf16[1024,256]{1,0:T(8,128)(2,1)} %pad_maximum_fusion.3.go_ref, f32[8,1024]{1,0:T(8,128)} %get-tuple-element.23.lse_ref, bf16[1024,256]{1,0:T(8,128)(2,1)} %get-tuple-element.20.k_ref, bf16[1024,256]{1,0:T(8,128)(2,1)} %get-tuple-element.21.v_ref, ...), custom_call_target="tpu_custom_call" | custom-call | flops 2684354560 | bytes 5242880 | tf_op jit(solution)/shard_map/attend_back/pallas_call | solution.py:314
  355.1 5.9 %fusion.86 = (bf16[1024,1024]{1,0:T(8,128)(2,1)S(1)}, f32[1024,1024]{1,0:T(8,128)}) fusion(bf16[1024,768]{1,0:T(8,128)(2,1)} %attend_back.1, bf16[1024,768]{1,0:T(8,128)(2,1)} %bitcast.9.refs_4_), kind=kOutput, calls=%fused_computation.278 | convolution fusion | flops 1611661312 | bytes 9437184 | tf_op jit(solution)/shard_map/dot_general | solution.py:359
  378.7 4.8 collective-permute-done.93
  386.1 15.2 %collective-permute-start.96 = (bf16[328,1,256]{2,0,1:T(8,128)(2,1)S(1)}, bf16[328,1,256]{2,0,1:T(8,128)(2,1)S(1)}, u32[]{:S(2)}, u32[]{:S(2)}) collective-permute-start(bf16[328,1,256]{2,0,1:T(8,128)(2,1)S(1)} %bitcast.387), channel_id=1, source_target_pairs={{0,8},{8,0},{16,24},{24,16},{1,9},{9,1},{17,25},{25,17},{2,10},{10... | collective-permute-start | bytes 503816 | tf_op jit(solution)/shard_map/ppermute | solution.py:22
  408.1 5.4 dynamic_update_slice.237
  413.5 5.2 dynamic_update_slice.238
  421.2 5.2 dynamic_update_slice.239
  428.8 3.3 fusion.77
  447.7 9.7 %collective-permute-done.67 = bf16[128,768]{0,1:T(8,128)(2,1)S(1)} collective-permute-done((bf16[128,768]{0,1:T(8,128)(2,1)S(1)}, bf16[128,768]{0,1:T(8,128)(2,1)S(1)}, u32[]{:S(2)}, u32[]{:S(2)}) %collective-permute-start.67) | collective-permute-done | bytes 196640 | tf_op jit(solution)/shard_map/ppermute | solution.py:22
  457.4 19.2 %collective-permute-start.84 = (bf16[128,1312]{0,1:T(8,128)(2,1)}, bf16[128,1312]{0,1:T(8,128)(2,1)}, u32[]{:S(2)}, u32[]{:S(2)}) collective-permute-start(bf16[128,1312]{0,1:T(8,128)(2,1)} %get-tuple-element.76), channel_id=1, source_target_pairs={{0,2},{1,3},{2,0},{3,1},{4,6},{5,7},{6,4},{7,5},{8,10},{9,11},{10,... | collective-permute-start | bytes 1007624 | tf_op jit(solution)/shard_map/ppermute | solution.py:22
  482.8 6.1 %dynamic_update_slice.224 = bf16[4,128,3,256]{3,0,2,1:T(4,128)(2,1)S(1)} dynamic-update-slice(bf16[4,128,3,256]{3,0,2,1:T(4,128)(2,1)S(1)} %broadcast_in_dim.278, bf16[1,128,3,256]{3,0,2,1:T(2,128)(2,1)S(1)} %copy.81, s32[]{:T(128)S(6)} %select_n.221, s32[]{:T(128)} %constant.295.clone.1, s32[]{:T(128)} %constant.295.clone.1, s32[]{:T(128)} %constant.295.clone.1) | dynamic-update-slice | bytes 393220 | tf_op jit(solution)/shard_map/jit(dynamic_update_index_in_dim)/dynamic_update_slice | solution.py:94
  508.6 6.1 %dynamic_update_slice.225 = bf16[4,128,3,256]{3,0,2,1:T(4,128)(2,1)S(1)} dynamic-update-slice(bf16[4,128,3,256]{3,0,2,1:T(4,128)(2,1)S(1)} %dynamic_update_slice.224, bf16[1,128,3,256]{3,0,2,1:T(2,128)(2,1)S(1)} %copy.82, s32[]{:T(128)S(6)} %select_n.222, s32[]{:T(128)} %constant.295.clone.1, s32[]{:T(128)} %constant.295.clone.1, s32[]{:T(128)} %constant.295.clone.1) | dynamic-update-slice | bytes 393220 | tf_op jit(solution)/shard_map/jit(dynamic_update_index_in_dim)/dynamic_update_slice | solution.py:94
  514.7 7.8 %dynamic_update_slice.226 = bf16[4,128,3,256]{3,0,2,1:T(4,128)(2,1)S(1)} dynamic-update-slice(bf16[4,128,3,256]{3,0,2,1:T(4,128)(2,1)S(1)} %dynamic_update_slice.225, bf16[1,128,3,256]{3,0,2,1:T(2,128)(2,1)} %copy.83, s32[]{:T(128)S(6)} %select_n.223, s32[]{:T(128)} %constant.295.clone.1, s32[]{:T(128)} %constant.295.clone.1, s32[]{:T(128)} %constant.295.clone.1) | dynamic-update-slice | bytes 393220 | tf_op jit(solution)/shard_map/jit(dynamic_update_index_in_dim)/dynamic_update_slice | solution.py:94
  530.9 6.1 %dynamic_update_slice.227 = bf16[4,128,3,256]{3,0,2,1:T(4,128)(2,1)S(1)} dynamic-update-slice(bf16[4,128,3,256]{3,0,2,1:T(4,128)(2,1)S(1)} %dynamic_update_slice.226, bf16[1,128,3,256]{3,0,2,1:T(2,128)(2,1)S(1)} %copy.85, s32[]{:T(128)S(6)} %select_n.224, s32[]{:T(128)} %constant.295.clone.1, s32[]{:T(128)} %constant.295.clone.1, s32[]{:T(128)} %constant.295.clone.1) | dynamic-update-slice | bytes 393220 | tf_op jit(solution)/shard_map/jit(dynamic_update_index_in_dim)/dynamic_update_slice | solution.py:94
  563.4 3.4 copy.99
  (560 shorter events, 290.7 us)
Async XLA Ops:
  2.2 38.1 %collective-permute-start.17 = (bf16[128,256]{1,0:T(8,128)(2,1)}, bf16[128,256]{1,0:T(8,128)(2,1)}, u32[]{:S(2)}, u32[]{:S(2)}) collective-permute-start(bf16[128,256]{1,0:T(8,128)(2,1)} %constant_dynamic-slice_fusion.15), channel_id=1, source_target_pairs={{0,1},{1,0},{2,3},{3,2},{4,5},{5,4},{6,7},{7,6},{8,9},{9,8},{10,11... | collective-permute-start | bytes 196616 | tf_op jit(solution)/shard_map/ppermute | solution.py:22
  2.7 36.3 %collective-permute-start.18 = (bf16[128,256]{1,0:T(8,128)(2,1)}, bf16[128,256]{1,0:T(8,128)(2,1)}, u32[]{:S(2)}, u32[]{:S(2)}) collective-permute-start(bf16[128,256]{1,0:T(8,128)(2,1)} %constant_dynamic-slice_fusion.15), channel_id=1, source_target_pairs={{0,2},{1,3},{2,0},{3,1},{4,6},{5,7},{6,4},{7,5},{8,10},{9,11},{10,... | collective-permute-start | bytes 196616 | tf_op jit(solution)/shard_map/ppermute | solution.py:22
  5.3 33.8 %collective-permute-start.20 = (bf16[128,256]{1,0:T(8,128)(2,1)}, bf16[128,256]{1,0:T(8,128)(2,1)}, u32[]{:S(2)}, u32[]{:S(2)}) collective-permute-start(bf16[128,256]{1,0:T(8,128)(2,1)} %constant_dynamic-slice_fusion.15), channel_id=1, source_target_pairs={{0,4},{1,5},{2,6},{3,7},{4,0},{5,1},{6,2},{7,3},{8,12},{9,13},{10,... | collective-permute-start | bytes 196616 | tf_op jit(solution)/shard_map/ppermute | solution.py:22
  7.9 31.7 %collective-permute-start.22 = (bf16[128,256]{1,0:T(8,128)(2,1)}, bf16[128,256]{1,0:T(8,128)(2,1)}, u32[]{:S(2)}, u32[]{:S(2)}) collective-permute-start(bf16[128,256]{1,0:T(8,128)(2,1)} %constant_dynamic-slice_fusion.15), channel_id=1, source_target_pairs={{0,6},{1,7},{2,4},{3,5},{4,2},{5,3},{6,0},{7,1},{8,14},{9,15},{10,... | collective-permute-start | bytes 196616 | tf_op jit(solution)/shard_map/ppermute | solution.py:22
  37.5 33.4 %collective-permute-start.35 = (bf16[328,256]{1,0:T(8,128)(2,1)S(1)}, bf16[328,256]{1,0:T(8,128)(2,1)}, u32[]{:S(2)}, u32[]{:S(2)}) collective-permute-start(bf16[328,256]{1,0:T(8,128)(2,1)S(1)} %copy-done.43), channel_id=1, source_target_pairs={{0,0},{1,1},{2,8},{3,9},{4,16},{5,17},{6,24},{7,25},{8,2},{9,3},{1... | collective-permute-start | bytes 503816 | tf_op jit(solution)/shard_map/ppermute | solution.py:86
  40.3 89.7 %collective-permute-start = (bf16[256,1024]{1,0:T(8,128)(2,1)S(1)}, bf16[256,1024]{1,0:T(8,128)(2,1)}, u32[]{:S(2)}, u32[]{:S(2)}) collective-permute-start(bf16[256,1024]{1,0:T(8,128)(2,1)S(1)} %bitcast.362), channel_id=1, source_target_pairs={{0,8},{8,0},{16,24},{24,16},{1,9},{9,1},{17,25},{25,17},{2,10},{10... | collective-permute-start | bytes 1572872 | tf_op jit(solution)/shard_map/ppermute | solution.py:22
  53.9 80.1 %collective-permute-start.1 = (bf16[256,1024]{1,0:T(8,128)(2,1)S(1)}, bf16[256,1024]{1,0:T(8,128)(2,1)}, u32[]{:S(2)}, u32[]{:S(2)}) collective-permute-start(bf16[256,1024]{1,0:T(8,128)(2,1)S(1)} %bitcast.363), channel_id=1, source_target_pairs={{0,16},{8,24},{16,0},{24,8},{1,17},{9,25},{17,1},{25,9},{2,18},{10... | collective-permute-start | bytes 1572872 | tf_op jit(solution)/shard_map/ppermute | solution.py:22
  70.9 31.5 %collective-permute-start.7 = (bf16[128,768]{1,0:T(8,128)(2,1)S(1)}, bf16[128,768]{1,0:T(8,128)(2,1)S(1)}, u32[]{:S(2)}, u32[]{:S(2)}) collective-permute-start(bf16[128,768]{1,0:T(8,128)(2,1)S(1)} %copy-done.42), channel_id=1, source_target_pairs={{0,4},{1,5},{2,6},{3,7},{4,0},{5,1},{6,2},{7,3},{8,12},{9,13},{10,... | collective-permute-start | bytes 589832 | tf_op jit(solution)/shard_map/ppermute | solution.py:22
  76.5 29.2 %collective-permute-start.9 = (bf16[128,768]{1,0:T(8,128)(2,1)S(1)}, bf16[128,768]{1,0:T(8,128)(2,1)S(1)}, u32[]{:S(2)}, u32[]{:S(2)}) collective-permute-start(bf16[128,768]{1,0:T(8,128)(2,1)S(1)} %copy-done.42), channel_id=1, source_target_pairs={{0,6},{1,7},{2,4},{3,5},{4,2},{5,3},{6,0},{7,1},{8,14},{9,15},{10,... | collective-permute-start | bytes 589832 | tf_op jit(solution)/shard_map/ppermute | solution.py:22
  102.4 33.6 %collective-permute-start.50 = (bf16[256,1024]{1,0:T(8,128)(2,1)S(1)}, bf16[256,1024]{1,0:T(8,128)(2,1)S(1)}, u32[]{:S(2)}, u32[]{:S(2)}) collective-permute-start(bf16[256,1024]{1,0:T(8,128)(2,1)S(1)} %bitcast.369), channel_id=1, source_target_pairs={{0,8},{8,0},{16,24},{24,16},{1,9},{9,1},{17,25},{25,17},{2,10},{10... | collective-permute-start | bytes 1572872 | tf_op jit(solution)/shard_map/ppermute | solution.py:22
  124.8 32.3 %collective-permute-start.52 = (bf16[256,1024]{1,0:T(8,128)(2,1)S(1)}, bf16[256,1024]{1,0:T(8,128)(2,1)S(1)}, u32[]{:S(2)}, u32[]{:S(2)}) collective-permute-start(bf16[256,1024]{1,0:T(8,128)(2,1)S(1)} %bitcast.370), channel_id=1, source_target_pairs={{0,16},{8,24},{16,0},{24,8},{1,17},{9,25},{17,1},{25,9},{2,18},{10... | collective-permute-start | bytes 1572872 | tf_op jit(solution)/shard_map/ppermute | solution.py:22
  134.0 28.5 %collective-permute-start.24 = (bf16[1024,256]{0,1:T(8,128)(2,1)S(1)}, bf16[1024,256]{0,1:T(8,128)(2,1)S(1)}, u32[]{:S(2)}, u32[]{:S(2)}) collective-permute-start(bf16[1024,256]{0,1:T(8,128)(2,1)S(1)} %bitcast.381), channel_id=1, source_target_pairs={{0,8},{8,0},{16,24},{24,16},{1,9},{9,1},{17,25},{25,17},{2,10},{10... | collective-permute-start | bytes 1572872 | tf_op jit(solution)/shard_map/ppermute | solution.py:22
  164.4 38.0 %collective-permute-start.55 = (bf16[128,1024]{1,0:T(8,128)(2,1)}, bf16[128,1024]{1,0:T(8,128)(2,1)}, u32[]{:S(2)}, u32[]{:S(2)}) collective-permute-start(bf16[128,1024]{1,0:T(8,128)(2,1)} %slice.177), channel_id=1, source_target_pairs={{0,16},{8,24},{16,0},{24,8},{1,17},{9,25},{17,1},{25,9},{2,18},{10... | collective-permute-start | bytes 786440 | tf_op jit(solution)/shard_map/ppermute | solution.py:22
  166.6 37.1 %collective-permute-start.54 = (bf16[128,1024]{1,0:T(8,128)(2,1)}, bf16[128,1024]{1,0:T(8,128)(2,1)}, u32[]{:S(2)}, u32[]{:S(2)}) collective-permute-start(bf16[128,1024]{1,0:T(8,128)(2,1)} %slice.176), channel_id=1, source_target_pairs={{0,8},{8,0},{16,24},{24,16},{1,9},{9,1},{17,25},{25,17},{2,10},{10... | collective-permute-start | bytes 786440 | tf_op jit(solution)/shard_map/ppermute | solution.py:22
  167.7 42.5 %collective-permute-start.27 = (bf16[512,256]{0,1:T(8,128)(2,1)S(1)}, bf16[512,256]{0,1:T(8,128)(2,1)}, u32[]{:S(2)}, u32[]{:S(2)}) collective-permute-start(bf16[512,256]{0,1:T(8,128)(2,1)S(1)} %slice.170), channel_id=1, source_target_pairs={{0,16},{8,24},{16,0},{24,8},{1,17},{9,25},{17,1},{25,9},{2,18},{10... | collective-permute-start | bytes 786440 | tf_op jit(solution)/shard_map/ppermute | solution.py:22
  171.6 38.7 %collective-permute-start.26 = (bf16[512,256]{0,1:T(8,128)(2,1)}, bf16[512,256]{0,1:T(8,128)(2,1)}, u32[]{:S(2)}, u32[]{:S(2)}) collective-permute-start(bf16[512,256]{0,1:T(8,128)(2,1)} %slice.169), channel_id=1, source_target_pairs={{0,8},{8,0},{16,24},{24,16},{1,9},{9,1},{17,25},{25,17},{2,10},{10... | collective-permute-start | bytes 786440 | tf_op jit(solution)/shard_map/ppermute | solution.py:22
  232.8 46.8 %collective-permute-start.53 = (bf16[256,1024]{1,0:T(8,128)(2,1)}, bf16[256,1024]{1,0:T(8,128)(2,1)}, u32[]{:S(2)}, u32[]{:S(2)}) collective-permute-start(bf16[256,1024]{1,0:T(8,128)(2,1)} %fusion.26), channel_id=1, source_target_pairs={{0,16},{8,24},{16,0},{24,8},{1,17},{9,25},{17,1},{25,9},{2,18},{10... | collective-permute-start | bytes 1572872 | tf_op jit(solution)/shard_map/ppermute | solution.py:22
  237.6 52.5 %collective-permute-start.51 = (bf16[256,1024]{1,0:T(8,128)(2,1)}, bf16[256,1024]{1,0:T(8,128)(2,1)}, u32[]{:S(2)}, u32[]{:S(2)}) collective-permute-start(bf16[256,1024]{1,0:T(8,128)(2,1)} %fusion.25), channel_id=1, source_target_pairs={{0,8},{8,0},{16,24},{24,16},{1,9},{9,1},{17,25},{25,17},{2,10},{10... | collective-permute-start | bytes 1572872 | tf_op jit(solution)/shard_map/ppermute | solution.py:22
  240.1 50.1 %collective-permute-start.46 = (bf16[256,1024]{1,0:T(8,128)(2,1)}, bf16[256,1024]{1,0:T(8,128)(2,1)}, u32[]{:S(2)}, u32[]{:S(2)}) collective-permute-start(bf16[256,1024]{1,0:T(8,128)(2,1)} %convolution_convert_fusion.2), channel_id=1, source_target_pairs={{0,16},{8,24},{16,0},{24,8},{1,17},{9,25},{17,1},{25,9},{2,18},{10... | collective-permute-start | bytes 1572872 | tf_op jit(solution)/shard_map/ppermute | solution.py:22
  242.6 48.1 %collective-permute-start.44 = (bf16[256,1024]{1,0:T(8,128)(2,1)}, bf16[256,1024]{1,0:T(8,128)(2,1)}, u32[]{:S(2)}, u32[]{:S(2)}) collective-permute-start(bf16[256,1024]{1,0:T(8,128)(2,1)} %convolution_convert_fusion.3), channel_id=1, source_target_pairs={{0,8},{8,0},{16,24},{24,16},{1,9},{9,1},{17,25},{25,17},{2,10},{10... | collective-permute-start | bytes 1572872 | tf_op jit(solution)/shard_map/ppermute | solution.py:22
  246.9 43.8 %collective-permute-start.56 = (bf16[256,1024]{1,0:T(8,128)(2,1)S(1)}, bf16[256,1024]{1,0:T(8,128)(2,1)S(1)}, u32[]{:S(2)}, u32[]{:S(2)}) collective-permute-start(bf16[256,1024]{1,0:T(8,128)(2,1)S(1)} %fusion.27), channel_id=1, source_target_pairs={{0,24},{8,16},{16,8},{24,0},{1,25},{9,17},{17,9},{25,1},{2,26},{10... | collective-permute-start | bytes 1572872 | tf_op jit(solution)/shard_map/ppermute | solution.py:22
  290.1 137.8 %collective-permute-start.83 = (bf16[4,128,1312]{1,2,0:T(8,128)(2,1)}, bf16[4,128,1312]{1,2,0:T(8,128)(2,1)}, u32[]{:S(2)}, u32[]{:S(2)}) collective-permute-start(bf16[4,128,1312]{1,2,0:T(8,128)(2,1)} %bitcast.324), channel_id=1, source_target_pairs={{0,1},{1,0},{2,3},{3,2},{4,5},{5,4},{6,7},{7,6},{8,9},{9,8},{10,11... | collective-permute-start | bytes 4030472 | tf_op jit(solution)/shard_map/ppermute | solution.py:22
  290.2 72.5 %collective-permute-start.91 = (bf16[1,328,1024]{2,1,0:T(8,128)(2,1)}, bf16[1,328,1024]{2,1,0:T(8,128)(2,1)}, u32[]{:S(2)}, u32[]{:S(2)}) collective-permute-start(bf16[1,328,1024]{2,1,0:T(8,128)(2,1)} %fusion.45), channel_id=1, source_target_pairs={{0,1},{1,0},{2,3},{3,2},{4,5},{5,4},{6,7},{7,6},{8,9},{9,8},{10,11... | collective-permute-start | bytes 2015240 | tf_op jit(solution)/shard_map/ppermute | solution.py:22
  383.5 62.6 %collective-permute-start.72 = (bf16[4,128,1024]{2,1,0:T(8,128)(2,1)}, bf16[4,128,1024]{2,1,0:T(8,128)(2,1)}, u32[]{:S(2)}, u32[]{:S(2)}) collective-permute-start(bf16[4,128,1024]{2,1,0:T(8,128)(2,1)} %fusion.41), channel_id=1, source_target_pairs={{0,1},{1,0},{2,3},{3,2},{4,5},{5,4},{6,7},{7,6},{8,9},{9,8},{10,11... | collective-permute-start | bytes 3145736 | tf_op jit(solution)/shard_map/ppermute | solution.py:22
  383.5 51.3 %collective-permute-start.64 = (bf16[4,128,768]{2,1,0:T(8,128)(2,1)}, bf16[4,128,768]{2,1,0:T(8,128)(2,1)}, u32[]{:S(2)}, u32[]{:S(2)}) collective-permute-start(bf16[4,128,768]{2,1,0:T(8,128)(2,1)} %fusion.44), channel_id=1, source_target_pairs={{0,1},{1,0},{2,3},{3,2},{4,5},{5,4},{6,7},{7,6},{8,9},{9,8},{10,11... | collective-permute-start | bytes 2359304 | tf_op jit(solution)/shard_map/ppermute | solution.py:22
  433.2 55.7 %collective-permute-start.86 = (bf16[128,1312]{0,1:T(8,128)(2,1)}, bf16[128,1312]{0,1:T(8,128)(2,1)}, u32[]{:S(2)}, u32[]{:S(2)}) collective-permute-start(bf16[128,1312]{0,1:T(8,128)(2,1)} %get-tuple-element.77), channel_id=1, source_target_pairs={{0,6},{1,7},{2,4},{3,5},{4,2},{5,3},{6,0},{7,1},{8,14},{9,15},{10,... | collective-permute-start | bytes 1007624 | tf_op jit(solution)/shard_map/ppermute | solution.py:22
  434.7 55.7 %collective-permute-start.85 = (bf16[128,1312]{0,1:T(8,128)(2,1)}, bf16[128,1312]{0,1:T(8,128)(2,1)}, u32[]{:S(2)}, u32[]{:S(2)}) collective-permute-start(bf16[128,1312]{0,1:T(8,128)(2,1)} %get-tuple-element.78), channel_id=1, source_target_pairs={{0,4},{1,5},{2,6},{3,7},{4,0},{5,1},{6,2},{7,3},{8,12},{9,13},{10,... | collective-permute-start | bytes 1007624 | tf_op jit(solution)/shard_map/ppermute | solution.py:22
  440.5 37.7 %collective-permute-start.66 = (bf16[128,768]{0,1:T(8,128)(2,1)}, bf16[128,768]{0,1:T(8,128)(2,1)S(1)}, u32[]{:S(2)}, u32[]{:S(2)}) collective-permute-start(bf16[128,768]{0,1:T(8,128)(2,1)} %bitcast.73), channel_id=1, source_target_pairs={{0,4},{1,5},{2,6},{3,7},{4,0},{5,1},{6,2},{7,3},{8,12},{9,13},{10,... | collective-permute-start | bytes 589832 | tf_op jit(solution)/shard_map/ppermute | solution.py:22
  446.1 33.5 %collective-permute-start.65 = (bf16[128,768]{0,1:T(8,128)(2,1)}, bf16[128,768]{0,1:T(8,128)(2,1)S(1)}, u32[]{:S(2)}, u32[]{:S(2)}) collective-permute-start(bf16[128,768]{0,1:T(8,128)(2,1)} %bitcast.72), channel_id=1, source_target_pairs={{0,2},{1,3},{2,0},{3,1},{4,6},{5,7},{6,4},{7,5},{8,10},{9,11},{10,... | collective-permute-start | bytes 589832 | tf_op jit(solution)/shard_map/ppermute | solution.py:22
  457.4 33.6 %collective-permute-start.84 = (bf16[128,1312]{0,1:T(8,128)(2,1)}, bf16[128,1312]{0,1:T(8,128)(2,1)}, u32[]{:S(2)}, u32[]{:S(2)}) collective-permute-start(bf16[128,1312]{0,1:T(8,128)(2,1)} %get-tuple-element.76), channel_id=1, source_target_pairs={{0,2},{1,3},{2,0},{3,1},{4,6},{5,7},{6,4},{7,5},{8,10},{9,11},{10,... | collective-permute-start | bytes 1007624 | tf_op jit(solution)/shard_map/ppermute | solution.py:22
  502.8 48.6 %collective-permute-start.87 = (bf16[128,2,656]{0,2,1:T(8,128)(2,1)}, bf16[128,2,656]{0,2,1:T(8,128)(2,1)}, u32[]{:S(2)}, u32[]{:S(2)}) collective-permute-start(bf16[128,2,656]{0,2,1:T(8,128)(2,1)} %bitcast.104), channel_id=1, source_target_pairs={{0,8},{8,0},{16,24},{24,16},{1,9},{9,1},{17,25},{25,17},{2,10},{10... | collective-permute-start | bytes 1007624 | tf_op jit(solution)/shard_map/ppermute | solution.py:22
  506.1 48.0 %collective-permute-start.88 = (bf16[128,2,656]{0,2,1:T(8,128)(2,1)}, bf16[128,2,656]{0,2,1:T(8,128)(2,1)}, u32[]{:S(2)}, u32[]{:S(2)}) collective-permute-start(bf16[128,2,656]{0,2,1:T(8,128)(2,1)} %bitcast.104), channel_id=1, source_target_pairs={{0,16},{8,24},{16,0},{24,8},{1,17},{9,25},{17,1},{25,9},{2,18},{10... | collective-permute-start | bytes 1007624 | tf_op jit(solution)/shard_map/ppermute | solution.py:22
  (135 other events, 1229.3 us)

commit v2 on v1

--- a/solution.py
+++ b/solution.py
@@ -14,6 +14,7 @@
 
 ROPE_BASE = 160000.0
 NORM_EPS = 1e-05
+LANES = 128
 BF = jnp.bfloat16
 F32 = jnp.float32
 
@@ -22,16 +23,12 @@
     return lax.ppermute(x, axis, [(i, i ^ bit) for i in range(lax.axis_size(axis))])
 
 
+def after(x, *others):
+    return lax.optimization_barrier((x, others))[0]
+
+
 def share_seq(block):
-    size = lax.axis_size("seq")
-    if size != 4:
-        return [block] + [swap(block, "seq", k) for k in range(1, size)]
-    half = block.shape[0] // 2
-    one = swap(block, "seq", 1)
-    two = swap(block, "seq", 2)
-    upper = swap(two[:half], "seq", 1)
-    lower = swap(one[half:], "seq", 2)
-    return [block, one, two, jnp.concatenate([upper, lower], axis=0)]
+    return [block] + [swap(block, "seq", k) for k in range(1, lax.axis_size("seq"))]
 
 
 def reduce_seq(blocks):
@@ -41,38 +38,12 @@
     return total
 
 
-def reduce_seq_relay(blocks):
-    if len(blocks) != 4:
-        return reduce_seq(blocks)
-    own, one, two, three = blocks
-    half = own.shape[0] // 2
-    upper = swap(three[:half].astype(BF), "seq", 1).astype(F32)
-    lower = swap(three[half:].astype(BF), "seq", 2).astype(F32)
-    to_two = jnp.concatenate([two[:half] + upper, two[half:]], axis=0).astype(BF)
-    to_one = jnp.concatenate([one[:half], one[half:] + lower], axis=0).astype(BF)
-    return own + swap(to_two, "seq", 2).astype(F32) + swap(to_one, "seq", 1).astype(F32)
-
-
 def paired():
     return lax.axis_size("fsdp") == 2 * lax.axis_size("seq")
 
 
-def spread_rows(block):
-    size = lax.axis_size("fsdp")
-    same = [block] + [swap(block, "fsdp", k) for k in range(2, size, 2)]
-    other = [swap(b, "fsdp", 1) for b in same]
-    return [b for pair in zip(same, other) for b in pair]
-
-
 def gather_rows(block):
-    if not paired():
-        return lax.all_gather(block, "fsdp", axis=0)
-    me = lax.axis_index("fsdp")
-    parts = spread_rows(block)
-    whole = jnp.zeros((len(parts),) + block.shape, block.dtype)
-    for k, part in enumerate(parts):
-        whole = lax.dynamic_update_index_in_dim(whole, part, me ^ k, 0)
-    return whole
+    return lax.all_gather(block, "fsdp", axis=0, tiled=True)
 
 
 def transpose_devices(x):
@@ -86,39 +57,14 @@
     return lax.ppermute(x, ("seq", "fsdp"), pairs)
 
 
-def stack_seq(block):
-    me = lax.axis_index("seq")
-    parts = share_seq(block)
-    whole = jnp.zeros((len(parts),) + block.shape, block.dtype)
-    for k, part in enumerate(parts):
-        whole = lax.dynamic_update_index_in_dim(whole, part, me ^ k, 0)
-    return whole
-
-
-def reduce_z(blocks):
-    count = blocks.shape[0]
-    z = lax.axis_index("fsdp") // 2
-    low = blocks.astype(BF)
-    total = lax.dynamic_index_in_dim(blocks, z, 0, keepdims=False)
-    for k in range(1, count):
-        part = lax.dynamic_index_in_dim(low, z ^ k, 0, keepdims=False)
+def reduce_rows(mine, away, size):
+    mine = mine + swap(away, "fsdp", 1).astype(F32)
+    rows = mine.shape[0] // (size // 2)
+    total = mine[:rows]
+    for k in range(1, size // 2):
+        part = mine[k * rows : (k + 1) * rows].astype(BF)
         total = total + swap(part, "fsdp", 2 * k).astype(F32)
     return total
-
-
-def reduce_core(pairs):
-    core = lax.axis_index("fsdp") % 2
-    away = lax.dynamic_index_in_dim(pairs, 1 - core, 1, keepdims=False)
-    mine = lax.dynamic_index_in_dim(pairs, core, 1, keepdims=False)
-    return mine + swap(away.astype(BF), "fsdp", 1).astype(F32)
-
-
-def reduce_rows(partial):
-    size = lax.axis_size("fsdp")
-    if not paired():
-        return lax.psum_scatter(partial, "fsdp", scatter_dimension=0, tiled=True)
-    rows = partial.shape[0] // size
-    return reduce_z(reduce_core(partial.reshape(size // 2, 2, rows, partial.shape[1])))
 
 
 def sum_everywhere(values):
@@ -331,6 +277,133 @@
     )(q, grad_out, lse, k, v, seg_col, valid_col, seg_row, cosine, sine)
 
 
+def erf(x):
+    x = jnp.clip(x, -3.832506856900711, 3.832506856900711)
+    square = x * x
+    top = 0.00022905065861350646
+    for c in (0.0034082910107109506, 0.050955695062380861, 0.18520832239976145, 1.128379143519084):
+        top = top * square + c
+    low = -1.1791602954361697e-7
+    for c in (0.000023547966471313185, 0.0010179625278914885, 0.014070470171167667, 0.11098505178285362, 0.49746925110067538, 1.0):
+        low = low * square + c
+    return x * top / low
+
+
+def nt(a, b):
+    return lax.dot_general(a, b, (((1,), (1,)), ((), ())), preferred_element_type=F32)
+
+
+def feed_kernel(b_ref, g_ref, w_ref, wd_ref, m_ref, gi_ref, gg_ref, gb_ref, mlp_ref):
+    b = b_ref[...]
+    hidden, slot = wd_ref.shape[0], w_ref.shape[1] // 2
+    wi_ref, wg_ref = w_ref.at[:, :hidden], w_ref.at[:, slot : slot + hidden]
+    inner = jnp.dot(b, wi_ref[...], preferred_element_type=F32)
+    gate = jnp.dot(b, wg_ref[...], preferred_element_type=F32)
+    upstream = nt(g_ref[...], wd_ref[...])
+    half = 0.5 * (1.0 + erf(inner * 0.7071067811865476))
+    gelu = inner * half
+    slope = half + inner * jnp.exp(-0.5 * inner * inner) * 0.3989422804014327
+    m = (gelu * gate).astype(BF)
+    gi = (upstream * gate * slope).astype(BF)
+    gg = (upstream * gelu).astype(BF)
+    m_ref[...] = m
+    gi_ref[...] = gi
+    gg_ref[...] = gg
+    gb_ref[...] = (nt(gi, wi_ref[...]) + nt(gg, wg_ref[...])).astype(gb_ref.dtype)
+    mlp_ref[...] = jnp.dot(m, wd_ref[...], preferred_element_type=F32).astype(mlp_ref.dtype)
+
+
+def feed_forward(b, g, w, wd, dtype):
+    rows, width = b.shape
+    hidden = wd.shape[0]
+    narrow = jax.ShapeDtypeStruct((rows, hidden), BF)
+    full = jax.ShapeDtypeStruct((rows, width), dtype)
+    return pl.pallas_call(
+        feed_kernel,
+        out_shape=[narrow, narrow, narrow, full, full],
+        cost_estimate=pl.CostEstimate(
+            flops=12 * rows * width * hidden,
+            bytes_accessed=6 * width * hidden + 8 * rows * width + 6 * rows * hidden,
+            transcendentals=rows * hidden,
+        ),
+        name="feed",
+    )(b, g, w, wd)
+
+
+def tn(a, b):
+    return lax.dot_general(a, b, (((0,), (0,)), ((), ())), preferred_element_type=F32)
+
+
+def weight_kernel(count, slot, *refs):
+    bs, gs, gis, ggs, ms = (refs[i * count : (i + 1) * count] for i in range(5))
+    out_ref = refs[5 * count]
+    hidden = gis[0].shape[1]
+    for place, (lefts, rights) in enumerate(((bs, gis), (bs, ggs), (gs, ms))):
+        total = tn(lefts[0][...], rights[0][...])
+        for left, right in zip(lefts[1:], rights[1:]):
+            total = total + tn(left[...], right[...])
+        out_ref[:, place * slot : place * slot + hidden] = total.astype(BF)
+
+
+def weight_gradients(bs, gs, gis, ggs, ms):
+    count = len(bs)
+    rows, width = bs[0].shape
+    hidden = gis[0].shape[1]
+    slot = -(-hidden // LANES) * LANES
+    wide_spec = pl.BlockSpec((rows, 256), lambda i: (0, i))
+    whole = pl.BlockSpec((rows, hidden), lambda i: (0, 0))
+    return pl.pallas_call(
+        functools.partial(weight_kernel, count, slot),
+        grid=(width // 256,),
+        in_specs=[wide_spec] * (2 * count) + [whole] * (3 * count),
+        out_specs=pl.BlockSpec((256, 3 * slot), lambda i: (i, 0)),
+        out_shape=jax.ShapeDtypeStruct((width, 3 * slot), BF),
+        cost_estimate=pl.CostEstimate(
+            flops=6 * rows * count * width * hidden,
+            bytes_accessed=4 * rows * count * width + 6 * rows * count * hidden + 6 * width * hidden,
+            transcendentals=0,
+        ),
+        name="weight_gradients",
+    )(*bs, *gs, *gis, *ggs, *ms)
+
+
+def last_kernel(me_ref, a_ref, gp_ref, mine_ref, away_ref):
+    total = tn(a_ref[...], gp_ref[...])
+
+    @pl.when(pl.program_id(0) % 2 == 0)
+    def _():
+        mine_ref[...] = total
+
+    @pl.when(pl.program_id(0) % 2 == 1)
+    def _():
+        away_ref[...] = total.astype(BF)
+
+
+def last_gradients(a, gp, me, size):
+    length, width = a.shape
+    rows, columns = width // size, gp.shape[1]
+    out = lambda dtype: jax.ShapeDtypeStruct((width // 2, columns), dtype)
+    return pl.pallas_call(
+        last_kernel,
+        grid_spec=pltpu.PrefetchScalarGridSpec(
+            num_scalar_prefetch=1,
+            grid=(size,),
+            in_specs=[
+                pl.BlockSpec((length, rows), lambda i, me: (0, me[0] ^ i)),
+                pl.BlockSpec((length, columns), lambda i, me: (0, 0)),
+            ],
+            out_specs=[pl.BlockSpec((rows, columns), lambda i, me: (i // 2, 0))] * 2,
+        ),
+        out_shape=[out(F32), out(BF)],
+        cost_estimate=pl.CostEstimate(
+            flops=2 * length * width * columns,
+            bytes_accessed=2 * length * (width + columns) + 3 * width * columns,
+            transcendentals=0,
+        ),
+        name="last_gradients",
+    )(me[None], a, gp)
+
+
 def normal(values):
     centered = values - jnp.mean(values, axis=-1, keepdims=True)
     scale = lax.rsqrt(jnp.mean(centered * centered, axis=-1, keepdims=True) + NORM_EPS)
@@ -345,10 +418,6 @@
         - jnp.mean(weighted, axis=-1, keepdims=True)
         - unit * jnp.mean(weighted * unit, axis=-1, keepdims=True)
     )
-
-
-def gelu_gate(inputs, gates):
-    return 0.5 * inputs * (1.0 + lax.erf(inputs * 0.7071067811865476)) * gates
 
 
 def matmul(a, b):
@@ -375,29 +444,42 @@
     hidden = FF // seq_size
     rel = [seq ^ k for k in range(seq_size)]
 
+    first_mine = [lax.dynamic_slice_in_dim(w_qkv, i * D + seq * part, part, axis=1) for i in range(3)]
+    first_mine.append(lax.dynamic_slice_in_dim(w_attn_out, seq * part, part, axis=1))
+    first_mine = jnp.concatenate(first_mine, axis=1)
+    first_weight = gather_rows(first_mine)
     x_blocks = share_seq(x_low)
     gains = gather_gains(jnp.stack([attn_gain, mlp_gain])).astype(F32)
     gain_one, gain_two = gains[0:1], gains[1:2]
-    qkv_mine = jnp.concatenate(
-        [lax.dynamic_slice_in_dim(w_qkv, i * D + seq * part, part, axis=1) for i in range(3)], axis=1
-    )
-    qkv_weight = gather_rows(qkv_mine).reshape(D, 3 * part)
-    cot_blocks = share_seq(cot)
-    in_mine = jnp.stack(
-        [lax.dynamic_slice_in_dim(w_in_proj, i * FF + seq * hidden, hidden, axis=1) for i in range(2)]
-    )
-    in_weight = jnp.swapaxes(gather_rows(in_mine), 0, 1).reshape(2, D, hidden)
+    qkv_weight, out_mine = first_weight[:, : 3 * part], first_weight[:, 3 * part :]
+    w_in_proj_late, w_out_proj_late, cot_late = after((w_in_proj, w_out_proj, cot), gains, *x_blocks)
+    slot = -(-hidden // LANES) * LANES
+    in_mine = [
+        jnp.pad(
+            lax.dynamic_slice_in_dim(w_in_proj_late, i * FF + seq * hidden, hidden, axis=1),
+            ((0, 0), (0, slot - hidden)),
+        )
+        for i in range(2)
+    ]
+    in_weight = gather_rows(jnp.concatenate(in_mine, axis=1))
     if paired():
-        down_mine = transpose_devices(lax.dynamic_slice_in_dim(w_out_proj, seq * part, part, axis=1))
+        down_mine = transpose_devices(lax.dynamic_slice_in_dim(w_out_proj_late, seq * part, part, axis=1))
         down_weight = gather_rows(down_mine).reshape(seq_size, 2, down_mine.shape[0], part)
         down_weight = down_weight.transpose(1, 2, 0, 3).reshape(hidden, D)
-        out_mine = gather_rows(lax.dynamic_slice_in_dim(w_attn_out, seq * part, part, axis=1)).reshape(D, part)
-        out_cols = stack_seq(out_mine)
-        out_weight = jnp.swapaxes(out_cols, 0, 1).reshape(D, D)
     else:
-        down_weight = lax.all_gather(w_out_proj, "fsdp", axis=0, tiled=True)
+        down_weight = lax.all_gather(w_out_proj_late, "fsdp", axis=0, tiled=True)
         down_weight = lax.dynamic_slice_in_dim(down_weight, seq * hidden, hidden, axis=0)
-        out_weight = lax.all_gather(w_attn_out, "fsdp", axis=0, tiled=True)
+    cot_blocks = [cot] + share_seq(cot_late)[1:]
+
+    def in_order(blocks):
+        bit = 1
+        while bit < seq_size:
+            flip = (seq & bit) != 0
+            blocks = [jnp.where(flip, blocks[k ^ bit], blocks[k]) for k in range(seq_size)]
+            bit *= 2
+        return blocks
+
+    out_weight = jnp.concatenate(in_order(share_seq(out_mine)), axis=1)
 
     def by_block(row):
         return jnp.concatenate([lax.dynamic_slice_in_dim(row, r * tokens, tokens) for r in rel])
@@ -418,10 +500,7 @@
         came = [blocks[:tokens]] + [
             swap(blocks[i * tokens : (i + 1) * tokens], "seq", i) for i in range(1, seq_size)
         ]
-        whole = jnp.zeros((tokens, D), blocks.dtype)
-        for r, block in zip(rel, came):
-            whole = lax.dynamic_update_slice(whole, block, (0, r * part))
-        return whole
+        return jnp.concatenate(in_order(came), axis=1)
 
     mixed_low = to_tokens(mixed)
     x = x_low.astype(F32)
@@ -430,17 +509,11 @@
     normed_two = (normal(middle)[0] * gain_two).astype(BF)
 
     b_blocks = share_seq(normed_two)
-    m_blocks, gz_i, gz_g, gb_blocks = [], [], [], []
-    for b, g in zip(b_blocks, cot_blocks):
-        grad_hidden = matmul_nt(g, down_weight)
-        inner, gate = matmul(b, in_weight[0]), matmul(b, in_weight[1])
-        value, pull = jax.vjp(gelu_gate, inner, gate)
-        gi, gg = pull(grad_hidden)
-        gi, gg = gi.astype(BF), gg.astype(BF)
-        m_blocks.append(value.astype(BF))
-        gz_i.append(gi)
-        gz_g.append(gg)
-        gb_blocks.append(matmul_nt(gi, in_weight[0]) + matmul_nt(gg, in_weight[1]))
+    fed = [
+        feed_forward(b, g, in_weight, down_weight, F32 if i == 0 else BF)
+        for i, (b, g) in enumerate(zip(b_blocks, cot_blocks))
+    ]
+    m_blocks, gz_i, gz_g, gb_blocks, mlp_blocks = zip(*fed)
     grad_normed_two = reduce_seq(gb_blocks)
     grad_middle = cot.astype(F32) + norm_back(grad_normed_two, gain_two, middle)
     grad_attn_low = grad_middle.astype(BF)
@@ -452,7 +525,7 @@
 
     grad_by_heads = to_heads(grad_mixed)
 
-    mlp_branch = reduce_seq([matmul(m, down_weight) for m in m_blocks])
+    mlp_branch = reduce_seq([mlp_blocks[0]] + [after(m, grad_by_heads) for m in mlp_blocks[1:]])
     result = middle + mlp_branch
     valid_mine = valid_all[:tokens].astype(F32)[:, None]
     stats = jnp.stack(
@@ -466,49 +539,53 @@
     stats = sum_everywhere(jnp.broadcast_to(stats[:, None], (4, 128)))[:, 0]
     root_means = jnp.sqrt(stats[:3] / (jnp.maximum(stats[3], 1.0) * D))
 
-    def share_columns(mine):
-        rows, count, width = mine.shape
-        low = mine.astype(BF)
-        if paired():
-            every = stack_seq(low)
-        else:
-            every = lax.all_gather(low, "seq", axis=0)
-        return every.transpose(1, 2, 0, 3).reshape(rows, count * seq_size * width).astype(F32)
-
-    b_all, m_all = jnp.concatenate(b_blocks), jnp.concatenate(m_blocks)
-    cot_all = jnp.concatenate(cot_blocks)
-    gz_all = jnp.concatenate([jnp.concatenate(gz_i), jnp.concatenate(gz_g)], axis=1)
-    grad_in_mine = reduce_rows(matmul_tn(b_all, gz_all))
-    grad_in_weight = share_columns(grad_in_mine.reshape(-1, 2, hidden))
-    grad_down_part = matmul_tn(m_all, cot_all)
-    grad_out_part = matmul_tn(mixed_low, grad_attn_low)
-    if paired():
-        rows = hidden // 2
-        halves = reduce_core(grad_down_part.reshape(1, 2, rows, D))[0]
-        quarter = reduce_z(halves.reshape(rows, seq_size, part).transpose(1, 0, 2))
-        quarter = transpose_devices(quarter.astype(BF)).astype(F32)
-        grad_down = share_columns(quarter[:, None, :])
-        rows = D // fsdp_size
-        out_core = reduce_core(grad_out_part.reshape(fsdp_size // 2, 2, rows, D)).reshape(D // 2, D)
-        out_seq = reduce_seq([lax.dynamic_slice_in_dim(out_core, r * part, part, axis=1) for r in rel])
-        out_mine = reduce_z(out_seq.reshape(fsdp_size // 2, rows, part))
-        grad_out_weight = share_columns(out_mine[:, None, :])
-    else:
-        spread = jnp.zeros((FF, D), F32)
-        spread = lax.dynamic_update_slice(spread, grad_down_part, (seq * hidden, 0))
-        grad_down = lax.psum(lax.psum_scatter(spread, "fsdp", scatter_dimension=0, tiled=True), "seq")
-        grad_out_weight = lax.psum(
-            lax.psum_scatter(grad_out_part, "fsdp", scatter_dimension=0, tiled=True), "seq"
-        )
+    def own_rows(partial):
+        return lax.psum_scatter(partial, "fsdp", scatter_dimension=0, tiled=True)
+
+    fed_grads = weight_gradients(b_blocks, cot_blocks, gz_i, gz_g, m_blocks)
+    fed_rows = own_rows(fed_grads)
+    out_part = matmul_tn(mixed_low, after(grad_attn_low, grad_by_heads)).astype(BF)
+    out_quarter = reduce_seq(
+        [lax.dynamic_slice_in_dim(out_part, r * part, part, axis=1) for r in rel]
+    )
+    out_rows = own_rows(after(out_quarter.astype(BF), fed_rows))
 
     gp = attend_backward(
         q, k, v, grad_by_heads, lse, seg_col, valid_col, seg_row, cosine, sine, tokens
     )
+    if paired():
+        mine, away = last_gradients(a_low, gp, fsdp, fsdp_size)
+        last = reduce_rows(mine, away, fsdp_size)
+    else:
+        last = lax.psum_scatter(matmul_tn(a_low, gp), "fsdp", scatter_dimension=0, tiled=True)
     ga_parts = matmul_nt(gp, qkv_weight)
-    grad_qkv_mine = reduce_rows(matmul_tn(a_low, gp))
-    grad_normed = reduce_seq_relay([ga_parts[i * tokens : (i + 1) * tokens] for i in range(seq_size)])
+
+    fed = [fed_rows[:, i * slot : i * slot + hidden] for i in range(3)]
+    if paired():
+        every = lax.all_gather(jnp.stack([fed[0], fed[1], transpose_devices(fed[2])]), "seq", axis=0)
+        half = hidden // 2
+        core = fsdp % 2
+        low, high = every[:, 2, :, :half], every[:, 2, :, half:]
+        kept, came = jnp.where(core == 0, low, high), swap(jnp.where(core == 0, high, low), "fsdp", 1)
+        even, odd = jnp.where(core == 0, kept, came), jnp.where(core == 0, came, kept)
+        grad_down = jnp.concatenate([half_rows[i].T for i in range(seq_size) for half_rows in (even, odd)], axis=1)
+        grad_down = grad_down.astype(F32)
+    else:
+        every = lax.all_gather(jnp.stack(fed[:2]), "seq", axis=0)
+        down = lax.all_gather(fed[2], ("seq", "fsdp"), axis=0, tiled=True)
+        down = down.reshape(seq_size, D, hidden).transpose(0, 2, 1).reshape(FF, D)
+        mine = FF // fsdp_size
+        grad_down = lax.dynamic_slice_in_dim(down, fsdp * mine, mine, axis=0).astype(F32)
+    grad_in_weight = jnp.concatenate([every[j, i] for i in range(2) for j in range(seq_size)], axis=1).astype(F32)
+
+    last = last.astype(BF)
+    last = jnp.stack([last[:, i * part : (i + 1) * part] for i in range(3)] + [out_rows])
+    last = in_order(share_seq(last))
+    grad_qkv_weight = jnp.concatenate([p[i] for i in range(3) for p in last], axis=1).astype(F32)
+    grad_out_weight = jnp.concatenate([p[3] for p in last], axis=1).astype(F32)
+
+    grad_normed = reduce_seq([ga_parts[i * tokens : (i + 1) * tokens] for i in range(seq_size)])
     grad_inputs = grad_middle + norm_back(grad_normed, gain_one, x)
-    grad_qkv_weight = share_columns(grad_qkv_mine.reshape(-1, 3, part))
 
     def gain_gradient(weight, gradient, gain):
         return jnp.sum(weight.astype(F32) * gradient, axis=1) / gain.astype(F32)

time: 575 us -> 424 us (0.74); the launches traced: 568 us -> 424 us
  local copies, waits for them, and re-layouts: 153 us -> 34.6 us
  starting transfers between devices: 141 us -> 72 us
  Pallas kernels: 50.5 us -> 108 us
  matrix products: 62.1 us -> 9.45 us
  waiting for transfers between devices: 114 us -> 141 us
  between operations: 3.55 us -> 15.9 us
    dynamic_update_slice x52 -> x0, local copies, waits for them, and re-layouts: 76.1 us -> none  [the longest x19 47.4 us: stack_seq(): whole = lax.dynamic_update_index_in_dim(whole, part, me ^ k, 0)]
    ppermute x103 -> x46, starting transfers between devices: 139 us -> 70.4 us  [swap(): lax.ppermute(x, axis, [(i, i ^ bit) for i in range(lax.axis_size(axis))])]
    pallas_call x0 -> x6, Pallas kernels: none -> 57.2 us  [the longest x4 39 us: feed_forward(): pl.pallas_call(feed_kernel, out_shape=[narrow, narrow, narrow, full, full...]
    dot_general x4 -> x1, matrix products: 24.1 us -> 0.73 us  [matmul_tn(): lax.dot_general(a, b, (((0,), (0,)), ((), ())), preferred_element_type=F32)]
    all_gather x0 -> x4, waiting for transfers between devices: none -> 23.2 us  [the longest x1 23.2 us: on_device(): lax.all_gather(jnp.stack([fed[0], fed[1], transpose_devices(fed[2])]), 's...]
    dot_general x14 -> x2, matrix products: 23.4 us -> 6.39 us  [matmul_nt(): lax.dot_general(a, b, (((1,), (1,)), ((), ())), preferred_element_type=F32)]
    broadcast_in_dim x27 -> x0, local copies, waits for them, and re-layouts: 12.8 us -> none  [the longest x8 5.19 us: stack_seq(): whole = lax.dynamic_update_index_in_dim(whole, part, me ^ k, 0)]
    dot_general x13 -> x1, matrix products: 14.6 us -> 2.33 us  [matmul(): return jnp.dot(a, b, preferred_element_type=F32)]
  transfers between devices with their start and end apart: 105 -> 54, of which waited for: 28 -> 25; matrix products, arithmetic and copies ran while one was open for 43% -> 17% of each run, Pallas kernels for 9% -> 18%
where the time goes in v2:
time: 424 us
  waiting for transfers between devices  141 us (33%)
  Pallas kernels  108 us (25%)
  starting transfers between devices  72 us (17%)
  other arithmetic  42.9 us (10%)
  local copies, waits for them, and re-layouts  34.6 us (8%)
  between operations  15.9 us (4%)
  matrix products  9.45 us (2%)
    ppermute x46, waiting for transfers between devices, swap(): lax.ppermute(x, axis, [(i, i ^ bit) for i in range(lax.axis_size(axis))])  109 us
    ppermute x46, starting transfers between devices, swap(): lax.ppermute(x, axis, [(i, i ^ bit) for i in range(lax.axis_size(axis))])  70.4 us
    pallas_call x4, Pallas kernels, feed_forward(): pl.pallas_call(feed_kernel, out_shape=[narrow, narrow, narrow, full, full...  39 us
    pallas_call x1, Pallas kernels, attend_backward(): pl.pallas_call(backward_kernel, grid=(length // rows,), in_specs=[tile, t...  24 us
    all_gather x1, waiting for transfers between devices, on_device(): lax.all_gather(jnp.stack([fed[0], fed[1], transpose_devices(fed[2])]), 's...  23.2 us
    pallas_call x1, Pallas kernels, attend_forward(): pl.pallas_call(forward_kernel, grid=(length // rows,), in_specs=[tile, wh...  19.3 us
    unnamed x113, local copies, waits for them, and re-layouts  13.9 us
    pallas_call x1, Pallas kernels, weight_gradients(): pl.pallas_call(functools.partial(weight_kernel, count, slot), grid=(width...  10 us
  transfers between devices with their start and end apart: 54, of which 25 were waited for; matrix products, arithmetic and copies ran while one was open for 17% of the time, Pallas kernels for 18%

profile of v2, /device:TPU:0, one launch (start us, length us, event | category | flops | bytes accessed | tf_op | source)
XLA Modules:
  0.0 423.8 jit_solution(1905486292705447968)
XLA Ops:
  9.1 3.0 collective-permute-start
  19.9 3.1 collective-permute-start.5
  25.1 11.8 %collective-permute-done.1.refs_2_ = bf16[256,1024]{1,0:T(8,128)(2,1)S(1)} collective-permute-done((bf16[256,1024]{1,0:T(8,128)(2,1)}, bf16[256,1024]{1,0:T(8,128)(2,1)S(1)}, u32[]{:S(2)}, u32[]{:S(2)}) %collective-permute-start.1) | collective-permute-done | bytes 524320 | tf_op jit(solution)/shard_map/ppermute | solution.py:23
  50.0 12.4 %collective-permute-start.10 = (bf16[1024,256]{1,0:T(8,128)(2,1)S(1)}, bf16[1024,256]{1,0:T(8,128)(2,1)S(1)}, u32[]{:S(2)}, u32[]{:S(2)}) collective-permute-start(bf16[1024,256]{1,0:T(8,128)(2,1)S(1)} %slice.245), channel_id=1, source_target_pairs={{0,16},{8,24},{16,0},{24,8},{1,17},{9,25},{17,1},{25,9},{2,18},{10... | collective-permute-start | bytes 1572872 | tf_op jit(solution)/shard_map/ppermute | solution.py:23
  62.4 3.6 collective-permute-start.11
  70.0 7.3 %qkv.1 = (bf16[1024,1024]{1,0:T(8,128)(2,1)}, bf16[1024,256]{1,0:T(8,128)(2,1)}, bf16[1024,256]{1,0:T(8,128)(2,1)}, bf16[1024,256]{1,0:T(8,128)(2,1)}) custom-call(bf16[256,1024]{1,0:T(8,128)(2,1)} %bitcast.199, bf16[256,1024]{1,0:T(8,128)(2,1)} %copy-done.39, bf16[256,1024]{1,0:T(8,128)(2,1)} %copy-done.40, bf16[256,1024]{1,0:T(8,128)(2,1)} %copy-done.41, ...), custom_call_target="tpu_custom_call" | custom-call | flops 1610612736 | bytes 7340032 | tf_op jit(solution)/shard_map/qkv/pallas_call | solution.py:134
  77.3 19.3 %attend.1 = (bf16[1024,256]{1,0:T(8,128)(2,1)}, f32[8,1024]{1,0:T(8,128)}) custom-call(bf16[1024,256]{1,0:T(8,128)(2,1)} %get-tuple-element.49.q_ref, bf16[1024,256]{1,0:T(8,128)(2,1)} %get-tuple-element.50.k_ref, bf16[1024,256]{1,0:T(8,128)(2,1)} %get-tuple-element.51.v_ref, s32[1024,1]{1,0:T(8,128)} %copy.33.segc_ref, s32[1024,1]{1,0:T(8,128)} %copy.34.valc_ref, ...), custom_call_target="tpu_custom_call" | custom-call | flops 1073741824 | bytes 2097152 | tf_op jit(solution)/shard_map/attend/pallas_call | solution.py:193
  125.5 6.8 %feed.4 = (bf16[256,656]{1,0:T(8,128)(2,1)}, bf16[256,656]{1,0:T(8,128)(2,1)}, bf16[256,656]{1,0:T(8,128)(2,1)}, f32[256,1024]{1,0:T(8,128)}, f32[256,1024]{1,0:T(8,128)}) custom-call(bf16[256,1024]{1,0:T(8,128)(2,1)} %copy-done.23, bf16[256,1024]{1,0:T(8,128)(2,1)} %bitcast.219, bf16[1024,1536]{1,0:T(8,128)(2,1)} %all-gather.8.cloned.1.call-done.w_ref, ...), custom_call_target="tpu_custom_call" | custom-call | flops 2063597568 | bytes 7135232 | tf_op jit(solution)/shard_map/feed/pallas_call | solution.py:321
  133.1 6.5 %feed.5 = (bf16[256,656]{1,0:T(8,128)(2,1)}, bf16[256,656]{1,0:T(8,128)(2,1)}, bf16[256,656]{1,0:T(8,128)(2,1)}, bf16[256,1024]{1,0:T(8,128)(2,1)}, bf16[256,1024]{1,0:T(8,128)(2,1)}) custom-call(bf16[256,1024]{1,0:T(8,128)(2,1)} %copy-done.42, bf16[256,1024]{1,0:T(8,128)(2,1)} %collective-permute-done.14.g_ref.refs_5_, ...), custom_call_target="tpu_custom_call" | custom-call | flops 2063597568 | bytes 7135232 | tf_op jit(solution)/shard_map/feed/pallas_call | solution.py:321
  139.6 15.0 %collective-permute-done.17.g_ref.refs_6_ = bf16[256,1024]{1,0:T(8,128)(2,1)} collective-permute-done((bf16[256,1024]{1,0:T(8,128)(2,1)S(1)}, bf16[256,1024]{1,0:T(8,128)(2,1)}, u32[]{:S(2)}, u32[]{:S(2)}) %collective-permute-start.17) | collective-permute-done | bytes 524320 | tf_op jit(solution)/shard_map/ppermute | solution.py:23
  154.5 6.5 %collective-permute-done.16.b_ref.refs_2_ = bf16[256,1024]{1,0:T(8,128)(2,1)} collective-permute-done((bf16[256,1024]{1,0:T(8,128)(2,1)S(1)}, bf16[256,1024]{1,0:T(8,128)(2,1)}, u32[]{:S(2)}, u32[]{:S(2)}) %collective-permute-start.16) | collective-permute-done | bytes 524320 | tf_op jit(solution)/shard_map/ppermute | solution.py:23
  161.1 6.4 %feed.6 = (bf16[256,656]{1,0:T(8,128)(2,1)}, bf16[256,656]{1,0:T(8,128)(2,1)}, bf16[256,656]{1,0:T(8,128)(2,1)}, bf16[256,1024]{1,0:T(8,128)(2,1)}, bf16[256,1024]{1,0:T(8,128)(2,1)}) custom-call(bf16[256,1024]{1,0:T(8,128)(2,1)} %collective-permute-done.16.b_ref.refs_2_, bf16[256,1024]{1,0:T(8,128)(2,1)} %collective-permute-done.17.g_ref.refs_6_, ...), custom_call_target="tpu_custom_call" | custom-call | flops 2063597568 | bytes 7135232 | tf_op jit(solution)/shard_map/feed/pallas_call | solution.py:321
  167.5 19.3 %feed.7 = (bf16[256,656]{1,0:T(8,128)(2,1)}, bf16[256,656]{1,0:T(8,128)(2,1)}, bf16[256,656]{1,0:T(8,128)(2,1)}, bf16[256,1024]{1,0:T(8,128)(2,1)}, bf16[256,1024]{1,0:T(8,128)(2,1)}) custom-call(bf16[256,1024]{1,0:T(8,128)(2,1)} %collective-permute-done.19.b_ref.refs_3_, bf16[256,1024]{1,0:T(8,128)(2,1)} %collective-permute-done.20.g_ref.refs_7_, ...), custom_call_target="tpu_custom_call" | custom-call | flops 2063597568 | bytes 7135232 | tf_op jit(solution)/shard_map/feed/pallas_call | solution.py:321
  186.8 10.0 %weight_gradients.1 = bf16[1024,2304]{1,0:T(8,128)(2,1)} custom-call(bf16[256,1024]{1,0:T(8,128)(2,1)} %copy-done.23, bf16[256,1024]{1,0:T(8,128)(2,1)} %copy-done.42, bf16[256,1024]{1,0:T(8,128)(2,1)} %collective-permute-done.16.b_ref.refs_2_, bf16[256,1024]{1,0:T(8,128)(2,1)} %collective-permute-done.19.b_ref.refs_3_, bf16[256,1024]{1,0:T(8,128)(2,1)} %bitcast.220, ...), custom_call_target="tpu_custom_call" | custom-call | flops 4127195136 | bytes 12255232 | tf_op jit(solution)/shard_map/weight_gradients/pallas_call | solution.py:355
  201.1 10.9 %collective-permute-done.15 = bf16[256,1024]{1,0:T(8,128)(2,1)S(1)} collective-permute-done((bf16[256,1024]{1,0:T(8,128)(2,1)}, bf16[256,1024]{1,0:T(8,128)(2,1)S(1)}, u32[]{:S(2)}, u32[]{:S(2)}) %collective-permute-start.15) | collective-permute-done | bytes 524320 | tf_op jit(solution)/shard_map/ppermute | solution.py:23
  212.0 7.6 %collective-permute-done.18 = bf16[256,1024]{1,0:T(8,128)(2,1)} collective-permute-done((bf16[256,1024]{1,0:T(8,128)(2,1)}, bf16[256,1024]{1,0:T(8,128)(2,1)}, u32[]{:S(2)}, u32[]{:S(2)}) %collective-permute-start.18) | collective-permute-done | bytes 524320 | tf_op jit(solution)/shard_map/ppermute | solution.py:23
  237.3 24.0 %attend_back.1.gp_ref = bf16[1024,768]{1,0:T(8,128)(2,1)} custom-call(bf16[1024,256]{1,0:T(8,128)(2,1)} %get-tuple-element.49.q_ref, bf16[1024,256]{1,0:T(8,128)(2,1)} %pad_maximum_fusion.5.go_ref, f32[8,1024]{1,0:T(8,128)} %get-tuple-element.67.lse_ref, bf16[1024,256]{1,0:T(8,128)(2,1)} %get-tuple-element.50.k_ref, ...), custom_call_target="tpu_custom_call" | custom-call | flops 2684354560 | bytes 5242880 | tf_op jit(solution)/shard_map/attend_back/pallas_call | solution.py:260
  261.3 5.6 %fusion.62 = (bf16[1024,1024]{1,0:T(8,128)(2,1)S(1)}, f32[1024,1024]{1,0:T(8,128)}) fusion(bf16[1024,768]{1,0:T(8,128)(2,1)} %attend_back.1.gp_ref, bf16[1024,1024]{1,0:T(8,128)(2,1)} %all-gather.6.cloned.1.call-done), kind=kOutput, calls=%fused_computation.200 | convolution fusion | flops 1611661312 | bytes 9437184 | tf_op jit(solution)/shard_map/dot_general | solution.py:428
  275.0 8.1 %last_gradients.1 = (f32[512,768]{1,0:T(8,128)}, bf16[512,768]{1,0:T(8,128)(2,1)}) custom-call(s32[1]{0:T(128)} %bitcast.21.me_ref, bf16[1024,1024]{1,0:T(8,128)(2,1)} %get-tuple-element.68.a_ref, bf16[1024,768]{1,0:T(8,128)(2,1)} %attend_back.1.gp_ref), custom_call_target="tpu_custom_call" | custom-call | flops 1610612736 | bytes 6029312 | tf_op jit(solution)/shard_map/last_gradients/pallas_call | solution.py:386
  285.2 4.3 %fusion.10 = (f32[]{:T(128)}, f32[]{:T(128)}, f32[]{:T(128)}, f32[256,1024]{1,0:T(8,128)}) fusion(f32[256]{0:T(256)S(1)} %copy-done.35, f32[256,1024]{1,0:T(8,128)S(1)} %get-tuple-element.106, f32[256,1024]{1,0:T(8,128)} %get-tuple-element.167, bf16[256,1024]{1,0:T(8,128)(2,1)} %collective-permute-done.27, bf16[256,1024]{1,0:T(8,128)(2,1)} %collective-permute-done.26, ...), kind=kLoop, calls=%fused_computation.22 | loop fusion | flops 4194301 | bytes 5768204 | tf_op jit(solution)/shard_map/reduce_sum | solution.py:533
  296.2 4.5 %collective-permute-done.44 = f32[4,128]{0,1:T(8,128)S(1)} collective-permute-done((f32[4,128]{0,1:T(8,128)S(1)}, f32[4,128]{0,1:T(8,128)S(1)}, u32[]{:S(2)}, u32[]{:S(2)}) %collective-permute-start.44) | collective-permute-done | bytes 2080 | tf_op jit(solution)/shard_map/ppermute | solution.py:23
  302.1 4.6 %collective-permute-done.45 = f32[4,128]{0,1:T(8,128)S(1)} collective-permute-done((f32[4,128]{0,1:T(8,128)S(1)}, f32[4,128]{0,1:T(8,128)S(1)}, u32[]{:S(2)}, u32[]{:S(2)}) %collective-permute-start.45) | collective-permute-done | bytes 2080 | tf_op jit(solution)/shard_map/ppermute | solution.py:23
  308.7 8.7 %collective-permute-done.36 = bf16[1024,256]{1,0:T(8,128)(2,1)S(1)} collective-permute-done((bf16[1024,256]{1,0:T(8,128)(2,1)S(1)}, bf16[1024,256]{1,0:T(8,128)(2,1)S(1)}, u32[]{:S(2)}, u32[]{:S(2)}) %collective-permute-start.36) | collective-permute-done | bytes 524320 | tf_op jit(solution)/shard_map/ppermute | solution.py:23
  320.8 3.0 fusion.53
  324.1 4.3 %collective-permute-start.34 = (bf16[128,768]{1,0:T(8,128)(2,1)S(1)}, bf16[128,768]{1,0:T(8,128)(2,1)S(1)}, u32[]{:S(2)}, u32[]{:S(2)}) collective-permute-start(bf16[128,768]{1,0:T(8,128)(2,1)S(1)} %get-tuple-element.137), channel_id=1, source_target_pairs={{0,6},{1,7},{2,4},{3,5},{4,2},{5,3},{6,0},{7,1},{8,14},{9,15},{10,... | collective-permute-start | bytes 589832 | tf_op jit(solution)/shard_map/ppermute | solution.py:23
  330.6 3.8 collective-permute-done.32
  334.4 8.4 %collective-permute-done.33 = bf16[128,768]{1,0:T(8,128)(2,1)S(1)} collective-permute-done((bf16[128,768]{1,0:T(8,128)(2,1)S(1)}, bf16[128,768]{1,0:T(8,128)(2,1)S(1)}, u32[]{:S(2)}, u32[]{:S(2)}) %collective-permute-start.33) | collective-permute-done | bytes 196640 | tf_op jit(solution)/shard_map/ppermute | solution.py:23
  344.7 8.7 %reduce-scatter.5.cloned.1.call-done = bf16[128,256]{1,0:T(8,128)(2,1)} async-done(((bf16[1024,256]{1,0:T(8,128)(2,1)}), bf16[128,256]{1,0:T(8,128)(2,1)}) %reduce-scatter.5.cloned.1.call-update) | async-done | bytes 65552 | tf_op jit(solution)/shard_map/reduce_scatter | solution.py:543
  359.6 7.3 %collective-permute-done.38 = bf16[4,128,256]{2,1,0:T(8,128)(2,1)S(1)} collective-permute-done((bf16[4,128,256]{2,1,0:T(8,128)(2,1)S(1)}, bf16[4,128,256]{2,1,0:T(8,128)(2,1)S(1)}, u32[]{:S(2)}, u32[]{:S(2)}) %collective-permute-start.38) | collective-permute-done | bytes 262176 | tf_op jit(solution)/shard_map/ppermute | solution.py:23
  368.6 3.9 collective-permute-done.40
  375.8 23.2 %all-gather.12.cloned.1.call-done = bf16[12,128,656]{1,2,0:T(8,128)(2,1)} async-done(((bf16[3,128,656]{1,2,0:T(8,128)(2,1)}), bf16[12,128,656]{1,2,0:T(8,128)(2,1)}) %all-gather.12.cloned.1.call-update) | async-done | bytes 2015248 | tf_op jit(solution)/shard_map/all_gather | solution.py:565
  410.5 3.2 multiply_reduce_fusion
  (303 shorter events, 132.8 us)
Async XLA Ops:
  7.2 41.7 %all-gather.6.cloned.1.call-start = ((), (), s32[]{:S(2)}) async-start(), calls=%async_computation.2 | async-start | bytes 2359296 | tf_op jit(solution)/shard_map/all_gather | solution.py:46
  9.0 110.2 %all-gather.10.cloned.1.call-start = ((), (), s32[]{:S(2)}) async-start(), calls=%async_computation.4 | async-start | bytes 1511424 | tf_op jit(solution)/shard_map/all_gather | solution.py:46
  9.1 16.0 %collective-permute-start = (bf16[256,1024]{1,0:T(8,128)(2,1)}, bf16[256,1024]{1,0:T(8,128)(2,1)S(1)}, u32[]{:S(2)}, u32[]{:S(2)}) collective-permute-start(bf16[256,1024]{1,0:T(8,128)(2,1)} %bitcast.196), channel_id=1, source_target_pairs={{0,8},{8,0},{16,24},{24,16},{1,9},{9,1},{17,25},{25,17},{2,10},{10... | collective-permute-start | bytes 1572872 | tf_op jit(solution)/shard_map/ppermute | solution.py:23
  12.1 24.8 %collective-permute-start.1 = (bf16[256,1024]{1,0:T(8,128)(2,1)}, bf16[256,1024]{1,0:T(8,128)(2,1)S(1)}, u32[]{:S(2)}, u32[]{:S(2)}) collective-permute-start(bf16[256,1024]{1,0:T(8,128)(2,1)} %bitcast.197), channel_id=1, source_target_pairs={{0,16},{8,24},{16,0},{24,8},{1,17},{9,25},{17,1},{25,9},{2,18},{10... | collective-permute-start | bytes 1572872 | tf_op jit(solution)/shard_map/ppermute | solution.py:23
  13.6 23.3 %collective-permute-start.2 = (bf16[256,1024]{1,0:T(8,128)(2,1)}, bf16[256,1024]{1,0:T(8,128)(2,1)S(1)}, u32[]{:S(2)}, u32[]{:S(2)}) collective-permute-start(bf16[256,1024]{1,0:T(8,128)(2,1)} %bitcast.198), channel_id=1, source_target_pairs={{0,24},{8,16},{16,8},{24,0},{1,25},{9,17},{17,9},{25,1},{2,26},{10... | collective-permute-start | bytes 1572872 | tf_op jit(solution)/shard_map/ppermute | solution.py:23
  39.2 86.3 %all-gather.8.cloned.1.call-start = ((), (), s32[]{:S(2)}) async-start(), calls=%async_computation.3 | async-start | bytes 3538944 | tf_op jit(solution)/shard_map/all_gather | solution.py:46
  41.3 282.5 %reduce-scatter.3.cloned.1.call-start = ((), (), s32[]{:S(2)}) async-start(), calls=%async_computation.5 | async-start | bytes 5308416 | tf_op jit(solution)/shard_map/reduce_scatter | solution.py:543
  50.0 60.3 %collective-permute-start.10 = (bf16[1024,256]{1,0:T(8,128)(2,1)S(1)}, bf16[1024,256]{1,0:T(8,128)(2,1)S(1)}, u32[]{:S(2)}, u32[]{:S(2)}) collective-permute-start(bf16[1024,256]{1,0:T(8,128)(2,1)S(1)} %slice.245), channel_id=1, source_target_pairs={{0,16},{8,24},{16,0},{24,8},{1,17},{9,25},{17,1},{25,9},{2,18},{10... | collective-permute-start | bytes 1572872 | tf_op jit(solution)/shard_map/ppermute | solution.py:23
  62.4 47.9 %collective-permute-start.11 = (bf16[1024,256]{1,0:T(8,128)(2,1)S(1)}, bf16[1024,256]{1,0:T(8,128)(2,1)S(1)}, u32[]{:S(2)}, u32[]{:S(2)}) collective-permute-start(bf16[1024,256]{1,0:T(8,128)(2,1)S(1)} %slice.245), channel_id=1, source_target_pairs={{0,8},{8,0},{16,24},{24,16},{1,9},{9,1},{17,25},{25,17},{2,10},{10... | collective-permute-start | bytes 1572872 | tf_op jit(solution)/shard_map/ppermute | solution.py:23
  65.9 44.4 %collective-permute-start.9 = (bf16[1024,256]{1,0:T(8,128)(2,1)S(1)}, bf16[1024,256]{1,0:T(8,128)(2,1)}, u32[]{:S(2)}, u32[]{:S(2)}) collective-permute-start(bf16[1024,256]{1,0:T(8,128)(2,1)S(1)} %slice.245), channel_id=1, source_target_pairs={{0,24},{8,16},{16,8},{24,0},{1,25},{9,17},{17,9},{25,1},{2,26},{10... | collective-permute-start | bytes 1572872 | tf_op jit(solution)/shard_map/ppermute | solution.py:23
  106.3 16.3 %collective-permute-start.14 = (bf16[256,1024]{1,0:T(8,128)(2,1)S(1)}, bf16[256,1024]{1,0:T(8,128)(2,1)}, u32[]{:S(2)}, u32[]{:S(2)}) collective-permute-start(bf16[256,1024]{1,0:T(8,128)(2,1)S(1)} %bitcast.221), channel_id=1, source_target_pairs={{0,8},{8,0},{16,24},{24,16},{1,9},{9,1},{17,25},{25,17},{2,10},{10... | collective-permute-start | bytes 1572872 | tf_op jit(solution)/shard_map/ppermute | solution.py:23
  114.6 17.7 %collective-permute-start.13 = (bf16[256,1024]{1,0:T(8,128)(2,1)S(1)}, bf16[256,1024]{1,0:T(8,128)(2,1)S(1)}, u32[]{:S(2)}, u32[]{:S(2)}) collective-permute-start(bf16[256,1024]{1,0:T(8,128)(2,1)S(1)} %multiply_convert_fusion.b_ref.refs_0_), channel_id=1, source_target_pairs={{0,8},{8,0},{16,24},{24,16},{1,9},{9,1},{17,25},{25,17},{2,10},{10... | collective-permute-start | bytes 1572872 | tf_op jit(solution)/shard_map/ppermute | solution.py:23
  117.2 37.4 %collective-permute-start.17 = (bf16[256,1024]{1,0:T(8,128)(2,1)S(1)}, bf16[256,1024]{1,0:T(8,128)(2,1)}, u32[]{:S(2)}, u32[]{:S(2)}) collective-permute-start(bf16[256,1024]{1,0:T(8,128)(2,1)S(1)} %bitcast.222), channel_id=1, source_target_pairs={{0,16},{8,24},{16,0},{24,8},{1,17},{9,25},{17,1},{25,9},{2,18},{10... | collective-permute-start | bytes 1572872 | tf_op jit(solution)/shard_map/ppermute | solution.py:23
  117.2 43.9 %collective-permute-start.16 = (bf16[256,1024]{1,0:T(8,128)(2,1)S(1)}, bf16[256,1024]{1,0:T(8,128)(2,1)}, u32[]{:S(2)}, u32[]{:S(2)}) collective-permute-start(bf16[256,1024]{1,0:T(8,128)(2,1)S(1)} %multiply_convert_fusion.b_ref.refs_0_), channel_id=1, source_target_pairs={{0,16},{8,24},{16,0},{24,8},{1,17},{9,25},{17,1},{25,9},{2,18},{10... | collective-permute-start | bytes 1572872 | tf_op jit(solution)/shard_map/ppermute | solution.py:23
  119.2 48.3 %collective-permute-start.20 = (bf16[256,1024]{1,0:T(8,128)(2,1)S(1)}, bf16[256,1024]{1,0:T(8,128)(2,1)}, u32[]{:S(2)}, u32[]{:S(2)}) collective-permute-start(bf16[256,1024]{1,0:T(8,128)(2,1)S(1)} %bitcast.223), channel_id=1, source_target_pairs={{0,24},{8,16},{16,8},{24,0},{1,25},{9,17},{17,9},{25,1},{2,26},{10... | collective-permute-start | bytes 1572872 | tf_op jit(solution)/shard_map/ppermute | solution.py:23
  122.6 44.9 %collective-permute-start.19 = (bf16[256,1024]{1,0:T(8,128)(2,1)S(1)}, bf16[256,1024]{1,0:T(8,128)(2,1)}, u32[]{:S(2)}, u32[]{:S(2)}) collective-permute-start(bf16[256,1024]{1,0:T(8,128)(2,1)S(1)} %multiply_convert_fusion.b_ref.refs_0_), channel_id=1, source_target_pairs={{0,24},{8,16},{16,8},{24,0},{1,25},{9,17},{17,9},{25,1},{2,26},{10... | collective-permute-start | bytes 1572872 | tf_op jit(solution)/shard_map/ppermute | solution.py:23
  196.9 156.5 %reduce-scatter.5.cloned.1.call-start = ((), (), s32[]{:S(2)}) async-start(), calls=%async_computation.6 | async-start | bytes 589824 | tf_op jit(solution)/shard_map/reduce_scatter | solution.py:543
  197.4 22.3 %collective-permute-start.18 = (bf16[256,1024]{1,0:T(8,128)(2,1)}, bf16[256,1024]{1,0:T(8,128)(2,1)}, u32[]{:S(2)}, u32[]{:S(2)}) collective-permute-start(bf16[256,1024]{1,0:T(8,128)(2,1)} %get-tuple-element.60), channel_id=1, source_target_pairs={{0,16},{8,24},{16,0},{24,8},{1,17},{9,25},{17,1},{25,9},{2,18},{10... | collective-permute-start | bytes 1572872 | tf_op jit(solution)/shard_map/ppermute | solution.py:23
  199.0 20.7 %collective-permute-start.21 = (bf16[256,1024]{1,0:T(8,128)(2,1)}, bf16[256,1024]{1,0:T(8,128)(2,1)}, u32[]{:S(2)}, u32[]{:S(2)}) collective-permute-start(bf16[256,1024]{1,0:T(8,128)(2,1)} %get-tuple-element.61), channel_id=1, source_target_pairs={{0,24},{8,16},{16,8},{24,0},{1,25},{9,17},{17,9},{25,1},{2,26},{10... | collective-permute-start | bytes 1572872 | tf_op jit(solution)/shard_map/ppermute | solution.py:23
  233.1 40.4 %collective-permute-start.25 = (bf16[256,1024]{1,0:T(8,128)(2,1)}, bf16[256,1024]{1,0:T(8,128)(2,1)}, u32[]{:S(2)}, u32[]{:S(2)}) collective-permute-start(bf16[256,1024]{1,0:T(8,128)(2,1)} %get-tuple-element.62), channel_id=1, source_target_pairs={{0,8},{8,0},{16,24},{24,16},{1,9},{9,1},{17,25},{25,17},{2,10},{10... | collective-permute-start | bytes 1572872 | tf_op jit(solution)/shard_map/ppermute | solution.py:23
  235.9 47.3 %collective-permute-start.26 = (bf16[256,1024]{1,0:T(8,128)(2,1)}, bf16[256,1024]{1,0:T(8,128)(2,1)}, u32[]{:S(2)}, u32[]{:S(2)}) collective-permute-start(bf16[256,1024]{1,0:T(8,128)(2,1)} %get-tuple-element.64), channel_id=1, source_target_pairs={{0,16},{8,24},{16,0},{24,8},{1,17},{9,25},{17,1},{25,9},{2,18},{10... | collective-permute-start | bytes 1572872 | tf_op jit(solution)/shard_map/ppermute | solution.py:23
  236.0 47.2 %collective-permute-start.27 = (bf16[256,1024]{1,0:T(8,128)(2,1)}, bf16[256,1024]{1,0:T(8,128)(2,1)}, u32[]{:S(2)}, u32[]{:S(2)}) collective-permute-start(bf16[256,1024]{1,0:T(8,128)(2,1)} %get-tuple-element.66), channel_id=1, source_target_pairs={{0,24},{8,16},{16,8},{24,0},{1,25},{9,17},{17,9},{25,1},{2,26},{10... | collective-permute-start | bytes 1572872 | tf_op jit(solution)/shard_map/ppermute | solution.py:23
  268.2 24.0 %collective-permute-start.28 = (bf16[256,1024]{1,0:T(8,128)(2,1)}, bf16[256,1024]{1,0:T(8,128)(2,1)}, u32[]{:S(2)}, u32[]{:S(2)}) collective-permute-start(bf16[256,1024]{1,0:T(8,128)(2,1)} %get-tuple-element.116), channel_id=1, source_target_pairs={{0,8},{8,0},{16,24},{24,16},{1,9},{9,1},{17,25},{25,17},{2,10},{10... | collective-permute-start | bytes 1572872 | tf_op jit(solution)/shard_map/ppermute | solution.py:23
  270.2 22.1 %collective-permute-start.29 = (bf16[256,1024]{1,0:T(8,128)(2,1)}, bf16[256,1024]{1,0:T(8,128)(2,1)}, u32[]{:S(2)}, u32[]{:S(2)}) collective-permute-start(bf16[256,1024]{1,0:T(8,128)(2,1)} %get-tuple-element.118), channel_id=1, source_target_pairs={{0,16},{8,24},{16,0},{24,8},{1,17},{9,25},{17,1},{25,9},{2,18},{10... | collective-permute-start | bytes 1572872 | tf_op jit(solution)/shard_map/ppermute | solution.py:23
  273.6 20.1 %collective-permute-start.30 = (bf16[256,1024]{1,0:T(8,128)(2,1)}, bf16[256,1024]{1,0:T(8,128)(2,1)}, u32[]{:S(2)}, u32[]{:S(2)}) collective-permute-start(bf16[256,1024]{1,0:T(8,128)(2,1)} %get-tuple-element.117), channel_id=1, source_target_pairs={{0,24},{8,16},{16,8},{24,0},{1,25},{9,17},{17,9},{25,1},{2,26},{10... | collective-permute-start | bytes 1572872 | tf_op jit(solution)/shard_map/ppermute | solution.py:23
  283.1 36.8 %collective-permute-start.31 = (bf16[512,768]{1,0:T(8,128)(2,1)}, bf16[512,768]{1,0:T(8,128)(2,1)S(1)}, u32[]{:S(2)}, u32[]{:S(2)}) collective-permute-start(bf16[512,768]{1,0:T(8,128)(2,1)} %get-tuple-element.70), channel_id=1, source_target_pairs={{0,1},{1,0},{2,3},{3,2},{4,5},{5,4},{6,7},{7,6},{8,9},{9,8},{10,11... | collective-permute-start | bytes 2359304 | tf_op jit(solution)/shard_map/ppermute | solution.py:23
  283.1 25.6 %collective-permute-start.35 = (bf16[1024,256]{1,0:T(8,128)(2,1)}, bf16[1024,256]{1,0:T(8,128)(2,1)S(1)}, u32[]{:S(2)}, u32[]{:S(2)}) collective-permute-start(bf16[1024,256]{1,0:T(8,128)(2,1)} %get-tuple-element.113), channel_id=1, source_target_pairs={{0,8},{8,0},{16,24},{24,16},{1,9},{9,1},{17,25},{25,17},{2,10},{10... | collective-permute-start | bytes 1572872 | tf_op jit(solution)/shard_map/ppermute | solution.py:23
  292.2 25.3 %collective-permute-start.36 = (bf16[1024,256]{1,0:T(8,128)(2,1)S(1)}, bf16[1024,256]{1,0:T(8,128)(2,1)S(1)}, u32[]{:S(2)}, u32[]{:S(2)}) collective-permute-start(bf16[1024,256]{1,0:T(8,128)(2,1)S(1)} %copy-done.22), channel_id=1, source_target_pairs={{0,16},{8,24},{16,0},{24,8},{1,17},{9,25},{17,1},{25,9},{2,18},{10... | collective-permute-start | bytes 1572872 | tf_op jit(solution)/shard_map/ppermute | solution.py:23
  292.3 25.1 %collective-permute-start.37 = (bf16[1024,256]{1,0:T(8,128)(2,1)S(1)}, bf16[1024,256]{1,0:T(8,128)(2,1)S(1)}, u32[]{:S(2)}, u32[]{:S(2)}) collective-permute-start(bf16[1024,256]{1,0:T(8,128)(2,1)S(1)} %copy-done.21), channel_id=1, source_target_pairs={{0,24},{8,16},{16,8},{24,0},{1,25},{9,17},{17,9},{25,1},{2,26},{10... | collective-permute-start | bytes 1572872 | tf_op jit(solution)/shard_map/ppermute | solution.py:23
  323.9 75.1 %all-gather.12.cloned.1.call-start = ((), (), s32[]{:S(2)}) async-start(), calls=%async_computation.7 | async-start | bytes 2519040 | tf_op jit(solution)/shard_map/all_gather | solution.py:565
  324.0 18.8 %collective-permute-start.33 = (bf16[128,768]{1,0:T(8,128)(2,1)S(1)}, bf16[128,768]{1,0:T(8,128)(2,1)S(1)}, u32[]{:S(2)}, u32[]{:S(2)}) collective-permute-start(bf16[128,768]{1,0:T(8,128)(2,1)S(1)} %get-tuple-element.138), channel_id=1, source_target_pairs={{0,4},{1,5},{2,6},{3,7},{4,0},{5,1},{6,2},{7,3},{8,12},{9,13},{10,... | collective-permute-start | bytes 589832 | tf_op jit(solution)/shard_map/ppermute | solution.py:23
  324.1 18.7 %collective-permute-start.34 = (bf16[128,768]{1,0:T(8,128)(2,1)S(1)}, bf16[128,768]{1,0:T(8,128)(2,1)S(1)}, u32[]{:S(2)}, u32[]{:S(2)}) collective-permute-start(bf16[128,768]{1,0:T(8,128)(2,1)S(1)} %get-tuple-element.137), channel_id=1, source_target_pairs={{0,6},{1,7},{2,4},{3,5},{4,2},{5,3},{6,0},{7,1},{8,14},{9,15},{10,... | collective-permute-start | bytes 589832 | tf_op jit(solution)/shard_map/ppermute | solution.py:23
  (65 other events, 516.6 us)
Sparse Core Ops, SparseCore 0:
  10.2 32.1 all-gather.5
  44.0 32.6 all-gather.9
  78.3 37.8 all-gather.7
  197.0 52.0 reduce-scatter.2
  324.0 29.3 reduce-scatter.4
  359.7 39.2 all-gather.11

commit v3 on v2

--- a/solution.py
+++ b/solution.py
@@ -31,10 +31,31 @@
     return [block] + [swap(block, "seq", k) for k in range(1, lax.axis_size("seq"))]
 
 
-def reduce_seq(blocks):
-    total = blocks[0]
-    for k in range(1, len(blocks)):
-        total = total + swap(blocks[k].astype(BF), "seq", k).astype(F32)
+def relay_first(block):
+    return swap(block, "seq", 1), swap(block, "seq", 2)
+
+
+def relay_last(block, one, two):
+    if lax.axis_size("seq") != 4:
+        return share_seq(block)
+    half = block.shape[0] // 2
+    upper, lower = swap(two[:half], "seq", 1), swap(one[half:], "seq", 2)
+    return [block, one, two, jnp.concatenate([upper, lower], axis=0)]
+
+
+def relay_seq(block):
+    return relay_last(block, *relay_first(block))
+
+
+def exchange_seq(blocks):
+    return lax.all_to_all(blocks, "seq", split_axis=0, concat_axis=0, tiled=True)
+
+
+def sum_blocks(blocks):
+    rows = blocks.shape[0] // lax.axis_size("seq")
+    total = blocks[:rows].astype(F32)
+    for i in range(1, lax.axis_size("seq")):
+        total = total + blocks[i * rows : (i + 1) * rows].astype(F32)
     return total
 
 
@@ -57,22 +78,10 @@
     return lax.ppermute(x, ("seq", "fsdp"), pairs)
 
 
-def reduce_rows(mine, away, size):
-    mine = mine + swap(away, "fsdp", 1).astype(F32)
-    rows = mine.shape[0] // (size // 2)
-    total = mine[:rows]
-    for k in range(1, size // 2):
-        part = mine[k * rows : (k + 1) * rows].astype(BF)
-        total = total + swap(part, "fsdp", 2 * k).astype(F32)
-    return total
-
-
-def sum_everywhere(values):
-    for axis in ("fsdp", "seq"):
-        bit = 1
-        while bit < lax.axis_size(axis):
-            values = values + swap(values, axis, bit)
-            bit *= 2
+def sum_along(values, axis, bit=1):
+    while bit < lax.axis_size(axis):
+        values = values + swap(values, axis, bit)
+        bit *= 2
     return values
 
 
@@ -293,13 +302,14 @@
     return lax.dot_general(a, b, (((1,), (1,)), ((), ())), preferred_element_type=F32)
 
 
-def feed_kernel(b_ref, g_ref, w_ref, wd_ref, m_ref, gi_ref, gg_ref, gb_ref, mlp_ref):
+def feed_kernel(hidden, me_ref, b_ref, g_ref, w_ref, *refs):
+    m_ref, gi_ref, gg_ref, gb_ref, mlp_ref = refs[-5:]
     b = b_ref[...]
-    hidden, slot = wd_ref.shape[0], w_ref.shape[1] // 2
-    wi_ref, wg_ref = w_ref.at[:, :hidden], w_ref.at[:, slot : slot + hidden]
+    slot = w_ref.shape[1] // 3
+    wi_ref, wg_ref, wd_ref = (w_ref.at[:, i * slot : i * slot + hidden] for i in range(3))
     inner = jnp.dot(b, wi_ref[...], preferred_element_type=F32)
     gate = jnp.dot(b, wg_ref[...], preferred_element_type=F32)
-    upstream = nt(g_ref[...], wd_ref[...])
+    upstream = jnp.dot(g_ref[...], wd_ref[...], preferred_element_type=F32)
     half = 0.5 * (1.0 + erf(inner * 0.7071067811865476))
     gelu = inner * half
     slope = half + inner * jnp.exp(-0.5 * inner * inner) * 0.3989422804014327
@@ -310,61 +320,83 @@
     gi_ref[...] = gi
     gg_ref[...] = gg
     gb_ref[...] = (nt(gi, wi_ref[...]) + nt(gg, wg_ref[...])).astype(gb_ref.dtype)
-    mlp_ref[...] = jnp.dot(m, wd_ref[...], preferred_element_type=F32).astype(mlp_ref.dtype)
-
-
-def feed_forward(b, g, w, wd, dtype):
+    mlp_ref[...] = nt(m, wd_ref[...]).astype(mlp_ref.dtype)
+
+
+def feed_forward(b, g, w, hidden, me, place, count, dtype, onto):
     rows, width = b.shape
-    hidden = wd.shape[0]
+    whole = lambda r, n: pl.BlockSpec((r, n), lambda i, me: (0, 0))
     narrow = jax.ShapeDtypeStruct((rows, hidden), BF)
-    full = jax.ShapeDtypeStruct((rows, width), dtype)
+    operands, specs = [b, g, w], [whole(rows, width), whole(rows, width), whole(*w.shape)]
+    if onto is not None:
+        operands.append(onto)
+        specs.append(pl.BlockSpec(memory_space=pl.ANY))
     return pl.pallas_call(
-        feed_kernel,
-        out_shape=[narrow, narrow, narrow, full, full],
+        functools.partial(feed_kernel, hidden),
+        grid_spec=pltpu.PrefetchScalarGridSpec(
+            num_scalar_prefetch=1,
+            grid=(1,),
+            in_specs=specs,
+            out_specs=[whole(rows, hidden)] * 3
+            + [whole(rows, width), pl.BlockSpec((rows, width), lambda i, me: (me[0] ^ place, 0))],
+        ),
+        out_shape=[narrow] * 3
+        + [jax.ShapeDtypeStruct((rows, width), dtype), jax.ShapeDtypeStruct((rows * count, width), BF)],
+        input_output_aliases={} if onto is None else {4: 4},
         cost_estimate=pl.CostEstimate(
             flops=12 * rows * width * hidden,
             bytes_accessed=6 * width * hidden + 8 * rows * width + 6 * rows * hidden,
             transcendentals=rows * hidden,
         ),
         name="feed",
-    )(b, g, w, wd)
+    )(me[None], *operands)
 
 
 def tn(a, b):
     return lax.dot_general(a, b, (((0,), (0,)), ((), ())), preferred_element_type=F32)
 
 
-def weight_kernel(count, slot, *refs):
-    bs, gs, gis, ggs, ms = (refs[i * count : (i + 1) * count] for i in range(5))
-    out_ref = refs[5 * count]
-    hidden = gis[0].shape[1]
-    for place, (lefts, rights) in enumerate(((bs, gis), (bs, ggs), (gs, ms))):
-        total = tn(lefts[0][...], rights[0][...])
-        for left, right in zip(lefts[1:], rights[1:]):
-            total = total + tn(left[...], right[...])
+def weight_kernel(count, slot, pairs, *refs):
+    out_ref = refs[-1]
+    hidden = refs[(pairs[0][1]) * count].shape[1]
+    for place, (left, right) in enumerate(pairs):
+        total = None
+        for i in range(count):
+            term = tn(refs[left * count + i][...], refs[right * count + i][...])
+            total = term if total is None else total + term
         out_ref[:, place * slot : place * slot + hidden] = total.astype(BF)
-
-
-def weight_gradients(bs, gs, gis, ggs, ms):
-    count = len(bs)
-    rows, width = bs[0].shape
-    hidden = gis[0].shape[1]
+        if hidden < slot:
+            out_ref[:, place * slot + hidden : (place + 1) * slot] = jnp.zeros((out_ref.shape[0], slot - hidden), BF)
+
+
+def weight_gradients(lefts, rights, pairs, slots, place, onto=None):
+    count = len(lefts[0])
+    rows, width = lefts[0][0].shape
+    hidden = rights[0][0].shape[1]
     slot = -(-hidden // LANES) * LANES
     wide_spec = pl.BlockSpec((rows, 256), lambda i: (0, i))
     whole = pl.BlockSpec((rows, hidden), lambda i: (0, 0))
+    operands = [b for group in lefts for b in group] + [b for group in rights for b in group]
+    specs = [wide_spec] * (len(lefts) * count) + [whole] * (len(rights) * count)
+    aliases = {}
+    if onto is not None:
+        aliases = {len(operands): 0}
+        operands.append(onto)
+        specs.append(pl.BlockSpec(memory_space=pl.ANY))
     return pl.pallas_call(
-        functools.partial(weight_kernel, count, slot),
+        functools.partial(weight_kernel, count, slot, pairs),
         grid=(width // 256,),
-        in_specs=[wide_spec] * (2 * count) + [whole] * (3 * count),
-        out_specs=pl.BlockSpec((256, 3 * slot), lambda i: (i, 0)),
-        out_shape=jax.ShapeDtypeStruct((width, 3 * slot), BF),
+        in_specs=specs,
+        out_specs=pl.BlockSpec((256, len(pairs) * slot), lambda i: (i, place // len(pairs))),
+        out_shape=jax.ShapeDtypeStruct((width, slots * slot), BF),
+        input_output_aliases=aliases,
         cost_estimate=pl.CostEstimate(
-            flops=6 * rows * count * width * hidden,
-            bytes_accessed=4 * rows * count * width + 6 * rows * count * hidden + 6 * width * hidden,
+            flops=2 * len(pairs) * rows * count * width * hidden,
+            bytes_accessed=2 * count * rows * (len(lefts) * width + len(rights) * hidden),
             transcendentals=0,
         ),
         name="weight_gradients",
-    )(*bs, *gs, *gis, *ggs, *ms)
+    )(*operands)
 
 
 def last_kernel(me_ref, a_ref, gp_ref, mine_ref, away_ref):
@@ -404,6 +436,86 @@
     )(me[None], a, gp)
 
 
+def qkv_back_kernel(me_ref, gp_ref, w_ref, out_ref):
+    out_ref[...] = nt(gp_ref[...], w_ref[...]).astype(BF)
+
+
+def project_back(gp, weight, me, count):
+    rows, width = gp.shape[0] // count, weight.shape[0]
+    return pl.pallas_call(
+        qkv_back_kernel,
+        grid_spec=pltpu.PrefetchScalarGridSpec(
+            num_scalar_prefetch=1,
+            grid=(count,),
+            in_specs=[
+                pl.BlockSpec((rows, gp.shape[1]), lambda i, me: (i, 0)),
+                pl.BlockSpec(weight.shape, lambda i, me: (0, 0)),
+            ],
+            out_specs=pl.BlockSpec((rows, width), lambda i, me: (me[0] ^ i, 0)),
+        ),
+        out_shape=jax.ShapeDtypeStruct((rows * count, width), BF),
+        cost_estimate=pl.CostEstimate(
+            flops=2 * rows * count * width * gp.shape[1],
+            bytes_accessed=2 * (rows * count * (width + gp.shape[1]) + width * gp.shape[1]),
+            transcendentals=0,
+        ),
+        name="project_back",
+    )(me[None], gp, weight)
+
+
+def ordered(refs, me, piece):
+    values = [ref[piece] for ref in refs]
+    bit = 1
+    while bit < len(values):
+        flip = (me & bit) != 0
+        values = [jnp.where(flip, values[k ^ bit], values[k]) for k in range(len(values))]
+        bit *= 2
+    return values
+
+
+def gain_part(w_ref, grad_ref, gain_ref, out_ref):
+    total = jnp.sum(w_ref[...].astype(F32) * grad_ref[...], axis=1, keepdims=True)
+    out_ref[...] = total / gain_ref[...].astype(F32)
+
+
+def last_rows_kernel(count, me_ref, *refs):
+    blocks, (w_ref, gain_ref, qkv_ref, out_ref, gg_ref) = refs[:count], refs[count:]
+    part = blocks[0].shape[1] // (3 + count)
+    piece = lambda i: (slice(None), slice(i * part, (i + 1) * part))
+    for i in range(3):
+        for j, value in enumerate(ordered(blocks, me_ref[0], piece(i))):
+            first = (i * count + j) * part
+            qkv_ref[:, first : first + part] = value.astype(F32)
+    for j in range(count):
+        total = None
+        for value in ordered(blocks, me_ref[0], piece(3 + j)):
+            total = value.astype(F32) if total is None else total + value.astype(F32)
+        out_ref[:, j * part : (j + 1) * part] = total
+    gain_part(w_ref, qkv_ref, gain_ref, gg_ref)
+
+
+def in_rows_kernel(count, hidden, me_ref, *refs):
+    blocks, (w_ref, gain_ref, in_ref, gg_ref) = refs[:count], refs[count:]
+    slot = blocks[0].shape[1] // 2
+    for i in range(2):
+        piece = (slice(None), slice(i * slot, i * slot + hidden))
+        values = [value.astype(F32) for value in ordered(blocks, me_ref[0], piece)]
+        in_ref[:, i * count * hidden : (i + 1) * count * hidden] = jnp.concatenate(values, axis=1)
+    gain_part(w_ref, in_ref, gain_ref, gg_ref)
+
+
+def finish_rows(kernel, blocks, weight, gain, me, widths, name):
+    rows = weight.shape[0]
+    shapes = [jax.ShapeDtypeStruct((rows, n), F32) for n in widths]
+    return pl.pallas_call(
+        kernel,
+        in_specs=[pl.BlockSpec(memory_space=pltpu.SMEM)] + [pl.BlockSpec(memory_space=pltpu.VMEM)] * (len(blocks) + 2),
+        out_shape=shapes,
+        cost_estimate=pl.CostEstimate(flops=0, bytes_accessed=8 * rows * sum(widths), transcendentals=0),
+        name=name,
+    )(me[None], *blocks, weight, gain[:, None])
+
+
 def normal(values):
     centered = values - jnp.mean(values, axis=-1, keepdims=True)
     scale = lax.rsqrt(jnp.mean(centered * centered, axis=-1, keepdims=True) + NORM_EPS)
@@ -448,28 +560,40 @@
     first_mine.append(lax.dynamic_slice_in_dim(w_attn_out, seq * part, part, axis=1))
     first_mine = jnp.concatenate(first_mine, axis=1)
     first_weight = gather_rows(first_mine)
-    x_blocks = share_seq(x_low)
+    x_near = relay_first(x_low)
+    x_blocks = relay_last(x_low, *x_near)
     gains = gather_gains(jnp.stack([attn_gain, mlp_gain])).astype(F32)
     gain_one, gain_two = gains[0:1], gains[1:2]
     qkv_weight, out_mine = first_weight[:, : 3 * part], first_weight[:, 3 * part :]
-    w_in_proj_late, w_out_proj_late, cot_late = after((w_in_proj, w_out_proj, cot), gains, *x_blocks)
+    core = fsdp % 2
     slot = -(-hidden // LANES) * LANES
+    w_out_proj_late = after(w_out_proj, *x_near)
+    w_in_proj_late, cot_late = after((w_in_proj, cot), gains, *x_blocks)
+
+    def padded(rows):
+        return jnp.pad(rows, ((0, 0), (0, slot - hidden)))
+
+    def halves(rows):
+        half = rows.shape[1] // 2
+        low, high = rows[:, :half], rows[:, half:]
+        return jnp.where(core == 0, low, high), jnp.where(core == 0, high, low)
+
+    def by_core(mine, other):
+        return jnp.where(core == 0, mine, other), jnp.where(core == 0, other, mine)
+
     in_mine = [
-        jnp.pad(
-            lax.dynamic_slice_in_dim(w_in_proj_late, i * FF + seq * hidden, hidden, axis=1),
-            ((0, 0), (0, slot - hidden)),
-        )
-        for i in range(2)
+        padded(lax.dynamic_slice_in_dim(w_in_proj_late, i * FF + seq * hidden, hidden, axis=1)) for i in range(2)
     ]
-    in_weight = gather_rows(jnp.concatenate(in_mine, axis=1))
     if paired():
         down_mine = transpose_devices(lax.dynamic_slice_in_dim(w_out_proj_late, seq * part, part, axis=1))
-        down_weight = gather_rows(down_mine).reshape(seq_size, 2, down_mine.shape[0], part)
-        down_weight = down_weight.transpose(1, 2, 0, 3).reshape(hidden, D)
+        kept, sent = halves(down_mine)
+        down_mine = jnp.concatenate(by_core(kept, swap(sent, "fsdp", 1)), axis=0)
+        feed_weight = gather_rows(jnp.concatenate(in_mine + [padded(down_mine.T)], axis=1))
     else:
         down_weight = lax.all_gather(w_out_proj_late, "fsdp", axis=0, tiled=True)
         down_weight = lax.dynamic_slice_in_dim(down_weight, seq * hidden, hidden, axis=0)
-    cot_blocks = [cot] + share_seq(cot_late)[1:]
+        feed_weight = jnp.concatenate([gather_rows(jnp.concatenate(in_mine, axis=1)), padded(down_weight.T)], axis=1)
+    cot_blocks = [cot] + relay_seq(cot_late)[1:]
 
     def in_order(blocks):
         bit = 1
@@ -507,25 +631,47 @@
     attn_branch = matmul(mixed_low, out_weight)
     middle = x + attn_branch
     normed_two = (normal(middle)[0] * gain_two).astype(BF)
+    normed_two = after(normed_two, *cot_blocks)
 
     b_blocks = share_seq(normed_two)
-    fed = [
-        feed_forward(b, g, in_weight, down_weight, F32 if i == 0 else BF)
-        for i, (b, g) in enumerate(zip(b_blocks, cot_blocks))
-    ]
-    m_blocks, gz_i, gz_g, gb_blocks, mlp_blocks = zip(*fed)
-    grad_normed_two = reduce_seq(gb_blocks)
+    fed, came, mlp_all = [None] * seq_size, [], None
+    for i in [*range(1, seq_size), 0]:
+        b = after(b_blocks[i], *came[:-2]) if len(came) > 2 else b_blocks[i]
+        fed[i] = feed_forward(
+            b, cot_blocks[i], feed_weight, hidden, seq, i, seq_size, F32 if i == 0 else BF, mlp_all
+        )
+        mlp_all = fed[i][4]
+        if i > 0:
+            came.append(swap(fed[i][3], "seq", i))
+    m_blocks, gz_i, gz_g, gb_blocks, _ = zip(*fed)
+    fed_grads = weight_gradients([after(b_blocks, *came[:-1])], [gz_i, gz_g], ((0, 1), (0, 2)), 3, 0)
+    fed_grads = weight_gradients([after(cot_blocks, *came)], [m_blocks], ((0, 1),), 3, 2, fed_grads)
+    grad_normed_two = gb_blocks[0]
+    for block in came:
+        grad_normed_two = grad_normed_two + block.astype(F32)
     grad_middle = cot.astype(F32) + norm_back(grad_normed_two, gain_two, middle)
     grad_attn_low = grad_middle.astype(BF)
     grad_mixed = matmul_nt(grad_attn_low, out_weight).astype(BF)
 
-    def to_heads(blocks):
-        sent = [lax.dynamic_slice_in_dim(blocks, r * part, part, axis=1) for r in rel]
-        return jnp.concatenate([sent[0]] + [swap(sent[i], "seq", i) for i in range(1, seq_size)], axis=0)
-
-    grad_by_heads = to_heads(grad_mixed)
-
-    mlp_branch = reduce_seq([mlp_blocks[0]] + [after(m, grad_by_heads) for m in mlp_blocks[1:]])
+    sent = [lax.dynamic_slice_in_dim(grad_mixed, r * part, part, axis=1) for r in rel]
+    came = [sent[0]] + [swap(sent[i], "seq", i) for i in range(1, seq_size)]
+    out_part = matmul_tn(mixed_low, after(grad_attn_low, came[-1])).astype(BF)
+    grad_by_heads = after(jnp.concatenate(came, axis=0), out_part, fed_grads)
+    mlp_came = exchange_seq(after(mlp_all, grad_by_heads))
+
+    def own_rows(partial):
+        return lax.psum_scatter(partial, "fsdp", scatter_dimension=0, tiled=True)
+
+    fed_rows = own_rows(fed_grads)
+    out_rows = own_rows(out_part)
+
+    gp = attend_backward(
+        q, k, v, grad_by_heads, lse, seg_col, valid_col, seg_row, cosine, sine, tokens
+    )
+    fed_late = after(fed_rows, gp)
+    in_rows, down_rows = fed_late[:, : 2 * slot], fed_late[:, 2 * slot : 2 * slot + hidden]
+    in_all = share_seq(in_rows)
+    mlp_branch = sum_blocks(after(mlp_came, gp))
     result = middle + mlp_branch
     valid_mine = valid_all[:tokens].astype(F32)[:, None]
     stats = jnp.stack(
@@ -536,59 +682,47 @@
             jnp.sum(valid_mine),
         ]
     )
-    stats = sum_everywhere(jnp.broadcast_to(stats[:, None], (4, 128)))[:, 0]
+    stats = sum_along(jnp.broadcast_to(stats[:, None], (4, 128)), "seq")
+    if paired():
+        down_rows = transpose_devices(down_rows)
+        mine, away = last_gradients(a_low, after(gp, fed_rows), fsdp, fsdp_size)
+        ga_parts = project_back(after(gp, away), qkv_weight, seq, seq_size)
+        mine = mine + after(swap(away, "fsdp", 1), ga_parts, down_rows, stats, *in_all[1:3]).astype(F32)
+        down_rows = after(down_rows, mine)
+        kept, sent = halves(down_rows)
+        down_rows = jnp.concatenate(by_core(kept, swap(sent, "fsdp", 1)), axis=0).T
+        rows = mine.shape[0] // (fsdp_size // 2)
+        came = [swap(mine[k * rows : (k + 1) * rows].astype(BF), "fsdp", 2 * k) for k in range(1, fsdp_size // 2)]
+        came = after(came, down_rows, out_rows, *in_all)
+        last = mine[:rows]
+        for block in came:
+            last = last + block.astype(F32)
+    else:
+        mine, ga_parts = matmul_tn(a_low, gp), project_back(gp, qkv_weight, seq, seq_size)
+        last = lax.psum_scatter(mine, "fsdp", scatter_dimension=0, tiled=True)
+    ga_came = exchange_seq(ga_parts)
+    stats = sum_along(stats, "fsdp")[:, 0]
     root_means = jnp.sqrt(stats[:3] / (jnp.maximum(stats[3], 1.0) * D))
-
-    def own_rows(partial):
-        return lax.psum_scatter(partial, "fsdp", scatter_dimension=0, tiled=True)
-
-    fed_grads = weight_gradients(b_blocks, cot_blocks, gz_i, gz_g, m_blocks)
-    fed_rows = own_rows(fed_grads)
-    out_part = matmul_tn(mixed_low, after(grad_attn_low, grad_by_heads)).astype(BF)
-    out_quarter = reduce_seq(
-        [lax.dynamic_slice_in_dim(out_part, r * part, part, axis=1) for r in rel]
-    )
-    out_rows = own_rows(after(out_quarter.astype(BF), fed_rows))
-
-    gp = attend_backward(
-        q, k, v, grad_by_heads, lse, seg_col, valid_col, seg_row, cosine, sine, tokens
+    last = jnp.concatenate([last.astype(BF), out_rows], axis=1)
+    ga_came, in_all = after((ga_came, in_all), last)
+
+    grad_in_weight, grad_gain_two = finish_rows(
+        functools.partial(in_rows_kernel, seq_size, hidden), in_all, w_in_proj, mlp_gain, seq, (2 * FF, 1), "in_rows"
     )
     if paired():
-        mine, away = last_gradients(a_low, gp, fsdp, fsdp_size)
-        last = reduce_rows(mine, away, fsdp_size)
+        grad_down = jnp.concatenate(in_order(share_seq(down_rows)), axis=1).astype(F32)
     else:
-        last = lax.psum_scatter(matmul_tn(a_low, gp), "fsdp", scatter_dimension=0, tiled=True)
-    ga_parts = matmul_nt(gp, qkv_weight)
-
-    fed = [fed_rows[:, i * slot : i * slot + hidden] for i in range(3)]
-    if paired():
-        every = lax.all_gather(jnp.stack([fed[0], fed[1], transpose_devices(fed[2])]), "seq", axis=0)
-        half = hidden // 2
-        core = fsdp % 2
-        low, high = every[:, 2, :, :half], every[:, 2, :, half:]
-        kept, came = jnp.where(core == 0, low, high), swap(jnp.where(core == 0, high, low), "fsdp", 1)
-        even, odd = jnp.where(core == 0, kept, came), jnp.where(core == 0, came, kept)
-        grad_down = jnp.concatenate([half_rows[i].T for i in range(seq_size) for half_rows in (even, odd)], axis=1)
-        grad_down = grad_down.astype(F32)
-    else:
-        every = lax.all_gather(jnp.stack(fed[:2]), "seq", axis=0)
-        down = lax.all_gather(fed[2], ("seq", "fsdp"), axis=0, tiled=True)
+        down = lax.all_gather(down_rows, ("seq", "fsdp"), axis=0, tiled=True)
         down = down.reshape(seq_size, D, hidden).transpose(0, 2, 1).reshape(FF, D)
-        mine = FF // fsdp_size
-        grad_down = lax.dynamic_slice_in_dim(down, fsdp * mine, mine, axis=0).astype(F32)
-    grad_in_weight = jnp.concatenate([every[j, i] for i in range(2) for j in range(seq_size)], axis=1).astype(F32)
-
-    last = last.astype(BF)
-    last = jnp.stack([last[:, i * part : (i + 1) * part] for i in range(3)] + [out_rows])
-    last = in_order(share_seq(last))
-    grad_qkv_weight = jnp.concatenate([p[i] for i in range(3) for p in last], axis=1).astype(F32)
-    grad_out_weight = jnp.concatenate([p[3] for p in last], axis=1).astype(F32)
-
-    grad_normed = reduce_seq([ga_parts[i * tokens : (i + 1) * tokens] for i in range(seq_size)])
+        rows = FF // fsdp_size
+        grad_down = lax.dynamic_slice_in_dim(down, fsdp * rows, rows, axis=0).astype(F32)
+
+    grad_normed = sum_blocks(ga_came)
     grad_inputs = grad_middle + norm_back(grad_normed, gain_one, x)
-
-    def gain_gradient(weight, gradient, gain):
-        return jnp.sum(weight.astype(F32) * gradient, axis=1) / gain.astype(F32)
+    last = after(share_seq(last), grad_in_weight, grad_down, grad_inputs)
+    grad_qkv_weight, grad_out_weight, grad_gain_one = finish_rows(
+        functools.partial(last_rows_kernel, seq_size), last, w_qkv, attn_gain, seq, (3 * D, D, 1), "last_rows"
+    )
 
     return (
         result.astype(BF)[None],
@@ -597,8 +731,8 @@
         grad_out_weight,
         grad_in_weight,
         grad_down,
-        gain_gradient(w_qkv, grad_qkv_weight, attn_gain),
-        gain_gradient(w_in_proj, grad_in_weight, mlp_gain),
+        grad_gain_one[:, 0],
+        grad_gain_two[:, 0],
         root_means,
     )
 

time: 424 us -> 387 us (0.913); the launches traced: 424 us -> 379 us
  waiting for transfers between devices: 141 us -> 114 us
  local copies, waits for them, and re-layouts: 34.6 us -> 22.4 us
  other arithmetic: 42.9 us -> 33.2 us
  starting transfers between devices: 72 us -> 77.4 us
  matrix products: 9.45 us -> 5.15 us
    all_gather x1 -> x0, waiting for transfers between devices: 23.2 us -> none  [on_device(): lax.all_gather(jnp.stack([fed[0], fed[1], transpose_devices(fed[2])]), 's...]
    all_to_all x0 -> x2, starting transfers between devices: none -> 9.73 us  [exchange_seq(): lax.all_to_all(blocks, 'seq', split_axis=0, concat_axis=0, tiled=True)]
    reduce_scatter x2, waiting for transfers between devices: 8.7 us -> 0.01 us  [own_rows(): return lax.psum_scatter(partial, 'fsdp', scatter_dimension=0, tiled=True)]
    unnamed x113 -> x81, local copies, waits for them, and re-layouts: 13.9 us -> 6.02 us
    dot_general x2 -> x1, matrix products: 6.39 us -> 0.74 us  [matmul_nt(): lax.dot_general(a, b, (((1,), (1,)), ((), ())), preferred_element_type=F32)]
    ppermute x46, starting transfers between devices: 70.4 us -> 65.3 us  [swap(): lax.ppermute(x, axis, [(i, i ^ bit) for i in range(lax.axis_size(axis))])]
    reduce_sum x2 -> x0, other arithmetic: 4.55 us -> none  [gain_gradient(): return jnp.sum(weight.astype(F32) * gradient, axis=1) / gain.astype(F32)]
    ppermute x46, waiting for transfers between devices: 109 us -> 113 us  [swap(): lax.ppermute(x, axis, [(i, i ^ bit) for i in range(lax.axis_size(axis))])]
  transfers between devices with their start and end apart: 54 -> 54, of which waited for: 25 -> 24; matrix products, arithmetic and copies ran while one was open for 17% -> 14% of each run, Pallas kernels for 18% -> 23%
where the time goes in v3:
time: 387 us; the launch traced here: 379 us
  waiting for transfers between devices  114 us (29%)
  Pallas kernels  112 us (29%)
  starting transfers between devices  77.4 us (20%)
  other arithmetic  33.2 us (9%)
  local copies, waits for them, and re-layouts  22.4 us (6%)
  between operations  15.4 us (4%)
  matrix products  5.15 us (1%)
    ppermute x46, waiting for transfers between devices, swap(): lax.ppermute(x, axis, [(i, i ^ bit) for i in range(lax.axis_size(axis))])  113 us
    ppermute x46, starting transfers between devices, swap(): lax.ppermute(x, axis, [(i, i ^ bit) for i in range(lax.axis_size(axis))])  65.3 us
    pallas_call x4, Pallas kernels, feed_forward(): pl.pallas_call(functools.partial(feed_kernel, hidden), grid_spec=pltpu.Pr...  26.8 us
    pallas_call x1, Pallas kernels, attend_backward(): pl.pallas_call(backward_kernel, grid=(length // rows,), in_specs=[tile, t...  24 us
    pallas_call x1, Pallas kernels, attend_forward(): pl.pallas_call(forward_kernel, grid=(length // rows,), in_specs=[tile, wh...  19.5 us
    pallas_call x2, Pallas kernels, weight_gradients(): pl.pallas_call(functools.partial(weight_kernel, count, slot, pairs), grid...  13.2 us
    all_to_all x2, starting transfers between devices, exchange_seq(): lax.all_to_all(blocks, 'seq', split_axis=0, concat_axis=0, tiled=True)  9.73 us
    pallas_call x1, Pallas kernels, last_gradients(): pl.pallas_call(last_kernel, grid_spec=pltpu.PrefetchScalarGridSpec(num_sc...  8.2 us
  transfers between devices with their start and end apart: 54, of which 24 were waited for; matrix products, arithmetic and copies ran while one was open for 14% of the time, Pallas kernels for 23%

profile of v3, /device:TPU:0, one launch (start us, length us, event | category | flops | bytes accessed | tf_op | source)
XLA Modules:
  0.0 379.4 jit_solution(10108828604435094960)
XLA Ops:
  13.6 10.6 %collective-permute-done.1.refs_2_ = bf16[256,1024]{1,0:T(8,128)(2,1)S(1)} collective-permute-done((bf16[256,1024]{1,0:T(8,128)(2,1)}, bf16[256,1024]{1,0:T(8,128)(2,1)S(1)}, u32[]{:S(2)}, u32[]{:S(2)}) %collective-permute-start.1) | collective-permute-done | bytes 524320 | tf_op jit(solution)/shard_map/ppermute | solution.py:23
  29.4 4.2 %collective-permute-start.5 = (bf16[2,1024]{1,0:T(2,128)(2,1)S(1)}, bf16[2,1024]{1,0:T(2,128)(2,1)S(1)}, u32[]{:S(2)}, u32[]{:S(2)}) collective-permute-start(bf16[2,1024]{1,0:T(2,128)(2,1)S(1)} %constant_dynamic-update-slice_fusion.4), channel_id=1, source_target_pairs={{0,2},{1,3},{2,0},{3,1},{4,6},{5,7},{6,4},{7,5},{8,10},{9,11},{10,... | collective-permute-start | bytes 12296 | tf_op jit(solution)/shard_map/ppermute | solution.py:23
  33.6 19.1 %collective-permute-done.5 = bf16[2,1024]{1,0:T(2,128)(2,1)S(1)} collective-permute-done((bf16[2,1024]{1,0:T(2,128)(2,1)S(1)}, bf16[2,1024]{1,0:T(2,128)(2,1)S(1)}, u32[]{:S(2)}, u32[]{:S(2)}) %collective-permute-start.5) | collective-permute-done | bytes 4128 | tf_op jit(solution)/shard_map/ppermute | solution.py:23
  52.9 4.4 %collective-permute-done.6 = bf16[2,1024]{1,0:T(2,128)(2,1)S(1)} collective-permute-done((bf16[2,1024]{1,0:T(2,128)(2,1)S(1)}, bf16[2,1024]{1,0:T(2,128)(2,1)S(1)}, u32[]{:S(2)}, u32[]{:S(2)}) %collective-permute-start.6) | collective-permute-done | bytes 4128 | tf_op jit(solution)/shard_map/ppermute | solution.py:23
  58.1 6.1 %collective-permute-done.2 = bf16[128,1024]{1,0:T(8,128)(2,1)S(1)} collective-permute-done((bf16[128,1024]{1,0:T(8,128)(2,1)S(1)}, bf16[128,1024]{1,0:T(8,128)(2,1)S(1)}, u32[]{:S(2)}, u32[]{:S(2)}) %collective-permute-start.2) | collective-permute-done | bytes 262176 | tf_op jit(solution)/shard_map/ppermute | solution.py:23
  77.1 4.9 %collective-permute-done.14.g_ref.refs_2_ = bf16[256,1024]{1,0:T(8,128)(2,1)S(1)} collective-permute-done((bf16[256,1024]{1,0:T(8,128)(2,1)S(1)}, bf16[256,1024]{1,0:T(8,128)(2,1)S(1)}, u32[]{:S(2)}, u32[]{:S(2)}) %collective-permute-start.14) | collective-permute-done | bytes 524320 | tf_op jit(solution)/shard_map/ppermute | solution.py:23
  93.4 7.3 %qkv.1 = (bf16[1024,1024]{1,0:T(8,128)(2,1)}, bf16[1024,256]{1,0:T(8,128)(2,1)}, bf16[1024,256]{1,0:T(8,128)(2,1)}, bf16[1024,256]{1,0:T(8,128)(2,1)}) custom-call(bf16[256,1024]{1,0:T(8,128)(2,1)} %bitcast.65, bf16[256,1024]{1,0:T(8,128)(2,1)} %copy-done.25, bf16[256,1024]{1,0:T(8,128)(2,1)} %copy-done.24, bf16[256,1024]{1,0:T(8,128)(2,1)} %copy-done.26, ...), custom_call_target="tpu_custom_call" | custom-call | flops 1610612736 | bytes 7340032 | tf_op jit(solution)/shard_map/qkv/pallas_call | solution.py:143
  100.7 19.5 %attend.1 = (bf16[1024,256]{1,0:T(8,128)(2,1)}, f32[8,1024]{1,0:T(8,128)}) custom-call(bf16[1024,256]{1,0:T(8,128)(2,1)} %get-tuple-element.80.q_ref, bf16[1024,256]{1,0:T(8,128)(2,1)} %get-tuple-element.81.k_ref, bf16[1024,256]{1,0:T(8,128)(2,1)} %get-tuple-element.82.v_ref, s32[1024,1]{1,0:T(8,128)} %copy.27.segc_ref, s32[1024,1]{1,0:T(8,128)} %copy.28.valc_ref, ...), custom_call_target="tpu_custom_call" | custom-call | flops 1073741824 | bytes 2097152 | tf_op jit(solution)/shard_map/attend/pallas_call | solution.py:202
  141.5 8.1 %collective-permute-done.17.b_ref.refs_1_ = bf16[256,1024]{1,0:T(8,128)(2,1)} collective-permute-done((bf16[256,1024]{1,0:T(8,128)(2,1)S(1)}, bf16[256,1024]{1,0:T(8,128)(2,1)}, u32[]{:S(2)}, u32[]{:S(2)}) %collective-permute-start.17) | collective-permute-done | bytes 524320 | tf_op jit(solution)/shard_map/ppermute | solution.py:23
  149.6 6.6 %feed.4 = (bf16[256,656]{1,0:T(8,128)(2,1)}, bf16[256,656]{1,0:T(8,128)(2,1)}, bf16[256,656]{1,0:T(8,128)(2,1)}, bf16[256,1024]{1,0:T(8,128)(2,1)}, bf16[1024,1024]{1,0:T(8,128)(2,1)}) custom-call(s32[1]{0:T(128)} %bitcast.14.me_ref, bf16[256,1024]{1,0:T(8,128)(2,1)} %collective-permute-done.17.b_ref.refs_1_, ...), custom_call_target="tpu_custom_call" | custom-call | flops 2063597568 | bytes 7135232 | tf_op jit(solution)/shard_map/feed/pallas_call | solution.py:334
  158.8 6.6 %feed.5 = (bf16[256,656]{1,0:T(8,128)(2,1)}, bf16[256,656]{1,0:T(8,128)(2,1)}, bf16[256,656]{1,0:T(8,128)(2,1)}, bf16[256,1024]{1,0:T(8,128)(2,1)}, bf16[1024,1024]{1,0:T(8,128)(2,1)}) custom-call(s32[1]{0:T(128)} %bitcast.14.me_ref, bf16[256,1024]{1,0:T(8,128)(2,1)} %copy-done.19, bf16[256,1024]{1,0:T(8,128)(2,1)} %copy-done.7, ...), custom_call_target="tpu_custom_call", output_to_operand_aliasing={{4}: (4, {})} | custom-call | flops 2063597568 | bytes 7135232 | tf_op jit(solution)/shard_map/feed/pallas_call | solution.py:334
  165.5 6.6 %feed.6 = (bf16[256,656]{1,0:T(8,128)(2,1)}, bf16[256,656]{1,0:T(8,128)(2,1)}, bf16[256,656]{1,0:T(8,128)(2,1)}, bf16[256,1024]{1,0:T(8,128)(2,1)}, bf16[1024,1024]{1,0:T(8,128)(2,1)}) custom-call(s32[1]{0:T(128)} %bitcast.14.me_ref, bf16[256,1024]{1,0:T(8,128)(2,1)} %collective-permute-done.21.b_ref.refs_3_, ...), custom_call_target="tpu_custom_call", output_to_operand_aliasing={{4}: (4, {})} | custom-call | flops 2063597568 | bytes 7135232 | tf_op jit(solution)/shard_map/feed/pallas_call | solution.py:334
  172.1 3.3 collective-permute-start.24
  175.4 7.4 %collective-permute-done.24 = bf16[256,1024]{1,0:T(8,128)(2,1)S(1)} collective-permute-done((bf16[256,1024]{1,0:T(8,128)(2,1)}, bf16[256,1024]{1,0:T(8,128)(2,1)S(1)}, u32[]{:S(2)}, u32[]{:S(2)}) %collective-permute-start.24) | collective-permute-done | bytes 524320 | tf_op jit(solution)/shard_map/ppermute | solution.py:23
  182.8 7.1 %feed.7 = (bf16[256,656]{1,0:T(8,128)(2,1)}, bf16[256,656]{1,0:T(8,128)(2,1)}, bf16[256,656]{1,0:T(8,128)(2,1)}, f32[256,1024]{1,0:T(8,128)}, bf16[1024,1024]{1,0:T(8,128)(2,1)}) custom-call(s32[1]{0:T(128)} %bitcast.14.me_ref, bf16[256,1024]{1,0:T(8,128)(2,1)} %copy-done.9, bf16[256,1024]{1,0:T(8,128)(2,1)} %bitcast.59, ...), custom_call_target="tpu_custom_call", output_to_operand_aliasing={{4}: (4, {})} | custom-call | flops 2063597568 | bytes 7135232 | tf_op jit(solution)/shard_map/feed/pallas_call | solution.py:334
  189.8 7.6 %weight_gradients.2.refs_8_ = bf16[1024,2304]{1,0:T(8,128)(2,1)} custom-call(bf16[256,1024]{1,0:T(8,128)(2,1)} %copy-done.9, bf16[256,1024]{1,0:T(8,128)(2,1)} %collective-permute-done.17.b_ref.refs_1_, bf16[256,1024]{1,0:T(8,128)(2,1)} %copy-done.19, bf16[256,1024]{1,0:T(8,128)(2,1)} %collective-permute-done.21.b_ref.refs_3_, ...), custom_call_target="tpu_custom_call" | custom-call | flops 2751463424 | bytes 4784128 | tf_op jit(solution)/shard_map/weight_gradients/pallas_call | solution.py:386
  197.4 5.6 %weight_gradients.3 = bf16[1024,2304]{1,0:T(8,128)(2,1)} custom-call(bf16[256,1024]{1,0:T(8,128)(2,1)} %bitcast.60, bf16[256,1024]{1,0:T(8,128)(2,1)} %collective-permute-done.13.g_ref.refs_1_, bf16[256,1024]{1,0:T(8,128)(2,1)} %copy-done.7, bf16[256,1024]{1,0:T(8,128)(2,1)} %copy-done.8, ...), custom_call_target="tpu_custom_call", output_to_operand_aliasing={{}: (8, {})} | custom-call | flops 1375731712 | bytes 3440640 | tf_op jit(solution)/shard_map/weight_gradients/pallas_call | solution.py:386
  212.1 3.8 collective-permute-done.27
  224.3 5.9 %all-to-all-start = ((bf16[4,256,1024]{2,1,0:T(8,128)(2,1)}), bf16[4,256,1024]{2,1,0:T(8,128)(2,1)S(1)}, u32[]{:S(2)}, u32[]{:S(2)}) async-start(bf16[4,256,1024]{2,1,0:T(8,128)(2,1)} %bitcast.18), calls=%async_computation | async-start | bytes 4194304 | tf_op jit(solution)/shard_map/all_to_all | solution.py:51
  230.9 24.0 %attend_back.1.gp_ref = bf16[1024,768]{1,0:T(8,128)(2,1)} custom-call(bf16[1024,256]{1,0:T(8,128)(2,1)} %get-tuple-element.80.q_ref, bf16[1024,256]{1,0:T(8,128)(2,1)} %pad_maximum_fusion.4.go_ref, f32[8,1024]{1,0:T(8,128)} %get-tuple-element.120.lse_ref, bf16[1024,256]{1,0:T(8,128)(2,1)} %get-tuple-element.81.k_ref, ...), custom_call_target="tpu_custom_call" | custom-call | flops 2684354560 | bytes 5242880 | tf_op jit(solution)/shard_map/attend_back/pallas_call | solution.py:269
  254.9 3.3 fusion.13
  267.3 8.2 %last_gradients.1 = (f32[512,768]{1,0:T(8,128)}, bf16[512,768]{1,0:T(8,128)(2,1)}) custom-call(s32[1]{0:T(128)} %bitcast.21.me_ref, bf16[1024,1024]{1,0:T(8,128)(2,1)} %get-tuple-element.122.a_ref, bf16[1024,768]{1,0:T(8,128)(2,1)} %attend_back.1.gp_ref), custom_call_target="tpu_custom_call" | custom-call | flops 1610612736 | bytes 6029312 | tf_op jit(solution)/shard_map/last_gradients/pallas_call | solution.py:418
  279.9 3.5 collective-permute-done.46
  287.2 5.2 %collective-permute-done.47 = f32[4,128]{0,1:T(8,128)S(1)} collective-permute-done((f32[4,128]{0,1:T(8,128)S(1)}, f32[4,128]{0,1:T(8,128)S(1)}, u32[]{:S(2)}, u32[]{:S(2)}) %collective-permute-start.47) | collective-permute-done | bytes 2080 | tf_op jit(solution)/shard_map/ppermute | solution.py:23
  296.4 4.6 %collective-permute-start.30 = (bf16[128,1536]{1,0:T(8,128)(2,1)S(1)}, bf16[128,1536]{1,0:T(8,128)(2,1)}, u32[]{:S(2)}, u32[]{:S(2)}) collective-permute-start(bf16[128,1536]{1,0:T(8,128)(2,1)S(1)} %slice.122.refs_0_), channel_id=1, source_target_pairs={{0,24},{8,16},{16,8},{24,0},{1,25},{9,17},{17,9},{25,1},{2,26},{10... | collective-permute-start | bytes 1179656 | tf_op jit(solution)/shard_map/ppermute | solution.py:23
  301.1 5.4 %project_back.1 = bf16[1024,1024]{1,0:T(8,128)(2,1)} custom-call(s32[1]{0:T(128)} %bitcast.14.me_ref, bf16[1024,768]{1,0:T(8,128)(2,1)} %attend_back.1.gp_ref, bf16[1024,768]{1,0:T(8,128)(2,1)} %slice.138.refs_4_.w_ref), custom_call_target="tpu_custom_call" | custom-call | flops 1610612736 | bytes 5242880 | tf_op jit(solution)/shard_map/project_back/pallas_call | solution.py:445
  306.5 3.8 %all-to-all-start.1 = ((bf16[4,256,1024]{2,1,0:T(8,128)(2,1)}), bf16[4,256,1024]{2,1,0:T(8,128)(2,1)S(1)}, u32[]{:S(2)}, u32[]{:S(2)}) async-start(bf16[4,256,1024]{2,1,0:T(8,128)(2,1)} %bitcast.66), calls=%async_computation.2 | async-start | bytes 4194304 | tf_op jit(solution)/shard_map/all_to_all | solution.py:51
  326.7 6.0 %collective-permute-done.36 = bf16[128,768]{1,0:T(8,128)(2,1)S(1)} collective-permute-done((bf16[128,768]{1,0:T(8,128)(2,1)}, bf16[128,768]{1,0:T(8,128)(2,1)S(1)}, u32[]{:S(2)}, u32[]{:S(2)}) %collective-permute-start.36) | collective-permute-done | bytes 196640 | tf_op jit(solution)/shard_map/ppermute | solution.py:23
  337.3 7.1 %collective-permute-done.42 = bf16[328,256]{0,1:T(8,128)(2,1)} collective-permute-done((bf16[328,256]{0,1:T(8,128)(2,1)}, bf16[328,256]{0,1:T(8,128)(2,1)}, u32[]{:S(2)}, u32[]{:S(2)}) %collective-permute-start.42) | collective-permute-done | bytes 167968 | tf_op jit(solution)/shard_map/ppermute | solution.py:23
  344.4 3.4 collective-permute-start.41
  355.6 4.3 %in_rows.1 = (f32[128,5248]{1,0:T(8,128)}, f32[128,1]{1,0:T(8,128)}) custom-call(s32[1]{0:T(128)} %bitcast.14.me_ref, bf16[128,1536]{1,0:T(8,128)(2,1)} %copy-done.11, bf16[128,1536]{1,0:T(8,128)(2,1)} %collective-permute-done.28.refs_1_, bf16[128,1536]{1,0:T(8,128)(2,1)} %collective-permute-done.29.refs_2_, ...), custom_call_target="tpu_custom_call" | custom-call | bytes 5374976 | tf_op jit(solution)/shard_map/in_rows/pallas_call | solution.py:510
  361.3 6.0 %collective-permute-done.41.refs_3_ = bf16[128,1792]{1,0:T(8,128)(2,1)} collective-permute-done((bf16[128,1792]{1,0:T(8,128)(2,1)S(1)}, bf16[128,1792]{1,0:T(8,128)(2,1)}, u32[]{:S(2)}, u32[]{:S(2)}) %collective-permute-start.41) | collective-permute-done | bytes 458784 | tf_op jit(solution)/shard_map/ppermute | solution.py:23
  (266 shorter events, 134.5 us)
Async XLA Ops:
  7.2 78.9 %all-gather.3.cloned.1.call-start = ((), (), s32[]{:S(2)}) async-start(), calls=%async_computation.4 | async-start | bytes 2359296 | tf_op jit(solution)/shard_map/all_gather | solution.py:67
  9.0 140.6 %all-gather.5.cloned.1.call-start = ((), (), s32[]{:S(2)}) async-start(), calls=%async_computation.5 | async-start | bytes 5308416 | tf_op jit(solution)/shard_map/all_gather | solution.py:67
  9.0 15.2 %collective-permute-start.1 = (bf16[256,1024]{1,0:T(8,128)(2,1)}, bf16[256,1024]{1,0:T(8,128)(2,1)S(1)}, u32[]{:S(2)}, u32[]{:S(2)}) collective-permute-start(bf16[256,1024]{1,0:T(8,128)(2,1)} %bitcast.63), channel_id=1, source_target_pairs={{0,16},{8,24},{16,0},{24,8},{1,17},{9,25},{17,1},{25,9},{2,18},{10... | collective-permute-start | bytes 1572872 | tf_op jit(solution)/shard_map/ppermute | solution.py:23
  12.1 13.6 %collective-permute-start = (bf16[256,1024]{1,0:T(8,128)(2,1)}, bf16[256,1024]{1,0:T(8,128)(2,1)S(1)}, u32[]{:S(2)}, u32[]{:S(2)}) collective-permute-start(bf16[256,1024]{1,0:T(8,128)(2,1)} %bitcast.64), channel_id=1, source_target_pairs={{0,8},{8,0},{16,24},{24,16},{1,9},{9,1},{17,25},{25,17},{2,10},{10... | collective-permute-start | bytes 1572872 | tf_op jit(solution)/shard_map/ppermute | solution.py:23
  27.4 25.4 %collective-permute-start.18 = (bf16[328,256]{0,1:T(8,128)(2,1)S(1)}, bf16[328,256]{0,1:T(8,128)(2,1)S(1)}, u32[]{:S(2)}, u32[]{:S(2)}) collective-permute-start(bf16[328,256]{0,1:T(8,128)(2,1)S(1)} %constant_dynamic-slice_fusion.4), channel_id=1, source_target_pairs={{0,0},{1,1},{2,8},{3,9},{4,16},{5,17},{6,24},{7,25},{8,2},{9,3},{1... | collective-permute-start | bytes 503816 | tf_op jit(solution)/shard_map/ppermute | solution.py:78
  29.4 23.3 %collective-permute-start.5 = (bf16[2,1024]{1,0:T(2,128)(2,1)S(1)}, bf16[2,1024]{1,0:T(2,128)(2,1)S(1)}, u32[]{:S(2)}, u32[]{:S(2)}) collective-permute-start(bf16[2,1024]{1,0:T(2,128)(2,1)S(1)} %constant_dynamic-update-slice_fusion.4), channel_id=1, source_target_pairs={{0,2},{1,3},{2,0},{3,1},{4,6},{5,7},{6,4},{7,5},{8,10},{9,11},{10,... | collective-permute-start | bytes 12296 | tf_op jit(solution)/shard_map/ppermute | solution.py:23
  67.3 200.0 %reduce-scatter.3.cloned.1.call-start = ((), (), s32[]{:S(2)}) async-start(), calls=%async_computation.6 | async-start | bytes 5308416 | tf_op jit(solution)/shard_map/reduce_scatter | solution.py:663
  70.9 12.6 %collective-permute-start.13 = (bf16[256,1024]{1,0:T(8,128)(2,1)S(1)}, bf16[256,1024]{1,0:T(8,128)(2,1)}, u32[]{:S(2)}, u32[]{:S(2)}) collective-permute-start(bf16[256,1024]{1,0:T(8,128)(2,1)S(1)} %bitcast.62), channel_id=1, source_target_pairs={{0,8},{8,0},{16,24},{24,16},{1,9},{9,1},{17,25},{25,17},{2,10},{10... | collective-permute-start | bytes 1572872 | tf_op jit(solution)/shard_map/ppermute | solution.py:23
  82.0 39.3 %collective-permute-start.15 = (bf16[128,1024]{1,0:T(8,128)(2,1)S(1)}, bf16[128,1024]{1,0:T(8,128)(2,1)S(1)}, u32[]{:S(2)}, u32[]{:S(2)}) collective-permute-start(bf16[128,1024]{1,0:T(8,128)(2,1)S(1)} %slice.142), channel_id=1, source_target_pairs={{0,8},{8,0},{16,24},{24,16},{1,9},{9,1},{17,25},{25,17},{2,10},{10... | collective-permute-start | bytes 786440 | tf_op jit(solution)/shard_map/ppermute | solution.py:23
  84.5 38.0 %collective-permute-start.16 = (bf16[128,1024]{1,0:T(8,128)(2,1)S(1)}, bf16[128,1024]{1,0:T(8,128)(2,1)S(1)}, u32[]{:S(2)}, u32[]{:S(2)}) collective-permute-start(bf16[128,1024]{1,0:T(8,128)(2,1)S(1)} %slice.143), channel_id=1, source_target_pairs={{0,16},{8,24},{16,0},{24,8},{1,17},{9,25},{17,1},{25,9},{2,18},{10... | collective-permute-start | bytes 786440 | tf_op jit(solution)/shard_map/ppermute | solution.py:23
  87.2 46.1 %collective-permute-start.10 = (bf16[1024,256]{1,0:T(8,128)(2,1)S(1)}, bf16[1024,256]{1,0:T(8,128)(2,1)S(1)}, u32[]{:S(2)}, u32[]{:S(2)}) collective-permute-start(bf16[1024,256]{1,0:T(8,128)(2,1)S(1)} %slice.140), channel_id=1, source_target_pairs={{0,24},{8,16},{16,8},{24,0},{1,25},{9,17},{17,9},{25,1},{2,26},{10... | collective-permute-start | bytes 1572872 | tf_op jit(solution)/shard_map/ppermute | solution.py:23
  88.4 44.9 %collective-permute-start.11 = (bf16[1024,256]{1,0:T(8,128)(2,1)S(1)}, bf16[1024,256]{1,0:T(8,128)(2,1)S(1)}, u32[]{:S(2)}, u32[]{:S(2)}) collective-permute-start(bf16[1024,256]{1,0:T(8,128)(2,1)S(1)} %slice.140), channel_id=1, source_target_pairs={{0,16},{8,24},{16,0},{24,8},{1,17},{9,25},{17,1},{25,9},{2,18},{10... | collective-permute-start | bytes 1572872 | tf_op jit(solution)/shard_map/ppermute | solution.py:23
  90.3 42.9 %collective-permute-start.12 = (bf16[1024,256]{1,0:T(8,128)(2,1)S(1)}, bf16[1024,256]{1,0:T(8,128)(2,1)}, u32[]{:S(2)}, u32[]{:S(2)}) collective-permute-start(bf16[1024,256]{1,0:T(8,128)(2,1)S(1)} %slice.140), channel_id=1, source_target_pairs={{0,8},{8,0},{16,24},{24,16},{1,9},{9,1},{17,25},{25,17},{2,10},{10... | collective-permute-start | bytes 1572872 | tf_op jit(solution)/shard_map/ppermute | solution.py:23
  137.6 12.0 %collective-permute-start.17 = (bf16[256,1024]{1,0:T(8,128)(2,1)S(1)}, bf16[256,1024]{1,0:T(8,128)(2,1)}, u32[]{:S(2)}, u32[]{:S(2)}) collective-permute-start(bf16[256,1024]{1,0:T(8,128)(2,1)S(1)} %multiply_convert_fusion.b_ref.refs_0_), channel_id=1, source_target_pairs={{0,8},{8,0},{16,24},{24,16},{1,9},{9,1},{17,25},{25,17},{2,10},{10... | collective-permute-start | bytes 1572872 | tf_op jit(solution)/shard_map/ppermute | solution.py:23
  139.9 18.0 %collective-permute-start.22 = (bf16[256,1024]{1,0:T(8,128)(2,1)S(1)}, bf16[256,1024]{1,0:T(8,128)(2,1)S(1)}, u32[]{:S(2)}, u32[]{:S(2)}) collective-permute-start(bf16[256,1024]{1,0:T(8,128)(2,1)S(1)} %multiply_convert_fusion.b_ref.refs_0_), channel_id=1, source_target_pairs={{0,16},{8,24},{16,0},{24,8},{1,17},{9,25},{17,1},{25,9},{2,18},{10... | collective-permute-start | bytes 1572872 | tf_op jit(solution)/shard_map/ppermute | solution.py:23
  139.9 25.5 %collective-permute-start.21 = (bf16[256,1024]{1,0:T(8,128)(2,1)S(1)}, bf16[256,1024]{1,0:T(8,128)(2,1)}, u32[]{:S(2)}, u32[]{:S(2)}) collective-permute-start(bf16[256,1024]{1,0:T(8,128)(2,1)S(1)} %multiply_convert_fusion.b_ref.refs_0_), channel_id=1, source_target_pairs={{0,24},{8,16},{16,8},{24,0},{1,25},{9,17},{17,9},{25,1},{2,26},{10... | collective-permute-start | bytes 1572872 | tf_op jit(solution)/shard_map/ppermute | solution.py:23
  224.3 30.6 %all-to-all-start = ((bf16[4,256,1024]{2,1,0:T(8,128)(2,1)}), bf16[4,256,1024]{2,1,0:T(8,128)(2,1)S(1)}, u32[]{:S(2)}, u32[]{:S(2)}) async-start(bf16[4,256,1024]{2,1,0:T(8,128)(2,1)} %bitcast.18), calls=%async_computation | async-start | bytes 4194304 | tf_op jit(solution)/shard_map/all_to_all | solution.py:51
  230.2 96.5 %reduce-scatter.5.cloned.1.call-start = ((), (), s32[]{:S(2)}) async-start(), calls=%async_computation.7 | async-start | bytes 2359296 | tf_op jit(solution)/shard_map/reduce_scatter | solution.py:663
  275.5 34.9 %collective-permute-start.31 = (bf16[512,768]{1,0:T(8,128)(2,1)}, bf16[512,768]{1,0:T(8,128)(2,1)S(1)}, u32[]{:S(2)}, u32[]{:S(2)}) collective-permute-start(bf16[512,768]{1,0:T(8,128)(2,1)} %get-tuple-element.124), channel_id=1, source_target_pairs={{0,1},{1,0},{2,3},{3,2},{4,5},{5,4},{6,7},{7,6},{8,9},{9,8},{10,11... | collective-permute-start | bytes 2359304 | tf_op jit(solution)/shard_map/ppermute | solution.py:23
  284.7 25.6 %collective-permute-start.28 = (bf16[128,1536]{1,0:T(8,128)(2,1)S(1)}, bf16[128,1536]{1,0:T(8,128)(2,1)}, u32[]{:S(2)}, u32[]{:S(2)}) collective-permute-start(bf16[128,1536]{1,0:T(8,128)(2,1)S(1)} %slice.122.refs_0_), channel_id=1, source_target_pairs={{0,8},{8,0},{16,24},{24,16},{1,9},{9,1},{17,25},{25,17},{2,10},{10... | collective-permute-start | bytes 1179656 | tf_op jit(solution)/shard_map/ppermute | solution.py:23
  286.2 24.1 %collective-permute-start.29 = (bf16[128,1536]{1,0:T(8,128)(2,1)S(1)}, bf16[128,1536]{1,0:T(8,128)(2,1)}, u32[]{:S(2)}, u32[]{:S(2)}) collective-permute-start(bf16[128,1536]{1,0:T(8,128)(2,1)S(1)} %slice.122.refs_0_), channel_id=1, source_target_pairs={{0,16},{8,24},{16,0},{24,8},{1,17},{9,25},{17,1},{25,9},{2,18},{10... | collective-permute-start | bytes 1179656 | tf_op jit(solution)/shard_map/ppermute | solution.py:23
  294.3 15.9 %collective-permute-start.32 = (bf16[128,656]{1,0:T(8,128)(2,1)}, bf16[128,656]{1,0:T(8,128)(2,1)S(1)}, u32[]{:S(2)}, u32[]{:S(2)}) collective-permute-start(bf16[128,656]{1,0:T(8,128)(2,1)} %slice.123), channel_id=1, source_target_pairs={{0,0},{1,1},{2,8},{3,9},{4,16},{5,17},{6,24},{7,25},{8,2},{9,3},{1... | collective-permute-start | bytes 503816 | tf_op jit(solution)/shard_map/ppermute | solution.py:78
  296.4 25.6 %collective-permute-start.30 = (bf16[128,1536]{1,0:T(8,128)(2,1)S(1)}, bf16[128,1536]{1,0:T(8,128)(2,1)}, u32[]{:S(2)}, u32[]{:S(2)}) collective-permute-start(bf16[128,1536]{1,0:T(8,128)(2,1)S(1)} %slice.122.refs_0_), channel_id=1, source_target_pairs={{0,24},{8,16},{16,8},{24,0},{1,25},{9,17},{17,9},{25,1},{2,26},{10... | collective-permute-start | bytes 1179656 | tf_op jit(solution)/shard_map/ppermute | solution.py:23
  306.5 47.7 %all-to-all-start.1 = ((bf16[4,256,1024]{2,1,0:T(8,128)(2,1)}), bf16[4,256,1024]{2,1,0:T(8,128)(2,1)S(1)}, u32[]{:S(2)}, u32[]{:S(2)}) async-start(bf16[4,256,1024]{2,1,0:T(8,128)(2,1)} %bitcast.66), calls=%async_computation.2 | async-start | bytes 4194304 | tf_op jit(solution)/shard_map/all_to_all | solution.py:51
  315.4 17.4 %collective-permute-start.36 = (bf16[128,768]{1,0:T(8,128)(2,1)}, bf16[128,768]{1,0:T(8,128)(2,1)S(1)}, u32[]{:S(2)}, u32[]{:S(2)}) collective-permute-start(bf16[128,768]{1,0:T(8,128)(2,1)} %get-tuple-element.198), channel_id=1, source_target_pairs={{0,4},{1,5},{2,6},{3,7},{4,0},{5,1},{6,2},{7,3},{8,12},{9,13},{10,... | collective-permute-start | bytes 589832 | tf_op jit(solution)/shard_map/ppermute | solution.py:23
  315.9 16.9 %collective-permute-start.37 = (bf16[128,768]{1,0:T(8,128)(2,1)S(1)}, bf16[128,768]{1,0:T(8,128)(2,1)}, u32[]{:S(2)}, u32[]{:S(2)}) collective-permute-start(bf16[128,768]{1,0:T(8,128)(2,1)S(1)} %get-tuple-element.197), channel_id=1, source_target_pairs={{0,6},{1,7},{2,4},{3,5},{4,2},{5,3},{6,0},{7,1},{8,14},{9,15},{10,... | collective-permute-start | bytes 589832 | tf_op jit(solution)/shard_map/ppermute | solution.py:23
  319.2 25.3 %collective-permute-start.42 = (bf16[328,256]{0,1:T(8,128)(2,1)}, bf16[328,256]{0,1:T(8,128)(2,1)}, u32[]{:S(2)}, u32[]{:S(2)}) collective-permute-start(bf16[328,256]{0,1:T(8,128)(2,1)} %maximum_bitcast_fusion.1), channel_id=1, source_target_pairs={{0,24},{8,16},{16,8},{24,0},{1,25},{9,17},{17,9},{25,1},{2,26},{10... | collective-permute-start | bytes 503816 | tf_op jit(solution)/shard_map/ppermute | solution.py:23
  322.1 25.8 %collective-permute-start.43 = (bf16[328,256]{0,1:T(8,128)(2,1)}, bf16[328,256]{0,1:T(8,128)(2,1)}, u32[]{:S(2)}, u32[]{:S(2)}) collective-permute-start(bf16[328,256]{0,1:T(8,128)(2,1)} %maximum_bitcast_fusion.1), channel_id=1, source_target_pairs={{0,16},{8,24},{16,0},{24,8},{1,17},{9,25},{17,1},{25,9},{2,18},{10... | collective-permute-start | bytes 503816 | tf_op jit(solution)/shard_map/ppermute | solution.py:23
  324.0 24.7 %collective-permute-start.44 = (bf16[328,256]{0,1:T(8,128)(2,1)}, bf16[328,256]{0,1:T(8,128)(2,1)}, u32[]{:S(2)}, u32[]{:S(2)}) collective-permute-start(bf16[328,256]{0,1:T(8,128)(2,1)} %maximum_bitcast_fusion.1), channel_id=1, source_target_pairs={{0,8},{8,0},{16,24},{24,16},{1,9},{9,1},{17,25},{25,17},{2,10},{10... | collective-permute-start | bytes 503816 | tf_op jit(solution)/shard_map/ppermute | solution.py:23
  334.9 26.4 %collective-permute-start.39 = (bf16[128,1792]{1,0:T(8,128)(2,1)S(1)}, bf16[128,1792]{1,0:T(8,128)(2,1)S(1)}, u32[]{:S(2)}, u32[]{:S(2)}) collective-permute-start(bf16[128,1792]{1,0:T(8,128)(2,1)S(1)} %pad_maximum_fusion.5.refs_0_), channel_id=1, source_target_pairs={{0,8},{8,0},{16,24},{24,16},{1,9},{9,1},{17,25},{25,17},{2,10},{10... | collective-permute-start | bytes 1376264 | tf_op jit(solution)/shard_map/ppermute | solution.py:23
  336.9 24.4 %collective-permute-start.40 = (bf16[128,1792]{1,0:T(8,128)(2,1)S(1)}, bf16[128,1792]{1,0:T(8,128)(2,1)}, u32[]{:S(2)}, u32[]{:S(2)}) collective-permute-start(bf16[128,1792]{1,0:T(8,128)(2,1)S(1)} %pad_maximum_fusion.5.refs_0_), channel_id=1, source_target_pairs={{0,16},{8,24},{16,0},{24,8},{1,17},{9,25},{17,1},{25,9},{2,18},{10... | collective-permute-start | bytes 1376264 | tf_op jit(solution)/shard_map/ppermute | solution.py:23
  344.4 22.9 %collective-permute-start.41 = (bf16[128,1792]{1,0:T(8,128)(2,1)S(1)}, bf16[128,1792]{1,0:T(8,128)(2,1)}, u32[]{:S(2)}, u32[]{:S(2)}) collective-permute-start(bf16[128,1792]{1,0:T(8,128)(2,1)S(1)} %pad_maximum_fusion.5.refs_0_), channel_id=1, source_target_pairs={{0,24},{8,16},{16,8},{24,0},{1,25},{9,17},{17,9},{25,1},{2,26},{10... | collective-permute-start | bytes 1376264 | tf_op jit(solution)/shard_map/ppermute | solution.py:23
  (61 other events, 548.6 us)
Sparse Core Ops, SparseCore 0:
  10.2 43.4 all-gather.2
  67.4 51.5 all-gather.4
  203.2 55.2 reduce-scatter.2
  260.7 35.7 reduce-scatter.4
